TPU v7x, 128 devices: a whole 4x4x4 slice. The times are simulated.
128 devices in a mesh: comp: 2 (over z_lo), ty: 8 (over y, z_hi), tx: 8 (over x, core).
Axes of the slice: x: 4, y: 4, z: 4 (z_hi: 2, z_lo: 2; z = z_hi * 2 + z_lo), core: 2. Of those that a mesh axis runs over, the one named last changes fastest.
Arguments:
- atm_flux: float32 [8, 2097152], P(None, ('comp', 'ty', 'tx')), may hold values from -6 to 6
- margin_source: int32 [32768, 128], P(('comp', 'ty', 'tx')), may hold values from 0 to 127
- margin_cell: int32 [32768, 128], P(('comp', 'ty', 'tx')), may hold values from 0 to 65535, as said below
- margin_weight: float32 [32768, 128], P(('comp', 'ty', 'tx')), may hold values from 0 to 1
- margin_tile: int32 [32768, 1], P(('comp', 'ty', 'tx')), may hold values from 0 to 127; in each aligned block of 256 rows (0 to 255, 256 to 511, ...) at most 4 rows name the same one
- land_mask: int32 [1024, 8192], P(('comp', 'ty'), 'tx'), may hold values 0 or 1
- sea_depth: float32 [1024, 8192], P(('comp', 'ty'), 'tx'), may hold values from 0.5 to 1.8
- sea_height: float32 [1024, 8192], P(('comp', 'ty'), 'tx'), may hold values from -3 to 3
- transport: float32 [2, 1024, 8192], P(None, ('comp', 'ty'), 'tx'), may hold values from -3 to 3
- tracers: float32 [2, 16, 1024, 8192], P(None, None, ('comp', 'ty'), 'tx'), may hold values from -6 to 6
Outputs:
- new_height: float32 [1024, 8192], P(('comp', 'ty'), 'tx')
- new_transport: float32 [2, 1024, 8192], P(None, ('comp', 'ty'), 'tx')
- new_tracers: float32 [2, 16, 1024, 8192], P(None, None, ('comp', 'ty'), 'tx')
Inputs may be any that keep to these rules, and one draw needn't show every extreme that they name: `margin_tile`: among the 256 blocks of one atmosphere owner (an aligned run of 256 rows), no ocean tile is named by more than 4 blocks. All entries of one block lie in one row of its tile: margin_cell[b, j] // 1024 is the same for every j.
All inputs are finite; a program needn't handle non-finite values. No bound on the sum of `land_mask` on one device may be relied on, other than what follows from the above.
Results may differ from a plain program's by a relative error of at most 0.000088.
Values sent between devices are 32-bit elements; how exact they have to be, the bound alone decides.
No kernel may reach another device: no remote copies, remote signals or barrier semaphores. Data moves between devices by JAX's collectives and lax.ppermute only.
A program may use at most 192 MiB of HBM per device.

v0:
```python
import math

import jax
import jax.numpy as jnp
from jax import lax
from jax.sharding import PartitionSpec as P

SUB = 3


damping = 0.95
advect = 0.15
diffuse = 0.1
exact = lax.Precision.HIGHEST


def with_halo(cells, sides, width):
    for axis, dim in sides:
        count = lax.axis_size(axis)
        ends = count - 1
        head = lax.slice_in_dim(cells, 0, width, axis=dim)
        tail = lax.slice_in_dim(cells, cells.shape[dim] - width, cells.shape[dim], axis=dim)
        cells = jnp.concatenate(
            [
                lax.ppermute(tail, axis, [(i, (i + 1) % count) for i in range(ends)]),
                cells,
                lax.ppermute(head, axis, [((i + 1) % count, i) for i in range(ends)]),
            ],
            axis=dim,
        )
    return cells


def four_sides(padded):
    eastern = padded[..., 1:-1, 2:]
    western = padded[..., 1:-1, :-2]
    northern = padded[..., 2:, 1:-1]
    southern = padded[..., :-2, 1:-1]
    return (eastern, western, northern, southern)


def momentum(pressure_sides, along_flow, across, ocean_mask, bottom, wind_x, wind_y):
    eastern, western, northern, southern = pressure_sides
    along_flow = ocean_mask * (
        damping * along_flow + (-0.5 * bottom * (eastern - western) + wind_x)
    )
    across = ocean_mask * (damping * across + (-0.5 * bottom * (northern - southern) + wind_y))
    return (along_flow, across)


def continuity(height, along_sides, across_sides, ocean_mask, source):
    divergence = along_sides[0] - along_sides[1] + across_sides[2] - across_sides[3]
    return ocean_mask * (height - 0.5 * divergence + source)


def horizontal(tracer_sides, mask_sides, tracers, transport, bottom):
    eastern, western, northern, southern = [
        edge_mask * near_value + (1.0 - edge_mask) * tracers
        for near_value, edge_mask in zip(tracer_sides, mask_sides)
    ]
    east_speed = transport[0] / bottom
    north_speed = transport[1] / bottom
    carried = (
        jnp.maximum(east_speed, 0.0) * (tracers - western)
        + jnp.minimum(east_speed, 0.0) * (eastern - tracers)
        + jnp.maximum(north_speed, 0.0) * (tracers - southern)
        + jnp.minimum(north_speed, 0.0) * (northern - tracers)
    )
    spread = eastern + western + northern + southern - 4.0 * tracers
    return tracers - advect * carried + diffuse * spread


def column_solve(heated, mixing):
    levels = heated.shape[1]
    nothing = jnp.zeros_like(mixing[0])
    ratios = []
    values = []
    last_ratio = nothing
    last_value = heated[:, 0]
    for k in range(levels):
        upper_mix = mixing[k] if k < levels - 1 else nothing
        lower_mix = mixing[k - 1] if k > 0 else nothing
        pivot_term = 1.0 + upper_mix + lower_mix
        right_side = heated[:, k]
        if k > 0:
            pivot_term = pivot_term + lower_mix * last_ratio
            right_side = right_side + lower_mix * last_value
        last_ratio = -upper_mix / pivot_term
        last_value = right_side / pivot_term
        ratios.append(last_ratio)
        values.append(last_value)
    result = [values[levels - 1]]
    for k in range(levels - 2, -1, -1):
        result.append(values[k] - ratios[k] * result[-1])
    return jnp.stack(result[::-1], axis=1)


def surface_and_mixing(moved, forcing):
    levels = moved.shape[1]
    depths = jnp.arange(levels, dtype=jnp.float32)
    absorb = jnp.exp(-depths / 3.0) - jnp.exp(-(depths + 1.0) / 3.0)
    heat = 0.5 * forcing[4][None] * absorb[:, None, None]
    heat = heat.at[0].add(0.5 * forcing[3])
    salt = jnp.zeros_like(heat).at[0].set(0.5 * forcing[5] - 0.3 * forcing[6])
    heated = moved + jnp.stack([heat, salt])
    mixing = (
        0.2 + 0.5 * (forcing[7] * forcing[7])[None] * jnp.exp(-depths[:-1] / 2.0)[:, None, None]
    )
    return column_solve(heated, mixing)


def local(
    atm_flux,
    margin_source,
    margin_cell,
    margin_weight,
    margin_tile,
    land_mask,
    sea_depth,
    sea_height,
    transport,
    tracers,
):
    ocean_mask = land_mask.astype(jnp.float32)
    levels = tracers.shape[1]
    tile_rows = sea_height.shape[0]
    tile_cols = sea_height.shape[1]
    planes = jnp.concatenate(
        [tracers.reshape(2 * levels, tile_rows, tile_cols), ocean_mask[None]], axis=0
    )
    tracer_band = with_halo(planes, ((("comp", "ty"), 1), ("tx", 2)), 1)
    band_sides = four_sides(tracer_band)
    tracer_sides = [edge_plane[:-1].reshape(tracers.shape) for edge_plane in band_sides]
    mask_sides = [edge_plane[-1] for edge_plane in band_sides]
    moved = horizontal(tracer_sides, mask_sides, tracers, transport, sea_depth)
    field_count = atm_flux.shape[0]
    block_count = margin_source.shape[0]
    block_width = margin_source.shape[1]
    tile_count = lax.axis_size(("comp", "ty", "tx"))
    capacity = 2 * block_count // tile_count
    slot_total = tile_count * capacity
    windows = atm_flux.reshape(field_count, block_count // 2, block_width)
    block_windows = jnp.repeat(windows, 2, axis=1)
    pick = (
        margin_source[:, :, None] == jnp.arange(block_width, dtype=jnp.int32)[None, None, :]
    ).astype(jnp.float32)
    picked = jnp.einsum("fbk,bjk->fbj", block_windows, pick, precision=exact)
    weighted = picked * margin_weight[None]
    target_tile = margin_tile[:, 0]
    tile_onehot = (target_tile[:, None] == jnp.arange(tile_count, dtype=jnp.int32)[None, :]).astype(
        jnp.float32
    )
    block_ids = jnp.arange(block_count, dtype=jnp.int32)
    earlier = (block_ids[:, None] > block_ids[None, :]).astype(jnp.float32)
    before = jnp.dot(earlier, tile_onehot, precision=exact)
    rank = jnp.sum(before * tile_onehot, axis=1).astype(jnp.int32)
    slot_index = target_tile * capacity + rank
    placing = (jnp.arange(slot_total, dtype=jnp.int32)[:, None] == slot_index[None, :]).astype(
        jnp.float32
    )
    outgoing = jnp.einsum("sb,fbj->fsj", placing, weighted, precision=exact)
    cell_values = jnp.dot(placing, margin_cell.astype(jnp.float32), precision=exact)
    cell_slots = cell_values.astype(jnp.int32)[None]
    arrived, arrived_cells = (
        lax.all_to_all(outgoing, ("comp", "ty", "tx"), split_axis=1, concat_axis=1, tiled=True),
        lax.all_to_all(cell_slots, ("comp", "ty", "tx"), split_axis=1, concat_axis=1, tiled=True),
    )
    cells = arrived_cells.reshape(-1, block_width)
    slot_rows = cells[:, 0] // tile_cols
    cell_cols = cells % tile_cols
    low_width = math.gcd(tile_cols, 128)
    high_count = tile_cols // low_width
    high_onehot = (
        (cell_cols // low_width)[:, :, None]
        == jnp.arange(high_count, dtype=jnp.int32)[None, None, :]
    ).astype(jnp.float32)
    low_onehot = (
        (cell_cols % low_width)[:, :, None] == jnp.arange(low_width, dtype=jnp.int32)[None, None, :]
    ).astype(jnp.float32)
    expanded = arrived[:, :, :, None] * high_onehot[None]
    row_values = jnp.einsum("fsjh,sjl->fshl", expanded, low_onehot, precision=exact)
    row_values = row_values.reshape(field_count, -1, tile_cols)
    row_onehot = (slot_rows[:, None] == jnp.arange(tile_rows, dtype=jnp.int32)[None, :]).astype(
        jnp.float32
    )
    forcing = jnp.einsum("sy,fsx->fyx", row_onehot, row_values, precision=exact)
    pressure_term = 0.5 * forcing[2]
    wind_x = 0.5 * forcing[0]
    wind_y = 0.5 * forcing[1]
    source = 0.1 * (forcing[6] - forcing[5])
    height = sea_height
    along_flow = transport[0]
    across = transport[1]
    for k in range(SUB):
        pressure = ocean_mask * (height + pressure_term)
        pressure_band = with_halo(pressure, ((("comp", "ty"), 0), ("tx", 1)), 1)
        along_flow, across = momentum(
            four_sides(pressure_band), along_flow, across, ocean_mask, sea_depth, wind_x, wind_y
        )
        flow_band = with_halo(jnp.stack([along_flow, across]), ((("comp", "ty"), 1), ("tx", 2)), 1)
        flow_sides = four_sides(flow_band)
        along_sides = [edge_plane[0] for edge_plane in flow_sides]
        across_sides = [edge_plane[1] for edge_plane in flow_sides]
        height = continuity(height, along_sides, across_sides, ocean_mask, source)
    solved = surface_and_mixing(moved, forcing)
    new_tracers = ocean_mask * solved + (1.0 - ocean_mask) * tracers
    return (height, jnp.stack([along_flow, across]), new_tracers)


def solution(mesh):
    in_specs = (
        P(None, ("comp", "ty", "tx")),
        P(("comp", "ty", "tx"), None),
        P(("comp", "ty", "tx"), None),
        P(("comp", "ty", "tx"), None),
        P(("comp", "ty", "tx"), None),
        P(("comp", "ty"), "tx"),
        P(("comp", "ty"), "tx"),
        P(("comp", "ty"), "tx"),
        P(None, ("comp", "ty"), "tx"),
        P(None, None, ("comp", "ty"), "tx"),
    )
    out_specs = (
        P(("comp", "ty"), "tx"),
        P(None, ("comp", "ty"), "tx"),
        P(None, None, ("comp", "ty"), "tx"),
    )
    return jax.shard_map(local, mesh=mesh, in_specs=in_specs, out_specs=out_specs, check_vma=False)
```

profile of v0, /device:TPU:98, one launch (start us, length us, event | category | flops | bytes accessed | tf_op | source)
XLA Modules:
  0.0 343.0 jit_solution(9252707325153266093)
XLA Ops:
  2.4 2.0 convolution_convert_fusion
  4.4 10.3 %all-to-all-start = ((s32[1,512,128]{2,0,1:T(1,128)}), s32[1,512,128]{2,0,1:T(1,128)}, u32[]{:S(2)}, u32[]{:S(2)}) async-start(s32[1,512,128]{2,0,1:T(1,128)} %bitcast.3), calls=%async_computation | async-start | bytes 524288 | tf_op jit(solution)/shard_map/all_to_all | solution.py:166
  18.2 3.9 %collective-permute-start.24 = (f32[33,1,1024]{2,1,0:T(1,128)S(1)}, f32[33,1,1024]{2,1,0:T(1,128)S(1)}, u32[]{:S(2)}, u32[]{:S(2)}) collective-permute-start(f32[33,1,1024]{2,1,0:T(1,128)S(1)} %get-tuple-element.87), channel_id=1, source_target_pairs={{0,8},{8,16},{16,24},{24,32},{32,40},{40,48},{48,56},{56,64},{64,7... | collective-permute-start | bytes 405512 | tf_op jit(solution)/shard_map/ppermute | solution.py:25
  22.1 3.5 %collective-permute-start.25 = (f32[33,1,1024]{2,1,0:T(1,128)S(1)}, f32[33,1,1024]{2,1,0:T(1,128)S(1)}, u32[]{:S(2)}, u32[]{:S(2)}) collective-permute-start(f32[33,1,1024]{2,1,0:T(1,128)S(1)} %get-tuple-element.88), channel_id=1, source_target_pairs={{8,0},{16,8},{24,16},{32,24},{40,32},{48,40},{56,48},{64,56},{72,6... | collective-permute-start | bytes 405512 | tf_op jit(solution)/shard_map/ppermute | solution.py:27
  25.8 19.1 %fusion.22 = f32[8,256,128]{2,0,1:T(8,128)S(1)} fusion(f32[8,256,128]{2,0,1:T(8,128)S(1)} %bitcast.269, s32[256,128]{1,0:T(8,128)S(1)} %copy-done.37, f32[256,128]{1,0:T(8,128)S(1)} %copy-done.38), kind=kOutput, calls=%fused_computation.36 | convolution fusion | flops 407109632 | bytes 2359296 | tf_op jit(solution)/shard_map/fbk,bjk->fbj/dot_general | solution.py:147
  47.9 2.0 pad_maximum_fusion.15
  53.3 1.9 collective-permute-start.27
  55.2 2.4 collective-permute-start.26
  61.4 2.3 broadcast_subtract_fusion.4
  63.8 10.9 %all-to-all-start.1 = ((f32[8,512,128]{2,0,1:T(8,128)}), f32[8,512,128]{2,0,1:T(8,128)}, u32[]{:S(2)}, u32[]{:S(2)}) async-start(f32[8,512,128]{2,0,1:T(8,128)} %copy.27), calls=%async_computation.1 | async-start | bytes 4194304 | tf_op jit(solution)/shard_map/all_to_all | solution.py:165
  74.7 31.4 %pad_maximum_fusion.8 = (f32[32,64,1024]{2,1,0:T(8,128)}, f32[32,64,1024]{2,1,0:T(8,128)}, f32[32,64,1024]{2,1,0:T(8,128)}, f32[32,64,1024]{2,1,0:T(8,128)}) fusion(f32[33,66,1]{2,1,0:T(8,128)S(1)} %copy.30, f32[33,1,1024]{2,1,0:T(1,128)S(1)} %copy-done.32, f32[33,1,1024]{2,1,0:T(1,128)S(1)} %copy-done.30, f32[1,64,1024]{2,1,0:T(8,128)S(1)} %get-tuple-element.146, ...), kind=kLoop, calls=%fused_computation.21 | loop fusion | flops 25165824 | bytes 42492944 | tf_op jit(solution)/shard_map/concatenate | solution.py:23
  108.7 27.9 %fusion.8 = f32[8,512,8,128]{3,2,0,1:T(8,128)} fusion(s32[512,128]{1,0:T(8,128)S(1)} %get-tuple-element.155, f32[512,128,8]{1,2,0:T(8,128)S(1)} %fusion.17, f32[8,512,128]{2,0,1:T(8,128)} %all-to-all-done.1), kind=kOutput, calls=%fused_computation.9 | convolution fusion | flops 6455033856 | bytes 21233664 | tf_op jit(solution)/shard_map/fsjh,sjl->fshl/dot_general | solution.py:181
  136.6 18.0 %reshape.262 = f32[8,512,1024]{2,0,1:T(8,128)} reshape(f32[8,512,8,128]{3,2,0,1:T(8,128)} %fusion.8) | data formatting | bytes 33554432 | tf_op jit(solution)/shard_map/reshape | solution.py:182
  154.6 21.3 %fusion.18 = f32[8,64,1024]{2,1,0:T(8,128)S(1)} fusion(f32[8,512,1024]{2,0,1:T(8,128)} %reshape.262, s32[512]{0:T(512)S(1)} %fusion.44), kind=kOutput, calls=%fused_computation.33 | convolution fusion | flops 3221258240 | bytes 18876416 | tf_op jit(solution)/shard_map/sy,fsx->fyx/dot_general | solution.py:186
  176.9 2.8 collective-permute-start.1
  179.7 5.4 %collective-permute-start = (f32[1,1024]{1,0:T(1,128)S(1)}, f32[1,1024]{1,0:T(1,128)S(1)}, u32[]{:S(2)}, u32[]{:S(2)}) collective-permute-start(f32[1,1024]{1,0:T(1,128)S(1)} %get-tuple-element.153), channel_id=1, source_target_pairs={{0,8},{8,16},{16,24},{24,32},{32,40},{40,48},{48,56},{56,64},{64,7... | collective-permute-start | bytes 12296 | tf_op jit(solution)/shard_map/ppermute | solution.py:25
  191.8 2.1 copy-done.4
  199.8 13.8 %fusion.13 = f32[2,16,64,1024]{3,2,1,0:T(8,128)S(1)} fusion(f32[1,1,64,1024]{3,2,1,0:T(8,128)} %get-tuple-element.122, f32[1,16,64,1024]{3,2,1,0:T(8,128)} %copy-done.4, f32[2,16,64,1024]{3,2,1,0:T(8,128)S(1)} %bitcast.236, f32[2,16,64,1024]{3,2,1,0:T(8,128)} %bitcast.242, f32[2,16,64,1024]{3,2,1,0:T(8,128)} %bitcast.241, f32[2,16,64,1024]{3,2,1,0:T(8,128)} %bitcast.240, ...), kind=kLoop, calls=%fused_computation.11 | loop fusion | flops 75497472 | bytes 57933824 | tf_op jit(solution)/shard_map/add | solution.py:105
  213.6 6.8 %subtract_dynamic-update-slice_fusion = (f32[2,16,64,1024]{3,2,1,0:T(8,128)}, f32[2,1,64,1024]{3,2,1,0:T(8,128)S(1)}, f32[2,1,64,1024]{3,2,1,0:T(8,128)S(1)}, f3...) fusion(f32[64,1024]{1,0:T(8,128)} %get-tuple-element.111, ...), kind=kLoop, calls=%fused_computation.81 | loop fusion | flops 9961471 | bytes 28311552
  225.7 2.1 collective-permute-start.2
  227.8 2.4 collective-permute-start.3
  231.1 2.0 collective-permute-done.3
  234.1 2.5 collective-permute-start.5
  236.6 5.8 %collective-permute-start.4 = (f32[2,1,1024]{2,1,0:T(1,128)S(1)}, f32[2,1,1024]{2,1,0:T(1,128)S(1)}, u32[]{:S(2)}, u32[]{:S(2)}) collective-permute-start(f32[2,1,1024]{2,1,0:T(1,128)S(1)} %get-tuple-element.138), channel_id=1, source_target_pairs={{0,8},{8,16},{16,24},{24,32},{32,40},{40,48},{48,56},{56,64},{64,7... | collective-permute-start | bytes 24584 | tf_op jit(solution)/shard_map/ppermute | solution.py:25
  244.3 1.9 collective-permute-start.6
  246.2 2.4 collective-permute-start.7
  249.5 2.4 collective-permute-done.7
  252.2 6.0 %collective-permute-start.9 = (f32[1,1024]{1,0:T(1,128)S(1)}, f32[1,1024]{1,0:T(1,128)S(1)}, u32[]{:S(2)}, u32[]{:S(2)}) collective-permute-start(f32[1,1024]{1,0:T(1,128)S(1)} %get-tuple-element.150), channel_id=1, source_target_pairs={{8,0},{16,8},{24,16},{32,24},{40,32},{48,40},{56,48},{64,56},{72,6... | collective-permute-start | bytes 12296 | tf_op jit(solution)/shard_map/ppermute | solution.py:27
  258.3 2.2 collective-permute-start.8
  261.4 3.9 %collective-permute-done.8 = f32[1,1024]{1,0:T(1,128)S(1)} collective-permute-done((f32[1,1024]{1,0:T(1,128)S(1)}, f32[1,1024]{1,0:T(1,128)S(1)}, u32[]{:S(2)}, u32[]{:S(2)}) %collective-permute-start.8) | collective-permute-done | bytes 4128 | tf_op jit(solution)/shard_map/ppermute | solution.py:25
  265.4 1.9 collective-permute-start.10
  267.3 2.4 collective-permute-start.11
  270.6 2.0 collective-permute-done.11
  272.9 2.7 collective-permute-start.13
  275.7 5.5 %collective-permute-start.12 = (f32[2,1,1024]{2,1,0:T(1,128)S(1)}, f32[2,1,1024]{2,1,0:T(1,128)S(1)}, u32[]{:S(2)}, u32[]{:S(2)}) collective-permute-start(f32[2,1,1024]{2,1,0:T(1,128)S(1)} %get-tuple-element.136), channel_id=1, source_target_pairs={{0,8},{8,16},{16,24},{24,32},{32,40},{40,48},{48,56},{56,64},{64,7... | collective-permute-start | bytes 24584 | tf_op jit(solution)/shard_map/ppermute | solution.py:25
  282.8 1.9 collective-permute-start.14
  284.7 2.4 collective-permute-start.15
  288.0 2.4 collective-permute-done.15
  291.4 6.4 %collective-permute-start.16 = (f32[1,1024]{1,0:T(1,128)S(1)}, f32[1,1024]{1,0:T(1,128)S(1)}, u32[]{:S(2)}, u32[]{:S(2)}) collective-permute-start(f32[1,1024]{1,0:T(1,128)S(1)} %get-tuple-element.148), channel_id=1, source_target_pairs={{0,8},{8,16},{16,24},{24,32},{32,40},{40,48},{48,56},{56,64},{64,7... | collective-permute-start | bytes 12296 | tf_op jit(solution)/shard_map/ppermute | solution.py:25
  297.9 1.9 collective-permute-start.17
  300.8 5.0 %collective-permute-done.17 = f32[1,1024]{1,0:T(1,128)S(1)} collective-permute-done((f32[1,1024]{1,0:T(1,128)S(1)}, f32[1,1024]{1,0:T(1,128)S(1)}, u32[]{:S(2)}, u32[]{:S(2)}) %collective-permute-start.17) | collective-permute-done | bytes 4128 | tf_op jit(solution)/shard_map/ppermute | solution.py:27
  305.8 1.9 collective-permute-start.18
  307.8 2.4 collective-permute-start.19
  311.1 1.9 collective-permute-done.19
  315.3 6.3 %collective-permute-start.20 = (f32[2,1,1024]{2,1,0:T(1,128)S(1)}, f32[2,1,1024]{2,1,0:T(1,128)S(1)}, u32[]{:S(2)}, u32[]{:S(2)}) collective-permute-start(f32[2,1,1024]{2,1,0:T(1,128)S(1)} %get-tuple-element.134), channel_id=1, source_target_pairs={{0,8},{8,16},{16,24},{24,32},{32,40},{40,48},{48,56},{56,64},{64,7... | collective-permute-start | bytes 24584 | tf_op jit(solution)/shard_map/ppermute | solution.py:25
  321.7 12.4 %multiply_add_fusion = f32[2,16,64,1024]{3,2,1,0:T(8,128)} fusion(f32[2,16,64,1024]{3,2,1,0:T(8,128)} %param.23, f32[2,16,64,1024]{3,2,1,0:T(8,128)} %constant_dynamic-update-slice_fusion, f32[64,1024]{1,0:T(8,128)} %get-tuple-element.147, f32[64,1024]{1,0:T(8,128)S(1)} %copy-done.33), kind=kLoop, calls=%fused_computation.25 | loop fusion | flops 6291456 | bytes 25690112 | tf_op jit(solution)/shard_map/add | solution.py:206
  336.1 2.4 collective-permute-start.23
  339.4 2.4 collective-permute-done.23
  (181 shorter events, 55.3 us)
Async XLA Ops:
  0.6 25.0 %copy-start = (f32[8,16384]{1,0:T(8,128)S(1)}, f32[8,16384]{1,0:T(8,128)}, u32[]{:S(2)}) copy-start(f32[8,16384]{1,0:T(8,128)} %param.14) | copy-start | bytes 1572868
  0.6 25.1 %copy-start.38 = (f32[256,128]{1,0:T(8,128)S(1)}, f32[256,128]{1,0:T(8,128)}, u32[]{:S(2)}) copy-start(f32[256,128]{1,0:T(8,128)} %param.17) | copy-start | bytes 393220
  0.7 25.1 %copy-start.37 = (s32[256,128]{1,0:T(8,128)S(1)}, s32[256,128]{1,0:T(8,128)}, u32[]{:S(2)}) copy-start(s32[256,128]{1,0:T(8,128)} %param.15) | copy-start | bytes 393220
  4.4 59.4 %all-to-all-start = ((s32[1,512,128]{2,0,1:T(1,128)}), s32[1,512,128]{2,0,1:T(1,128)}, u32[]{:S(2)}, u32[]{:S(2)}) async-start(s32[1,512,128]{2,0,1:T(1,128)} %bitcast.3), calls=%async_computation | async-start | bytes 524288 | tf_op jit(solution)/shard_map/all_to_all | solution.py:166
  18.1 28.6 %copy-start.6 = (f32[64,1024]{1,0:T(8,128)S(1)}, f32[64,1024]{1,0:T(8,128)}, u32[]{:S(2)}) copy-start(f32[64,1024]{1,0:T(8,128)} %param.20) | copy-start | bytes 786436
  18.2 28.6 %copy-start.27 = (f32[2,64,1024]{2,1,0:T(8,128)S(1)}, f32[2,64,1024]{2,1,0:T(8,128)}, u32[]{:S(2)}) copy-start(f32[2,64,1024]{2,1,0:T(8,128)} %param.22) | copy-start | bytes 1572868
  18.2 29.6 %collective-permute-start.24 = (f32[33,1,1024]{2,1,0:T(1,128)S(1)}, f32[33,1,1024]{2,1,0:T(1,128)S(1)}, u32[]{:S(2)}, u32[]{:S(2)}) collective-permute-start(f32[33,1,1024]{2,1,0:T(1,128)S(1)} %get-tuple-element.87), channel_id=1, source_target_pairs={{0,8},{8,16},{16,24},{24,32},{32,40},{40,48},{48,56},{56,64},{64,7... | collective-permute-start | bytes 405512 | tf_op jit(solution)/shard_map/ppermute | solution.py:25
  22.1 25.7 %collective-permute-start.25 = (f32[33,1,1024]{2,1,0:T(1,128)S(1)}, f32[33,1,1024]{2,1,0:T(1,128)S(1)}, u32[]{:S(2)}, u32[]{:S(2)}) collective-permute-start(f32[33,1,1024]{2,1,0:T(1,128)S(1)} %get-tuple-element.88), channel_id=1, source_target_pairs={{8,0},{16,8},{24,16},{32,24},{40,32},{48,40},{56,48},{64,56},{72,6... | collective-permute-start | bytes 405512 | tf_op jit(solution)/shard_map/ppermute | solution.py:27
  25.7 22.1 %slice-start = ((s8[8388608]{0:T(1024)(128)(4,1)}), s8[4194304]{0:T(1024)(128)(4,1)S(1)}, s32[]{:S(2)}) async-start(s8[8388608]{0:T(1024)(128)(4,1)} %bitcast.232), calls=%async_computation.2 | async-start | bytes 8388608
  25.8 22.1 %slice-start.1 = ((s8[8388608]{0:T(1024)(128)(4,1)}), s8[4194304]{0:T(1024)(128)(4,1)S(1)}, s32[]{:S(2)}) async-start(s8[8388608]{0:T(1024)(128)(4,1)} %bitcast.232), calls=%async_computation.3 | async-start | bytes 8388608
  53.3 7.5 %collective-permute-start.27 = (f32[33,66,1]{1,2,0:T(1,128)S(1)}, f32[33,66,1]{1,2,0:T(1,128)S(1)}, u32[]{:S(2)}, u32[]{:S(2)}) collective-permute-start(f32[33,66,1]{1,2,0:T(1,128)S(1)} %copy.31), channel_id=1, source_target_pairs={{1,0},{2,1},{3,2},{4,3},{5,4},{6,5},{7,6},{9,8},{10,9},{11,10},{12... | collective-permute-start | bytes 26144 | tf_op jit(solution)/shard_map/ppermute | solution.py:27
  55.2 5.1 %collective-permute-start.26 = (f32[33,66,1]{1,2,0:T(1,128)S(1)}, f32[33,66,1]{1,2,0:T(1,128)S(1)}, u32[]{:S(2)}, u32[]{:S(2)}) collective-permute-start(f32[33,66,1]{1,2,0:T(1,128)S(1)} %copy.29), channel_id=1, source_target_pairs={{0,1},{1,2},{2,3},{3,4},{4,5},{5,6},{6,7},{8,9},{9,10},{10,11},{11... | collective-permute-start | bytes 26144 | tf_op jit(solution)/shard_map/ppermute | solution.py:25
  61.4 13.3 %copy-start.32 = (f32[33,1,1024]{2,1,0:T(1,128)S(1)}, f32[33,1,1024]{2,1,0:T(1,128)}, u32[]{:S(2)}) copy-start(f32[33,1,1024]{2,1,0:T(1,128)} %copy-done.31) | copy-start | bytes 405508
  63.8 44.9 %all-to-all-start.1 = ((f32[8,512,128]{2,0,1:T(8,128)}), f32[8,512,128]{2,0,1:T(8,128)}, u32[]{:S(2)}, u32[]{:S(2)}) async-start(f32[8,512,128]{2,0,1:T(8,128)} %copy.27), calls=%async_computation.1 | async-start | bytes 4194304 | tf_op jit(solution)/shard_map/all_to_all | solution.py:165
  154.6 22.2 %copy-start.5 = (s32[64,1024]{1,0:T(8,128)S(1)}, s32[64,1024]{1,0:T(8,128)}, u32[]{:S(2)}) copy-start(s32[64,1024]{1,0:T(8,128)} %param.19) | copy-start | bytes 786436
  154.6 22.2 %copy-start.35 = (f32[64,1024]{1,0:T(8,128)S(1)}, f32[64,1024]{1,0:T(8,128)}, u32[]{:S(2)}) copy-start(f32[64,1024]{1,0:T(8,128)} %param.21) | copy-start | bytes 786436
  175.9 15.9 %copy-start.2 = (f32[8,64,1024]{2,1,0:T(8,128)}, f32[8,64,1024]{2,1,0:T(8,128)S(1)}, u32[]{:S(2)}) copy-start(f32[8,64,1024]{2,1,0:T(8,128)S(1)} %fusion.18) | copy-start | bytes 6291460
  176.9 48.8 %collective-permute-start.1 = (f32[1,1024]{1,0:T(1,128)S(1)}, f32[1,1024]{1,0:T(1,128)S(1)}, u32[]{:S(2)}, u32[]{:S(2)}) collective-permute-start(f32[1,1024]{1,0:T(1,128)S(1)} %get-tuple-element.152), channel_id=1, source_target_pairs={{8,0},{16,8},{24,16},{32,24},{40,32},{48,40},{56,48},{64,56},{72,6... | collective-permute-start | bytes 12296 | tf_op jit(solution)/shard_map/ppermute | solution.py:27
  179.7 45.9 %collective-permute-start = (f32[1,1024]{1,0:T(1,128)S(1)}, f32[1,1024]{1,0:T(1,128)S(1)}, u32[]{:S(2)}, u32[]{:S(2)}) collective-permute-start(f32[1,1024]{1,0:T(1,128)S(1)} %get-tuple-element.153), channel_id=1, source_target_pairs={{0,8},{8,16},{16,24},{24,32},{32,40},{40,48},{48,56},{56,64},{64,7... | collective-permute-start | bytes 12296 | tf_op jit(solution)/shard_map/ppermute | solution.py:25
  220.4 21.9 %copy-start.17 = (f32[64,1024]{1,0:T(8,128)S(1)}, f32[64,1024]{1,0:T(8,128)}, u32[]{:S(2)}) copy-start(f32[64,1024]{1,0:T(8,128)} %get-tuple-element.51) | copy-start | bytes 786436
  220.4 31.5 %copy-start.36 = (f32[64,1024]{1,0:T(8,128)S(1)}, f32[64,1024]{1,0:T(8,128)}, u32[]{:S(2)}) copy-start(f32[64,1024]{1,0:T(8,128)} %param.21) | copy-start | bytes 786436
  222.2 38.3 %copy-start.8 = (f32[64,1024]{1,0:T(8,128)S(1)}, f32[64,1024]{1,0:T(8,128)}, u32[]{:S(2)}) copy-start(f32[64,1024]{1,0:T(8,128)} %get-tuple-element.54) | copy-start | bytes 786436
  225.7 55.5 %copy-start.7 = (f32[64,1024]{1,0:T(8,128)S(1)}, f32[64,1024]{1,0:T(8,128)}, u32[]{:S(2)}) copy-start(f32[64,1024]{1,0:T(8,128)} %get-tuple-element.57) | copy-start | bytes 786436
  225.7 5.3 %collective-permute-start.2 = (f32[66,1]{1,0:T(8,128)S(1)}, f32[66,1]{1,0:T(8,128)S(1)}, u32[]{:S(2)}, u32[]{:S(2)}) collective-permute-start(f32[66,1]{1,0:T(8,128)S(1)} %get-tuple-element.143), channel_id=1, source_target_pairs={{1,0},{2,1},{3,2},{4,3},{5,4},{6,5},{7,6},{9,8},{10,9},{11,10},{12... | collective-permute-start | bytes 800 | tf_op jit(solution)/shard_map/ppermute | solution.py:27
  227.8 5.3 %collective-permute-start.3 = (f32[66,1]{1,0:T(8,128)S(1)}, f32[66,1]{1,0:T(8,128)S(1)}, u32[]{:S(2)}, u32[]{:S(2)}) collective-permute-start(f32[66,1]{1,0:T(8,128)S(1)} %get-tuple-element.144), channel_id=1, source_target_pairs={{0,1},{1,2},{2,3},{3,4},{4,5},{5,6},{6,7},{8,9},{9,10},{10,11},{11... | collective-permute-start | bytes 800 | tf_op jit(solution)/shard_map/ppermute | solution.py:25
  234.1 9.2 %collective-permute-start.5 = (f32[2,1,1024]{2,1,0:T(1,128)S(1)}, f32[2,1,1024]{2,1,0:T(1,128)S(1)}, u32[]{:S(2)}, u32[]{:S(2)}) collective-permute-start(f32[2,1,1024]{2,1,0:T(1,128)S(1)} %get-tuple-element.137), channel_id=1, source_target_pairs={{8,0},{16,8},{24,16},{32,24},{40,32},{48,40},{56,48},{64,56},{72,6... | collective-permute-start | bytes 24584 | tf_op jit(solution)/shard_map/ppermute | solution.py:27
  236.6 7.7 %collective-permute-start.4 = (f32[2,1,1024]{2,1,0:T(1,128)S(1)}, f32[2,1,1024]{2,1,0:T(1,128)S(1)}, u32[]{:S(2)}, u32[]{:S(2)}) collective-permute-start(f32[2,1,1024]{2,1,0:T(1,128)S(1)} %get-tuple-element.138), channel_id=1, source_target_pairs={{0,8},{8,16},{16,24},{24,32},{32,40},{40,48},{48,56},{56,64},{64,7... | collective-permute-start | bytes 24584 | tf_op jit(solution)/shard_map/ppermute | solution.py:25
  244.3 5.2 %collective-permute-start.6 = (f32[2,66,1]{2,1,0:T(8,128)S(1)}, f32[2,66,1]{2,1,0:T(8,128)S(1)}, u32[]{:S(2)}, u32[]{:S(2)}) collective-permute-start(f32[2,66,1]{2,1,0:T(8,128)S(1)} %get-tuple-element.131), channel_id=1, source_target_pairs={{1,0},{2,1},{3,2},{4,3},{5,4},{6,5},{7,6},{9,8},{10,9},{11,10},{12... | collective-permute-start | bytes 1592 | tf_op jit(solution)/shard_map/ppermute | solution.py:27
  246.2 5.7 %collective-permute-start.7 = (f32[2,66,1]{2,1,0:T(8,128)S(1)}, f32[2,66,1]{2,1,0:T(8,128)S(1)}, u32[]{:S(2)}, u32[]{:S(2)}) collective-permute-start(f32[2,66,1]{2,1,0:T(8,128)S(1)} %get-tuple-element.132), channel_id=1, source_target_pairs={{0,1},{1,2},{2,3},{3,4},{4,5},{5,6},{6,7},{8,9},{9,10},{10,11},{11... | collective-permute-start | bytes 1592 | tf_op jit(solution)/shard_map/ppermute | solution.py:25
  252.2 9.2 %collective-permute-start.9 = (f32[1,1024]{1,0:T(1,128)S(1)}, f32[1,1024]{1,0:T(1,128)S(1)}, u32[]{:S(2)}, u32[]{:S(2)}) collective-permute-start(f32[1,1024]{1,0:T(1,128)S(1)} %get-tuple-element.150), channel_id=1, source_target_pairs={{8,0},{16,8},{24,16},{32,24},{40,32},{48,40},{56,48},{64,56},{72,6... | collective-permute-start | bytes 12296 | tf_op jit(solution)/shard_map/ppermute | solution.py:27
  258.3 7.0 %collective-permute-start.8 = (f32[1,1024]{1,0:T(1,128)S(1)}, f32[1,1024]{1,0:T(1,128)S(1)}, u32[]{:S(2)}, u32[]{:S(2)}) collective-permute-start(f32[1,1024]{1,0:T(1,128)S(1)} %get-tuple-element.151), channel_id=1, source_target_pairs={{0,8},{8,16},{16,24},{24,32},{32,40},{40,48},{48,56},{56,64},{64,7... | collective-permute-start | bytes 12296 | tf_op jit(solution)/shard_map/ppermute | solution.py:25
  265.4 5.2 %collective-permute-start.10 = (f32[66,1]{1,0:T(8,128)S(1)}, f32[66,1]{1,0:T(8,128)S(1)}, u32[]{:S(2)}, u32[]{:S(2)}) collective-permute-start(f32[66,1]{1,0:T(8,128)S(1)} %get-tuple-element.141), channel_id=1, source_target_pairs={{1,0},{2,1},{3,2},{4,3},{5,4},{6,5},{7,6},{9,8},{10,9},{11,10},{12... | collective-permute-start | bytes 800 | tf_op jit(solution)/shard_map/ppermute | solution.py:27
  267.3 5.3 %collective-permute-start.11 = (f32[66,1]{1,0:T(8,128)S(1)}, f32[66,1]{1,0:T(8,128)S(1)}, u32[]{:S(2)}, u32[]{:S(2)}) collective-permute-start(f32[66,1]{1,0:T(8,128)S(1)} %get-tuple-element.142), channel_id=1, source_target_pairs={{0,1},{1,2},{2,3},{3,4},{4,5},{5,6},{6,7},{8,9},{9,10},{10,11},{11... | collective-permute-start | bytes 800 | tf_op jit(solution)/shard_map/ppermute | solution.py:25
  270.5 51.1 %copy-start.33 = (f32[64,1024]{1,0:T(8,128)S(1)}, f32[64,1024]{1,0:T(8,128)}, u32[]{:S(2)}) copy-start(f32[64,1024]{1,0:T(8,128)} %get-tuple-element.145) | copy-start | bytes 786436
  272.9 9.2 %collective-permute-start.13 = (f32[2,1,1024]{2,1,0:T(1,128)S(1)}, f32[2,1,1024]{2,1,0:T(1,128)S(1)}, u32[]{:S(2)}, u32[]{:S(2)}) collective-permute-start(f32[2,1,1024]{2,1,0:T(1,128)S(1)} %get-tuple-element.135), channel_id=1, source_target_pairs={{8,0},{16,8},{24,16},{32,24},{40,32},{48,40},{56,48},{64,56},{72,6... | collective-permute-start | bytes 24584 | tf_op jit(solution)/shard_map/ppermute | solution.py:27
  275.7 7.0 %collective-permute-start.12 = (f32[2,1,1024]{2,1,0:T(1,128)S(1)}, f32[2,1,1024]{2,1,0:T(1,128)S(1)}, u32[]{:S(2)}, u32[]{:S(2)}) collective-permute-start(f32[2,1,1024]{2,1,0:T(1,128)S(1)} %get-tuple-element.136), channel_id=1, source_target_pairs={{0,8},{8,16},{16,24},{24,32},{32,40},{40,48},{48,56},{56,64},{64,7... | collective-permute-start | bytes 24584 | tf_op jit(solution)/shard_map/ppermute | solution.py:25
  282.8 5.2 %collective-permute-start.14 = (f32[2,66,1]{2,1,0:T(8,128)S(1)}, f32[2,66,1]{2,1,0:T(8,128)S(1)}, u32[]{:S(2)}, u32[]{:S(2)}) collective-permute-start(f32[2,66,1]{2,1,0:T(8,128)S(1)} %get-tuple-element.129), channel_id=1, source_target_pairs={{1,0},{2,1},{3,2},{4,3},{5,4},{6,5},{7,6},{9,8},{10,9},{11,10},{12... | collective-permute-start | bytes 1592 | tf_op jit(solution)/shard_map/ppermute | solution.py:27
  284.7 5.7 %collective-permute-start.15 = (f32[2,66,1]{2,1,0:T(8,128)S(1)}, f32[2,66,1]{2,1,0:T(8,128)S(1)}, u32[]{:S(2)}, u32[]{:S(2)}) collective-permute-start(f32[2,66,1]{2,1,0:T(8,128)S(1)} %get-tuple-element.130), channel_id=1, source_target_pairs={{0,1},{1,2},{2,3},{3,4},{4,5},{5,6},{6,7},{8,9},{9,10},{10,11},{11... | collective-permute-start | bytes 1592 | tf_op jit(solution)/shard_map/ppermute | solution.py:25
  291.4 9.3 %collective-permute-start.16 = (f32[1,1024]{1,0:T(1,128)S(1)}, f32[1,1024]{1,0:T(1,128)S(1)}, u32[]{:S(2)}, u32[]{:S(2)}) collective-permute-start(f32[1,1024]{1,0:T(1,128)S(1)} %get-tuple-element.148), channel_id=1, source_target_pairs={{0,8},{8,16},{16,24},{24,32},{32,40},{40,48},{48,56},{56,64},{64,7... | collective-permute-start | bytes 12296 | tf_op jit(solution)/shard_map/ppermute | solution.py:25
  297.9 7.9 %collective-permute-start.17 = (f32[1,1024]{1,0:T(1,128)S(1)}, f32[1,1024]{1,0:T(1,128)S(1)}, u32[]{:S(2)}, u32[]{:S(2)}) collective-permute-start(f32[1,1024]{1,0:T(1,128)S(1)} %get-tuple-element.149), channel_id=1, source_target_pairs={{8,0},{16,8},{24,16},{32,24},{40,32},{48,40},{56,48},{64,56},{72,6... | collective-permute-start | bytes 12296 | tf_op jit(solution)/shard_map/ppermute | solution.py:27
  305.8 5.3 %collective-permute-start.18 = (f32[66,1]{1,0:T(8,128)S(1)}, f32[66,1]{1,0:T(8,128)S(1)}, u32[]{:S(2)}, u32[]{:S(2)}) collective-permute-start(f32[66,1]{1,0:T(8,128)S(1)} %get-tuple-element.139), channel_id=1, source_target_pairs={{1,0},{2,1},{3,2},{4,3},{5,4},{6,5},{7,6},{9,8},{10,9},{11,10},{12... | collective-permute-start | bytes 800 | tf_op jit(solution)/shard_map/ppermute | solution.py:27
  307.8 5.3 %collective-permute-start.19 = (f32[66,1]{1,0:T(8,128)S(1)}, f32[66,1]{1,0:T(8,128)S(1)}, u32[]{:S(2)}, u32[]{:S(2)}) collective-permute-start(f32[66,1]{1,0:T(8,128)S(1)} %get-tuple-element.140), channel_id=1, source_target_pairs={{0,1},{1,2},{2,3},{3,4},{4,5},{5,6},{6,7},{8,9},{9,10},{10,11},{11... | collective-permute-start | bytes 800 | tf_op jit(solution)/shard_map/ppermute | solution.py:25
  313.4 20.7 %collective-permute-start.21 = (f32[2,1,1024]{2,1,0:T(1,128)S(1)}, f32[2,1,1024]{2,1,0:T(1,128)S(1)}, u32[]{:S(2)}, u32[]{:S(2)}) collective-permute-start(f32[2,1,1024]{2,1,0:T(1,128)S(1)} %get-tuple-element.133), channel_id=1, source_target_pairs={{8,0},{16,8},{24,16},{32,24},{40,32},{48,40},{56,48},{64,56},{72,6... | collective-permute-start | bytes 24584 | tf_op jit(solution)/shard_map/ppermute | solution.py:27
  315.3 18.8 %collective-permute-start.20 = (f32[2,1,1024]{2,1,0:T(1,128)S(1)}, f32[2,1,1024]{2,1,0:T(1,128)S(1)}, u32[]{:S(2)}, u32[]{:S(2)}) collective-permute-start(f32[2,1,1024]{2,1,0:T(1,128)S(1)} %get-tuple-element.134), channel_id=1, source_target_pairs={{0,8},{8,16},{16,24},{24,32},{32,40},{40,48},{48,56},{56,64},{64,7... | collective-permute-start | bytes 24584 | tf_op jit(solution)/shard_map/ppermute | solution.py:25
  321.7 21.1 %copy-start.1 = (f32[8,16384]{1,0:T(8,128)S(1)}, f32[8,16384]{1,0:T(8,128)}, u32[]{:S(2)}) copy-start(f32[8,16384]{1,0:T(8,128)} %param.14) | copy-start | bytes 1572868
  321.7 20.1 %copy-start.34 = (f32[64,1024]{1,0:T(8,128)S(1)}, f32[64,1024]{1,0:T(8,128)}, u32[]{:S(2)}) copy-start(f32[64,1024]{1,0:T(8,128)} %get-tuple-element.72) | copy-start | bytes 786436
  334.2 5.2 %collective-permute-start.22 = (f32[2,66,1]{2,1,0:T(8,128)S(1)}, f32[2,66,1]{2,1,0:T(8,128)S(1)}, u32[]{:S(2)}, u32[]{:S(2)}) collective-permute-start(f32[2,66,1]{2,1,0:T(8,128)S(1)} %get-tuple-element.127), channel_id=1, source_target_pairs={{1,0},{2,1},{3,2},{4,3},{5,4},{6,5},{7,6},{9,8},{10,9},{11,10},{12... | collective-permute-start | bytes 1592 | tf_op jit(solution)/shard_map/ppermute | solution.py:27
  336.1 5.7 %collective-permute-start.23 = (f32[2,66,1]{2,1,0:T(8,128)S(1)}, f32[2,66,1]{2,1,0:T(8,128)S(1)}, u32[]{:S(2)}, u32[]{:S(2)}) collective-permute-start(f32[2,66,1]{2,1,0:T(8,128)S(1)} %get-tuple-element.128), channel_id=1, source_target_pairs={{0,1},{1,2},{2,3},{3,4},{4,5},{5,6},{6,7},{8,9},{9,10},{10,11},{11... | collective-permute-start | bytes 1592 | tf_op jit(solution)/shard_map/ppermute | solution.py:25
  (27 other events, 201.4 us)
where the time goes:
time: 350 us; the launch traced here: 343 us
  starting transfers between devices  109 us (31%)
  other arithmetic  99.8 us (29%)
  matrix products  73.1 us (21%)
  local copies, waits for them, and re-layouts  35.2 us (10%)
  waiting for transfers between devices  24.5 us (7%)
    ppermute x14, starting transfers between devices, with_halo(): lax.ppermute(tail, axis, [(i, (i + 1) % count) for i in range(ends)])  52.4 us
    ppermute x14, starting transfers between devices, with_halo(): lax.ppermute(head, axis, [((i + 1) % count, i) for i in range(ends)])  35 us
    concatenate x1, other arithmetic, with_halo(): jnp.concatenate([lax.ppermute(tail, axis, [(i, (i + 1) % count) for i in...  31.4 us
    dot_general x1, matrix products, local(): jnp.einsum('fsjh,sjl->fshl', expanded, low_onehot, precision=exact)  27.9 us
    dot_general x1, matrix products, local(): forcing = jnp.einsum('sy,fsx->fyx', row_onehot, row_values, precision=exact)  21.3 us
    ppermute x14, waiting for transfers between devices, with_halo(): lax.ppermute(tail, axis, [(i, (i + 1) % count) for i in range(ends)])  19.5 us
    dot_general x1, matrix products, local(): picked = jnp.einsum('fbk,bjk->fbj', block_windows, pick, precision=exact)  19.1 us
    reshape x1, local copies, waits for them, and re-layouts, local(): row_values = row_values.reshape(field_count, -1, tile_cols)  18 us
  transfers between devices with their start and end apart: 30, of which 11 were waited for; matrix products, arithmetic and copies ran while one was open for 37% of the time, Pallas kernels for 0%

commit v1 on v0

v1 whole, which is shorter than its diff:
```python
import functools

import jax
import jax.numpy as jnp
import numpy as np
from jax import lax
from jax.experimental import pallas as pl
from jax.experimental.pallas import tpu as pltpu
from jax.sharding import PartitionSpec as P

SUB = 3
EDGE = 8
LANES = 128
EVERY = ("comp", "ty", "tx")
ROWS = ("comp", "ty")
f32 = jnp.float32
i32 = jnp.int32
VM = pl.BlockSpec(memory_space=pltpu.VMEM)
SM = pl.BlockSpec(memory_space=pltpu.SMEM)


def params(mib):
    return pltpu.CompilerParams(vmem_limit_bytes=mib << 20)


def pack_kernel(tile_ref, flux_ref, source_ref, cell_ref, weight_ref, first_ref, second_ref, count_ref):
    blocks = source_ref.shape[0]
    tiles = first_ref.shape[0]
    group = 4
    first_ref[...] = jnp.zeros_like(first_ref)
    second_ref[...] = jnp.zeros_like(second_ref)

    def clear(t, carry):
        count_ref[t] = 0
        return carry

    lax.fori_loop(0, tiles, clear, 0)
    sub = lax.broadcasted_iota(i32, (8, LANES), 0)

    def step(i, carry):
        for g in range(group):
            w = i * group + g
            x = flux_ref[:, pl.ds(pl.multiple_of(w * LANES, LANES), LANES)]
            after = pltpu.roll(x, 1, 0)
            six = pltpu.roll(x, 5, 0)
            five = pltpu.roll(x, 6, 0)
            y = jnp.where((sub == 4) | (sub == 5), after, x)
            y = jnp.where(sub == 6, 0.5 * after - 0.3 * x, y)
            y = jnp.where(sub == 3, 0.1 * (six - five), y)
            for half in range(2):
                b = 2 * w + half
                tile = tile_ref[b]
                slot = count_ref[tile]
                count_ref[tile] = slot + 1
                index = jnp.broadcast_to(source_ref[pl.ds(b, 1), :], (8, LANES))
                picked = jnp.take_along_axis(y, index, axis=1)
                value = picked * jnp.broadcast_to(weight_ref[pl.ds(b, 1), :], (8, LANES))
                first_ref[tile, slot] = value[0:4]
                second_ref[tile, slot] = value[4:8]
                first_ref[tile, 4, pl.ds(slot, 1), :] = cell_ref[pl.ds(b, 1), :].astype(f32)
        return carry

    lax.fori_loop(0, blocks // (2 * group), step, 0)


def pack(tile, flux, source, cell, weight, tiles):
    return pl.pallas_call(
        pack_kernel,
        name="pack_margin",
        in_specs=[SM, VM, VM, VM, VM],
        out_specs=[VM, VM],
        out_shape=[
            jax.ShapeDtypeStruct((tiles, 5, 4, LANES), f32),
            jax.ShapeDtypeStruct((tiles, 4, 4, LANES), f32),
        ],
        scratch_shapes=[pltpu.SMEM((tiles,), i32)],
        compiler_params=params(24),
        cost_estimate=pl.CostEstimate(flops=1 << 22, bytes_accessed=4 << 20, transcendentals=0),
    )(tile, flux, source, cell, weight)


def spread_kernel(cells_ref, value_ref, out_ref, acc_ref, *, group):
    sources = value_ref.shape[0]
    rows = out_ref.shape[1]
    columns = out_ref.shape[2]
    high = columns // LANES
    depth = 4 * high
    acc_ref[...] = jnp.zeros_like(acc_ref)
    sub_high = lax.broadcasted_iota(i32, (high, LANES), 0)
    sub_low = lax.broadcasted_iota(i32, (LANES, LANES), 0)
    blank = jnp.zeros((LANES, LANES), jnp.bfloat16)

    def step(i, carry):
        for g in range(group):
            s = i * group + g
            cells = cells_ref[s, 4].astype(i32)
            highs = (cells & (columns - 1)) >> 7
            lows = cells & (LANES - 1)
            for pair in range(2):
                left = []
                right = []
                for k in (2 * pair, 2 * pair + 1):
                    value = value_ref[s, k]
                    coarse = value.astype(jnp.bfloat16).astype(f32)
                    fine = value - coarse
                    hit = jnp.broadcast_to(highs[k : k + 1], (high, LANES)) == sub_high
                    parts = [
                        jnp.where(hit, jnp.broadcast_to(piece[f : f + 1], (high, LANES)), 0.0)
                        for piece in (coarse, fine)
                        for f in range(4)
                    ]
                    left.append(jnp.concatenate(parts, axis=0).astype(jnp.bfloat16))
                    one = jnp.where(jnp.broadcast_to(lows[k : k + 1], (LANES, LANES)) == sub_low, 1.0, 0.0)
                    right.append(one.astype(jnp.bfloat16))
                lhs = jnp.concatenate(left, axis=1)
                rhs = jnp.concatenate(
                    [
                        jnp.concatenate([right[0], blank], axis=1),
                        jnp.concatenate([blank, right[1]], axis=1),
                    ],
                    axis=0,
                )
                both = lax.dot_general(lhs, rhs, (((1,), (1,)), ((), ())), preferred_element_type=f32)
                both = both[:depth] + both[depth:]
                for n in range(2):
                    k = 2 * pair + n
                    row = cells[k, 0] // columns
                    place = pl.ds(pl.multiple_of(row * depth, depth), depth)
                    acc_ref[place, :] += both[:, n * LANES : (n + 1) * LANES]
        return carry

    lax.fori_loop(0, sources // group, step, 0)
    for f in range(4):
        for h in range(high):
            for r in range(0, rows, 8):
                out_ref[f, r : r + 8, h * LANES : (h + 1) * LANES] = acc_ref[
                    pl.ds(r * depth + f * high + h, 8, stride=depth), :
                ]


def spread(cells, values, rows, columns, name):
    depth = 4 * columns // LANES
    group = 8 if values.shape[0] % 8 == 0 else 1
    return pl.pallas_call(
        functools.partial(spread_kernel, group=group),
        name=name,
        in_specs=[VM, VM],
        out_specs=VM,
        out_shape=jax.ShapeDtypeStruct((4, rows, columns), f32),
        scratch_shapes=[pltpu.VMEM((rows * depth, LANES), f32)],
        compiler_params=params(24),
        cost_estimate=pl.CostEstimate(flops=1 << 30, bytes_accessed=4 << 20, transcendentals=0),
    )(cells, values)


def edges_kernel(low_ref, high_ref, west_ref, east_ref, south_ref, north_ref, columns_ref):
    levels = low_ref.shape[0]
    rows = west_ref.shape[1]
    lane = lax.broadcasted_iota(i32, (rows, LANES), 1)
    lasts = jnp.zeros((rows, LANES), f32)
    firsts = jnp.zeros((rows, LANES), f32)
    for p in range(levels):
        south_ref[p : p + 1, :] = low_ref[p, 0:1, :]
        north_ref[p : p + 1, :] = high_ref[p, EDGE - 1 : EDGE, :]
        firsts = jnp.where(lane == p, west_ref[p, :, 0:1], firsts)
        lasts = jnp.where(lane == p, east_ref[p, :, LANES - 1 : LANES], lasts)
    columns_ref[0] = firsts
    columns_ref[1] = lasts


def edges(planes):
    levels, rows, columns = planes.shape
    last_row = rows // EDGE - 1
    last_lane = columns // LANES - 1
    return pl.pallas_call(
        edges_kernel,
        name="tracer_edges",
        grid=(1,),
        in_specs=[
            pl.BlockSpec((levels, EDGE, columns), lambda i: (0, 0, 0)),
            pl.BlockSpec((levels, EDGE, columns), lambda i: (0, last_row, 0)),
            pl.BlockSpec((levels, rows, LANES), lambda i: (0, 0, 0)),
            pl.BlockSpec((levels, rows, LANES), lambda i: (0, 0, last_lane)),
        ],
        out_specs=[
            pl.BlockSpec((levels, columns), lambda i: (0, 0)),
            pl.BlockSpec((levels, columns), lambda i: (0, 0)),
            pl.BlockSpec((2, rows, LANES), lambda i: (0, 0, 0)),
        ],
        out_shape=[
            jax.ShapeDtypeStruct((levels, columns), f32),
            jax.ShapeDtypeStruct((levels, columns), f32),
            jax.ShapeDtypeStruct((2, rows, LANES), f32),
        ],
        compiler_params=params(24),
        cost_estimate=pl.CostEstimate(flops=1 << 20, bytes_accessed=4 << 20, transcendentals=0),
    )(planes, planes, planes, planes)


def beside(array, amount, axis):
    return pltpu.roll(array, amount % array.shape[axis], axis)


def move_kernel(south_ref, north_ref, sides_ref, fixed_ref, side_fixed_ref, planes_ref, out_ref, coef_ref, *, per):
    step = pl.program_id(0)
    rows = planes_ref.shape[1]
    columns = planes_ref.shape[2]

    @pl.when(step == 0)
    def _():
        middle = slice(EDGE, EDGE + rows)
        mask = fixed_ref[0, middle, :]
        lane = lax.broadcasted_iota(i32, (rows, columns), 1)
        beyond = side_fixed_ref[0, middle, :]
        east = jnp.where(lane == columns - 1, beyond[:, 0:1], beside(mask, -1, 1))
        west = jnp.where(lane == 0, beyond[:, LANES - 1 : LANES], beside(mask, 1, 1))
        tall = fixed_ref[0]
        north = beside(tall, -1, 0)[middle]
        south = beside(tall, 1, 0)[middle]
        depth = fixed_ref[1, middle, :]
        u = fixed_ref[3, middle, :] / depth
        v = fixed_ref[4, middle, :] / depth
        east = mask * east * (0.1 - 0.15 * jnp.minimum(u, 0.0))
        west = mask * west * (0.1 + 0.15 * jnp.maximum(u, 0.0))
        north = mask * north * (0.1 - 0.15 * jnp.minimum(v, 0.0))
        south = mask * south * (0.1 + 0.15 * jnp.maximum(v, 0.0))
        coef_ref[0] = 1.0 - (east + west + north + south)
        coef_ref[1] = east
        coef_ref[2] = west
        coef_ref[3] = north
        coef_ref[4] = south

    lane_side = lax.broadcasted_iota(i32, (rows, LANES), 1)
    for n in range(per):
        p = step * per + n
        chosen = lane_side == p
        first = jnp.sum(jnp.where(chosen, sides_ref[0], 0.0), axis=1, keepdims=True)
        last = jnp.sum(jnp.where(chosen, sides_ref[1], 0.0), axis=1, keepdims=True)
        south_row = south_ref[pl.ds(p, 1), :]
        north_row = north_ref[pl.ds(p, 1), :]
        for r in range(0, rows, 8):
            span = slice(r, r + 8)
            q = planes_ref[n, span, :]
            lane = lax.broadcasted_iota(i32, (8, columns), 1)
            sub = lax.broadcasted_iota(i32, (8, columns), 0)
            east = jnp.where(lane == columns - 1, first[span], beside(q, -1, 1))
            west = jnp.where(lane == 0, last[span], beside(q, 1, 1))
            below = south_row if r == 0 else planes_ref[n, r - 1 : r, :]
            above = north_row if r + 8 == rows else planes_ref[n, r + 8 : r + 9, :]
            north = jnp.where(sub == 7, above, beside(q, -1, 0))
            south = jnp.where(sub == 0, below, beside(q, 1, 0))
            out_ref[n, span, :] = (
                coef_ref[0, span, :] * q
                + coef_ref[1, span, :] * east
                + coef_ref[2, span, :] * west
                + coef_ref[3, span, :] * north
                + coef_ref[4, span, :] * south
            )


def move(south, north, sides, fixed, side_fixed, planes):
    levels, rows, columns = planes.shape
    per = 4
    whole = lambda a: pl.BlockSpec(a.shape, lambda i: (0,) * a.ndim)
    return pl.pallas_call(
        functools.partial(move_kernel, per=per),
        name="tracer_move",
        grid=(levels // per,),
        in_specs=[
            whole(south),
            whole(north),
            whole(sides),
            whole(fixed),
            whole(side_fixed),
            pl.BlockSpec((per, rows, columns), lambda i: (i, 0, 0)),
        ],
        out_specs=pl.BlockSpec((per, rows, columns), lambda i: (i, 0, 0)),
        out_shape=jax.ShapeDtypeStruct(planes.shape, f32),
        scratch_shapes=[pltpu.VMEM((5, rows, columns), f32)],
        compiler_params=params(32),
        cost_estimate=pl.CostEstimate(flops=1 << 25, bytes_accessed=18 << 20, transcendentals=0),
    )(south, north, sides, fixed, side_fixed, planes)


def solve_kernel(flux_ref, mask_ref, moved_ref, out_ref, ratio_ref, *, absorb, decay):
    levels = moved_ref.shape[1]
    mask = mask_ref[...]
    heat_top = 0.5 * mask * flux_ref[0]
    sun = 0.5 * mask * flux_ref[1]
    salt_top = mask * flux_ref[2]
    stir = flux_ref[3]
    base = 0.2 * mask
    stir = 0.5 * mask * (stir * stir)
    above = jnp.zeros_like(mask)
    link = jnp.zeros_like(mask)
    heat_last = None
    salt_last = None
    for k in range(levels):
        heat = moved_ref[0, k] + absorb[k] * sun
        salt = moved_ref[1, k]
        if k == 0:
            heat = heat + heat_top
            salt = salt + salt_top
        below = base + decay[k] * stir if k < levels - 1 else jnp.zeros_like(mask)
        pivot = 1.0 + below + above
        if k > 0:
            pivot = pivot + above * link
            heat = heat + above * heat_last
            salt = salt + above * salt_last
        inverse = 1.0 / pivot
        link = -below * inverse
        heat_last = heat * inverse
        salt_last = salt * inverse
        above = below
        if k < levels - 1:
            ratio_ref[k] = link
        out_ref[0, k] = heat_last
        out_ref[1, k] = salt_last
    for k in range(levels - 2, -1, -1):
        link = ratio_ref[k]
        heat_last = out_ref[0, k] - link * heat_last
        salt_last = out_ref[1, k] - link * salt_last
        out_ref[0, k] = heat_last
        out_ref[1, k] = salt_last


def solve(flux, mask, moved):
    count, levels, rows, columns = moved.shape
    depths = np.arange(levels, dtype=np.float64)
    absorb = tuple(float(a) for a in np.exp(-depths / 3.0) - np.exp(-(depths + 1.0) / 3.0))
    decay = tuple(float(a) for a in np.exp(-depths / 2.0))
    return pl.pallas_call(
        functools.partial(solve_kernel, absorb=absorb, decay=decay),
        name="column_solve",
        grid=(rows // 8,),
        in_specs=[
            pl.BlockSpec((4, 8, columns), lambda i: (0, i, 0)),
            pl.BlockSpec((8, columns), lambda i: (i, 0)),
            pl.BlockSpec((count, levels, 8, columns), lambda i: (0, 0, i, 0)),
        ],
        out_specs=pl.BlockSpec((count, levels, 8, columns), lambda i: (0, 0, i, 0)),
        out_shape=jax.ShapeDtypeStruct(moved.shape, f32),
        scratch_shapes=[pltpu.VMEM((levels, 8, columns), f32)],
        compiler_params=params(16),
        cost_estimate=pl.CostEstimate(flops=1 << 25, bytes_accessed=18 << 20, transcendentals=0),
    )(flux, mask, moved)


def barotropic_kernel(fixed_ref, fixed_side_ref, flux_ref, flux_side_ref, height_ref, flow_ref, wide_ref):
    rows = height_ref.shape[0]
    columns = height_ref.shape[1]
    wide_ref[0:5, :, :columns] = fixed_ref[...]
    wide_ref[0:5, :, columns:] = fixed_side_ref[...]
    wide_ref[5:9, :, :columns] = flux_ref[...]
    wide_ref[5:9, :, columns:] = flux_side_ref[...]
    mask = wide_ref[0]
    drag = -0.5 * wide_ref[1]
    height = wide_ref[2]
    along = wide_ref[3]
    across = wide_ref[4]
    wind_x = 0.5 * wide_ref[5]
    wind_y = 0.5 * wide_ref[6]
    push = 0.5 * wide_ref[7]
    source = wide_ref[8]
    for k in range(SUB):
        level = mask * (height + push)
        along = mask * (0.95 * along + drag * (beside(level, -1, 1) - beside(level, 1, 1)) + wind_x)
        across = mask * (0.95 * across + drag * (beside(level, -1, 0) - beside(level, 1, 0)) + wind_y)
        spread_out = beside(along, -1, 1) - beside(along, 1, 1) + beside(across, -1, 0) - beside(across, 1, 0)
        height = mask * (height - 0.5 * spread_out + source)
    middle = slice(EDGE, EDGE + rows)
    height_ref[...] = height[middle, :columns]
    flow_ref[0] = along[middle, :columns]
    flow_ref[1] = across[middle, :columns]


def barotropic(fixed, fixed_side, flux, flux_side):
    _, tall, columns = fixed.shape
    rows = tall - 2 * EDGE
    return pl.pallas_call(
        barotropic_kernel,
        name="barotropic",
        in_specs=[VM] * 4,
        out_specs=[VM, VM],
        out_shape=[
            jax.ShapeDtypeStruct((rows, columns), f32),
            jax.ShapeDtypeStruct((2, rows, columns), f32),
        ],
        scratch_shapes=[pltpu.VMEM((9, tall, columns + LANES), f32)],
        compiler_params=params(24),
        cost_estimate=pl.CostEstimate(flops=1 << 24, bytes_accessed=6 << 20, transcendentals=0),
    )(fixed, fixed_side, flux, flux_side)


def to_next(array, axes):
    ends = lax.axis_size(axes) - 1
    return lax.ppermute(array, axes, [(i, i + 1) for i in range(ends)])


def to_previous(array, axes):
    ends = lax.axis_size(axes) - 1
    return lax.ppermute(array, axes, [(i + 1, i) for i in range(ends)])


def merge_sides(from_west, from_east):
    lane = lax.broadcasted_iota(i32, from_west.shape, from_west.ndim - 1)
    return jnp.where(lane < LANES // 2, from_east, from_west)


def all_to_all(array):
    return lax.all_to_all(array, EVERY, split_axis=0, concat_axis=0, tiled=True)


def local(
    atm_flux,
    margin_source,
    margin_cell,
    margin_weight,
    margin_tile,
    land_mask,
    sea_depth,
    sea_height,
    transport,
    tracers,
):
    tiles = lax.axis_size(EVERY)
    count, levels, rows, columns = tracers.shape
    first, second = pack(margin_tile.reshape(-1), atm_flux, margin_source, margin_cell, margin_weight, tiles)
    first = all_to_all(first)
    second = all_to_all(second)

    mask = land_mask.astype(f32)
    planes = tracers.reshape(count * levels, rows, columns)
    tracer_south, tracer_north, tracer_sides = edges(planes)
    fixed = jnp.concatenate([jnp.stack([mask, sea_depth, sea_height]), transport], axis=0)
    tops = fixed[:, rows - EDGE :].reshape(5 * EDGE, columns)
    bottoms = fixed[:, :EDGE].reshape(5 * EDGE, columns)
    from_south = to_next(jnp.concatenate([tracer_north, tops], axis=0), ROWS)
    from_north = to_previous(jnp.concatenate([tracer_south, bottoms], axis=0), ROWS)
    wide = count * levels
    fixed = jnp.concatenate(
        [
            from_south[wide:].reshape(5, EDGE, columns),
            fixed,
            from_north[wide:].reshape(5, EDGE, columns),
        ],
        axis=1,
    )
    tall = rows + 2 * EDGE
    east_edge = jnp.concatenate([fixed[:, :, -LANES:].reshape(5 * tall, LANES), tracer_sides[1]], axis=0)
    west_edge = jnp.concatenate([fixed[:, :, :LANES].reshape(5 * tall, LANES), tracer_sides[0]], axis=0)
    from_west = to_next(east_edge, "tx")
    from_east = to_previous(west_edge, "tx")
    fixed_side = merge_sides(from_west[: 5 * tall], from_east[: 5 * tall]).reshape(5, tall, LANES)
    sides = jnp.stack([from_east[5 * tall :], from_west[5 * tall :]])
    moved = move(from_south[:wide], from_north[:wide], sides, fixed, fixed_side, planes)

    winds = spread(first, first, rows, columns, "spread_first")
    flux_south = to_next(winds[:, rows - EDGE :], ROWS)
    flux_north = to_previous(winds[:, :EDGE], ROWS)
    winds = jnp.concatenate([flux_south, winds, flux_north], axis=1)
    flux_west = to_next(winds[:, :, -LANES:], "tx")
    flux_east = to_previous(winds[:, :, :LANES], "tx")
    winds_side = merge_sides(flux_west, flux_east)

    heats = spread(first, second, rows, columns, "spread_second")
    solved = solve(heats, mask, moved.reshape(tracers.shape))
    new_height, new_transport = barotropic(fixed, fixed_side, winds, winds_side)
    return new_height, new_transport, solved


def solution(mesh):
    in_specs = (
        P(None, EVERY),
        P(EVERY, None),
        P(EVERY, None),
        P(EVERY, None),
        P(EVERY, None),
        P(ROWS, "tx"),
        P(ROWS, "tx"),
        P(ROWS, "tx"),
        P(None, ROWS, "tx"),
        P(None, None, ROWS, "tx"),
    )
    out_specs = (P(ROWS, "tx"), P(None, ROWS, "tx"), P(None, None, ROWS, "tx"))
    return jax.shard_map(local, mesh=mesh, in_specs=in_specs, out_specs=out_specs, check_vma=False)
```

time: 350 us -> 141 us (0.40)
  the two profiles are of different devices: /device:TPU:98 before, /device:TPU:15 now
where the time goes in v1:
time: 141 us; the launch traced here: 139 us
  Pallas kernels  51.9 us (37%)
  starting transfers between devices  46 us (33%)
  local copies, waits for them, and re-layouts  23.3 us (17%)
  waiting for transfers between devices  12.8 us (9%)
  other arithmetic  4.1 us (3%)
    pallas_call x2, Pallas kernels, spread(): pl.pallas_call(functools.partial(spread_kernel, group=group), name=name,...  28.8 us
    all_to_all x2, starting transfers between devices, all_to_all(): return lax.all_to_all(array, EVERY, split_axis=0, concat_axis=0, tiled=True)  20.6 us
    unnamed x38, local copies, waits for them, and re-layouts  16.8 us
    ppermute x4, starting transfers between devices, to_previous(): return lax.ppermute(array, axes, [(i + 1, i) for i in range(ends)])  15.7 us
    ppermute x4, starting transfers between devices, to_next(): return lax.ppermute(array, axes, [(i, i + 1) for i in range(ends)])  9.7 us
    all_to_all x2, waiting for transfers between devices, all_to_all(): return lax.all_to_all(array, EVERY, split_axis=0, concat_axis=0, tiled=True)  8.34 us
    pallas_call x1, Pallas kernels, move(): pl.pallas_call(functools.partial(move_kernel, per=per), name='tracer_move...  7.6 us
    pallas_call x1, Pallas kernels, solve(): pl.pallas_call(functools.partial(solve_kernel, absorb=absorb, decay=decay...  6.28 us
  transfers between devices with their start and end apart: 10, of which 3 were waited for; matrix products, arithmetic and copies ran while one was open for 6% of the time, Pallas kernels for 35%

profile of v1, /device:TPU:15, one launch (start us, length us, event | category | flops | bytes accessed | tf_op | source)
XLA Modules:
  0.0 139.1 jit_solution(11662069485446235529)
XLA Ops:
  0.6 0.0 copy-start
  0.6 3.4 %copy-done = f32[2,16,64,1024]{3,2,1,0:T(8,128)S(1)} copy-done((f32[2,16,64,1024]{3,2,1,0:T(8,128)S(1)}, f32[2,16,64,1024]{3,2,1,0:T(8,128)}, u32[]{:S(2)}) %copy-start) | copy-done | bytes 8388632
  4.0 0.9 tracer_edges.1
  4.9 0.1 copy-done.16
  5.0 0.0 copy-start.12
  5.0 0.1 copy-done.13
  5.1 0.1 copy-done.14
  5.2 0.1 copy-done.15
  5.3 0.7 pad_maximum_fusion.3
  6.0 5.4 %collective-permute-start.1 = (f32[72,1024]{1,0:T(8,128)}, f32[72,1024]{1,0:T(8,128)}, u32[]{:S(2)}, u32[]{:S(2)}) collective-permute-start(f32[72,1024]{1,0:T(8,128)} %pad_maximum_fusion.3), channel_id=1, source_target_pairs={{8,0},{16,8},{24,16},{32,24},{40,32},{48,40},{56,48},{64,56},{72,6... | collective-permute-start | bytes 884744 | tf_op jit(solution)/shard_map/ppermute | solution.py:402
  11.4 0.7 pad_maximum_fusion.2
  12.2 2.0 %collective-permute-start = (f32[72,1024]{1,0:T(8,128)}, f32[72,1024]{1,0:T(8,128)}, u32[]{:S(2)}, u32[]{:S(2)}) collective-permute-start(f32[72,1024]{1,0:T(8,128)} %pad_maximum_fusion.2), channel_id=1, source_target_pairs={{0,8},{8,16},{16,24},{24,32},{32,40},{40,48},{48,56},{56,64},{64,7... | collective-permute-start | bytes 884744 | tf_op jit(solution)/shard_map/ppermute | solution.py:397
  14.3 5.7 %pack_margin.1 = (f32[128,5,4,128]{3,2,1,0:T(4,128)}, f32[128,4,4,128]{3,2,1,0:T(4,128)S(1)}) custom-call(s32[256]{0:T(256)S(1)} %bitcast.34, f32[8,16384]{1,0:T(8,128)S(1)} %copy-done.8, s32[256,128]{1,0:T(8,128)S(1)} %copy-done.9, s32[256,128]{1,0:T(8,128)S(1)} %copy-done.10, f32[256,128]{1,0:T(8,128)S(1)} %copy-done.11), custom_call_target="tpu_custom_call" | custom-call | flops 4194304 | bytes 4194304 | tf_op jit(solution)/shard_map/pack_margin/pallas_call | solution.py:67
  20.0 1.0 copy-done.6
  20.9 11.5 %all-to-all-start = ((f32[128,5,4,128]{3,2,1,0:T(4,128)}), f32[128,5,4,128]{3,2,1,0:T(4,128)S(1)}, u32[]{:S(2)}, u32[]{:S(2)}) async-start(f32[128,5,4,128]{3,2,1,0:T(4,128)} %get-tuple-element.13), calls=%async_computation | async-start | bytes 2621440 | tf_op jit(solution)/shard_map/all_to_all | solution.py:411
  32.4 0.9 slice_bitcast_fusion
  33.4 0.9 slice_bitcast_fusion.1
  34.3 1.4 pad_maximum_fusion.fixed_ref
  35.8 1.3 collective-permute-start.3
  37.1 3.0 %collective-permute-start.2 = (f32[464,128]{1,0:T(8,128)S(1)}, f32[464,128]{1,0:T(8,128)S(1)}, u32[]{:S(2)}, u32[]{:S(2)}) collective-permute-start(f32[464,128]{1,0:T(8,128)S(1)} %pad_maximum_fusion.4), channel_id=1, source_target_pairs={{1,0},{2,1},{3,2},{4,3},{5,4},{6,5},{7,6},{9,8},{10,9},{11,10},{12... | collective-permute-start | bytes 712712 | tf_op jit(solution)/shard_map/ppermute | solution.py:402
  40.1 0.9 slice.83.north_ref
  41.1 1.6 %slice.82.south_ref = f32[32,1024]{1,0:T(8,128)} slice(f32[72,1024]{1,0:T(8,128)} %collective-permute-done), slice={[0:32], [0:1024]} | slice | bytes 262144 | tf_op jit(solution)/shard_map/slice | solution.py:456
  42.6 0.6 slice_bitcast_fusion.2
  43.2 0.7 copy-done.17
  44.0 8.3 %all-to-all-done.cells_ref.value_ref = f32[128,5,4,128]{3,2,1,0:T(4,128)S(1)} async-done(((f32[128,5,4,128]{3,2,1,0:T(4,128)}), f32[128,5,4,128]{3,2,1,0:T(4,128)S(1)}, u32[]{:S(2)}, u32[]{:S(2)}) %all-to-all-start) | async-done | bytes 1310752 | tf_op jit(solution)/shard_map/all_to_all | solution.py:411
  52.3 9.1 %all-to-all-start.1 = ((f32[128,4,4,128]{3,2,1,0:T(4,128)}), f32[128,4,4,128]{3,2,1,0:T(4,128)}, u32[]{:S(2)}, u32[]{:S(2)}) async-start(f32[128,4,4,128]{3,2,1,0:T(4,128)} %copy-done.6), calls=%async_computation.1 | async-start | bytes 2097152 | tf_op jit(solution)/shard_map/all_to_all | solution.py:411
  61.4 13.8 %spread_first.1 = f32[4,64,1024]{2,1,0:T(8,128)S(1)} custom-call(f32[128,5,4,128]{3,2,1,0:T(4,128)S(1)} %all-to-all-done.cells_ref.value_ref, f32[128,5,4,128]{3,2,1,0:T(4,128)S(1)} %all-to-all-done.cells_ref.value_ref), custom_call_target="tpu_custom_call" | custom-call | flops 1073741824 | bytes 4194304 | tf_op jit(solution)/shard_map/spread_first/pallas_call | solution.py:144
  75.3 5.1 %collective-permute-start.4 = (f32[4,8,1024]{2,1,0:T(8,128)S(1)}, f32[4,8,1024]{2,1,0:T(8,128)S(1)}, u32[]{:S(2)}, u32[]{:S(2)}) collective-permute-start(f32[4,8,1024]{2,1,0:T(8,128)S(1)} %get-tuple-element.23), channel_id=1, source_target_pairs={{0,8},{8,16},{16,24},{24,32},{32,40},{40,48},{48,56},{56,64},{64,7... | collective-permute-start | bytes 393224 | tf_op jit(solution)/shard_map/ppermute | solution.py:397
  80.4 2.6 %collective-permute-start.5 = (f32[4,8,1024]{2,1,0:T(8,128)S(1)}, f32[4,8,1024]{2,1,0:T(8,128)S(1)}, u32[]{:S(2)}, u32[]{:S(2)}) collective-permute-start(f32[4,8,1024]{2,1,0:T(8,128)S(1)} %get-tuple-element.24), channel_id=1, source_target_pairs={{8,0},{16,8},{24,16},{32,24},{40,32},{48,40},{56,48},{64,56},{72,6... | collective-permute-start | bytes 393224 | tf_op jit(solution)/shard_map/ppermute | solution.py:402
  83.0 0.8 slice_bitcast_fusion.3
  83.7 0.5 collective-permute-done.4
  84.2 3.9 %collective-permute-done.5 = f32[4,8,1024]{2,1,0:T(8,128)S(1)} collective-permute-done((f32[4,8,1024]{2,1,0:T(8,128)S(1)}, f32[4,8,1024]{2,1,0:T(8,128)S(1)}, u32[]{:S(2)}, u32[]{:S(2)}) %collective-permute-start.5) | collective-permute-done | bytes 131104 | tf_op jit(solution)/shard_map/ppermute | solution.py:402
  88.2 0.1 pad_maximum_fusion.1.flux_ref
  88.3 0.7 fusion.2
  89.0 1.3 collective-permute-start.7
  90.3 4.7 %collective-permute-start.6 = (f32[4,80,128]{2,1,0:T(8,128)}, f32[4,80,128]{2,1,0:T(8,128)}, u32[]{:S(2)}, u32[]{:S(2)}) collective-permute-start(f32[4,80,128]{2,1,0:T(8,128)} %get-tuple-element.20), channel_id=1, source_target_pairs={{1,0},{2,1},{3,2},{4,3},{5,4},{6,5},{7,6},{9,8},{10,9},{11,10},{12... | collective-permute-start | bytes 491528 | tf_op jit(solution)/shard_map/ppermute | solution.py:402
  95.0 0.0 copy-start.1
  95.0 3.4 %copy-done.1 = f32[2,16,64,1024]{3,2,1,0:T(8,128)S(1)} copy-done((f32[2,16,64,1024]{3,2,1,0:T(8,128)S(1)}, f32[2,16,64,1024]{3,2,1,0:T(8,128)}, u32[]{:S(2)}) %copy-start.1) | copy-done | bytes 8388632
  98.4 7.6 %tracer_move.1 = f32[32,64,1024]{2,1,0:T(8,128)S(1)} custom-call(f32[32,1024]{1,0:T(8,128)S(1)} %copy-done.7, f32[32,1024]{1,0:T(8,128)S(1)} %slice.83.north_ref, f32[2,64,128]{2,1,0:T(8,128)S(1)} %pad_maximum_fusion.9.sides_ref, f32[5,80,1024]{2,1,0:T(8,128)S(1)} %pad_maximum_fusion.fixed_ref, f32[5,80,128]{2,1,0:T(8,128)S(1)} %bitcast.32, ...), custom_call_target="tpu_custom_call" | custom-call | flops 33554432 | bytes 18874368 | tf_op jit(solution)/shard_map/tracer_move/pallas_call | solution.py:265
  106.0 0.0 copy-start.2
  106.0 3.4 %copy-done.2 = f32[32,64,1024]{2,1,0:T(8,128)} copy-done((f32[32,64,1024]{2,1,0:T(8,128)}, f32[32,64,1024]{2,1,0:T(8,128)S(1)}, u32[]{:S(2)}) %copy-start.2) | copy-done | bytes 8388632
  109.4 1.3 copy-done.5
  110.7 15.0 %spread_second.1.flux_ref = f32[4,64,1024]{2,1,0:T(8,128)S(1)} custom-call(f32[128,5,4,128]{3,2,1,0:T(4,128)S(1)} %copy-done.5, f32[128,4,4,128]{3,2,1,0:T(4,128)} %all-to-all-done.1.value_ref), custom_call_target="tpu_custom_call" | custom-call | flops 1073741824 | bytes 4194304 | tf_op jit(solution)/shard_map/spread_second/pallas_call | solution.py:144
  125.7 0.0 copy-start.3
  125.7 3.4 %copy-done.3 = f32[32,64,1024]{2,1,0:T(8,128)S(1)} copy-done((f32[32,64,1024]{2,1,0:T(8,128)S(1)}, f32[32,64,1024]{2,1,0:T(8,128)}, u32[]{:S(2)}) %copy-start.3) | copy-done | bytes 8388632
  129.1 6.3 %column_solve.1 = f32[2,16,64,1024]{3,2,1,0:T(8,128)} custom-call(f32[4,64,1024]{2,1,0:T(8,128)S(1)} %spread_second.1.flux_ref, f32[64,1024]{1,0:T(8,128)S(1)} %get-tuple-element.25.mask_ref, f32[2,16,64,1024]{3,2,1,0:T(8,128)S(1)} %bitcast.31), custom_call_target="tpu_custom_call" | custom-call | flops 33554432 | bytes 18874368 | tf_op jit(solution)/shard_map/column_solve/pallas_call | solution.py:332
  135.4 1.0 broadcast_select_fusion.flux_side_ref
  136.4 2.7 %barotropic.1 = (f32[64,1024]{1,0:T(8,128)}, f32[2,64,1024]{2,1,0:T(8,128)}) custom-call(f32[5,80,1024]{2,1,0:T(8,128)S(1)} %pad_maximum_fusion.fixed_ref, f32[5,80,128]{2,1,0:T(8,128)S(1)} %bitcast.33, f32[4,80,1024]{2,1,0:T(8,128)S(1)} %pad_maximum_fusion.1.flux_ref, f32[4,80,128]{2,1,0:T(8,128)S(1)} %broadcast_select_fusion.flux_side_ref), custom_call_target="tpu_custom_call" | custom-call | flops 16777216 | bytes 6291456 | tf_op jit(solution)/shard_map/barotropic/pallas_call | solution.py:380
  (39 shorter events, 0.3 us)
Async XLA Ops:
  0.6 3.4 %copy-start = (f32[2,16,64,1024]{3,2,1,0:T(8,128)S(1)}, f32[2,16,64,1024]{3,2,1,0:T(8,128)}, u32[]{:S(2)}) copy-start(f32[2,16,64,1024]{3,2,1,0:T(8,128)} %param.19) | copy-start | bytes 25165828
  4.0 0.9 copy-start.16
  4.0 1.1 copy-start.13
  4.0 1.2 copy-start.14
  4.0 1.3 copy-start.15
  5.0 9.2 %copy-start.8 = (f32[8,16384]{1,0:T(8,128)S(1)}, f32[8,16384]{1,0:T(8,128)}, u32[]{:S(2)}) copy-start(f32[8,16384]{1,0:T(8,128)} %flux_ref.1) | copy-start | bytes 1572868
  5.0 9.3 %copy-start.9 = (s32[256,128]{1,0:T(8,128)S(1)}, s32[256,128]{1,0:T(8,128)}, u32[]{:S(2)}) copy-start(s32[256,128]{1,0:T(8,128)} %source_ref.1) | copy-start | bytes 393220
  5.0 9.3 %copy-start.10 = (s32[256,128]{1,0:T(8,128)S(1)}, s32[256,128]{1,0:T(8,128)}, u32[]{:S(2)}) copy-start(s32[256,128]{1,0:T(8,128)} %cell_ref.1) | copy-start | bytes 393220
  5.0 9.3 %copy-start.11 = (f32[256,128]{1,0:T(8,128)S(1)}, f32[256,128]{1,0:T(8,128)}, u32[]{:S(2)}) copy-start(f32[256,128]{1,0:T(8,128)} %weight_ref.1) | copy-start | bytes 393220
  5.0 9.3 %copy-start.12 = (s32[256,1]{0,1:T(1,128)S(1)}, s32[256,1]{0,1:T(1,128)}, u32[]{:S(2)}) copy-start(s32[256,1]{0,1:T(1,128)} %param.14) | copy-start | bytes 3076
  6.0 26.4 %collective-permute-start.1 = (f32[72,1024]{1,0:T(8,128)}, f32[72,1024]{1,0:T(8,128)}, u32[]{:S(2)}, u32[]{:S(2)}) collective-permute-start(f32[72,1024]{1,0:T(8,128)} %pad_maximum_fusion.3), channel_id=1, source_target_pairs={{8,0},{16,8},{24,16},{32,24},{40,32},{48,40},{56,48},{64,56},{72,6... | collective-permute-start | bytes 884744 | tf_op jit(solution)/shard_map/ppermute | solution.py:402
  12.2 21.2 %collective-permute-start = (f32[72,1024]{1,0:T(8,128)}, f32[72,1024]{1,0:T(8,128)}, u32[]{:S(2)}, u32[]{:S(2)}) collective-permute-start(f32[72,1024]{1,0:T(8,128)} %pad_maximum_fusion.2), channel_id=1, source_target_pairs={{0,8},{8,16},{16,24},{24,32},{32,40},{40,48},{48,56},{56,64},{64,7... | collective-permute-start | bytes 884744 | tf_op jit(solution)/shard_map/ppermute | solution.py:397
  20.0 1.0 copy-start.6
  20.9 31.4 %all-to-all-start = ((f32[128,5,4,128]{3,2,1,0:T(4,128)}), f32[128,5,4,128]{3,2,1,0:T(4,128)S(1)}, u32[]{:S(2)}, u32[]{:S(2)}) async-start(f32[128,5,4,128]{3,2,1,0:T(4,128)} %get-tuple-element.13), calls=%async_computation | async-start | bytes 2621440 | tf_op jit(solution)/shard_map/all_to_all | solution.py:411
  35.8 6.9 %collective-permute-start.3 = (f32[464,128]{1,0:T(8,128)S(1)}, f32[464,128]{1,0:T(8,128)S(1)}, u32[]{:S(2)}, u32[]{:S(2)}) collective-permute-start(f32[464,128]{1,0:T(8,128)S(1)} %pad_maximum_fusion.5), channel_id=1, source_target_pairs={{0,1},{1,2},{2,3},{3,4},{4,5},{5,6},{6,7},{8,9},{9,10},{10,11},{11... | collective-permute-start | bytes 712712 | tf_op jit(solution)/shard_map/ppermute | solution.py:397
  37.1 6.2 %collective-permute-start.2 = (f32[464,128]{1,0:T(8,128)S(1)}, f32[464,128]{1,0:T(8,128)S(1)}, u32[]{:S(2)}, u32[]{:S(2)}) collective-permute-start(f32[464,128]{1,0:T(8,128)S(1)} %pad_maximum_fusion.4), channel_id=1, source_target_pairs={{1,0},{2,1},{3,2},{4,3},{5,4},{6,5},{7,6},{9,8},{10,9},{11,10},{12... | collective-permute-start | bytes 712712 | tf_op jit(solution)/shard_map/ppermute | solution.py:402
  43.2 0.7 copy-start.17
  52.3 22.9 %copy-start.4 = (f32[128,5,4,128]{3,2,1,0:T(4,128)}, f32[128,5,4,128]{3,2,1,0:T(4,128)S(1)}, u32[]{:S(2)}) copy-start(f32[128,5,4,128]{3,2,1,0:T(4,128)S(1)} %all-to-all-done.cells_ref.value_ref) | copy-start | bytes 3932164
  52.3 57.1 %all-to-all-start.1 = ((f32[128,4,4,128]{3,2,1,0:T(4,128)}), f32[128,4,4,128]{3,2,1,0:T(4,128)}, u32[]{:S(2)}, u32[]{:S(2)}) async-start(f32[128,4,4,128]{3,2,1,0:T(4,128)} %copy-done.6), calls=%async_computation.1 | async-start | bytes 2097152 | tf_op jit(solution)/shard_map/all_to_all | solution.py:411
  75.3 9.0 %collective-permute-start.4 = (f32[4,8,1024]{2,1,0:T(8,128)S(1)}, f32[4,8,1024]{2,1,0:T(8,128)S(1)}, u32[]{:S(2)}, u32[]{:S(2)}) collective-permute-start(f32[4,8,1024]{2,1,0:T(8,128)S(1)} %get-tuple-element.23), channel_id=1, source_target_pairs={{0,8},{8,16},{16,24},{24,32},{32,40},{40,48},{48,56},{56,64},{64,7... | collective-permute-start | bytes 393224 | tf_op jit(solution)/shard_map/ppermute | solution.py:397
  80.4 7.8 %collective-permute-start.5 = (f32[4,8,1024]{2,1,0:T(8,128)S(1)}, f32[4,8,1024]{2,1,0:T(8,128)S(1)}, u32[]{:S(2)}, u32[]{:S(2)}) collective-permute-start(f32[4,8,1024]{2,1,0:T(8,128)S(1)} %get-tuple-element.24), channel_id=1, source_target_pairs={{8,0},{16,8},{24,16},{32,24},{40,32},{48,40},{56,48},{64,56},{72,6... | collective-permute-start | bytes 393224 | tf_op jit(solution)/shard_map/ppermute | solution.py:402
  83.7 11.3 %copy-start.18 = (f32[1,64,128]{2,1,0:T(8,128)S(1)}, f32[1,64,128]{2,1,0:T(8,128)}, u32[]{:S(2)}) copy-start(f32[1,64,128]{2,1,0:T(8,128)} %slice_bitcast_fusion.2) | copy-start | bytes 98308
  83.7 11.3 %copy-start.7 = (f32[32,1024]{1,0:T(8,128)S(1)}, f32[32,1024]{1,0:T(8,128)}, u32[]{:S(2)}) copy-start(f32[32,1024]{1,0:T(8,128)} %slice.82.south_ref) | copy-start | bytes 393220
  89.0 46.4 %collective-permute-start.7 = (f32[4,80,128]{2,1,0:T(8,128)}, f32[4,80,128]{2,1,0:T(8,128)}, u32[]{:S(2)}, u32[]{:S(2)}) collective-permute-start(f32[4,80,128]{2,1,0:T(8,128)} %get-tuple-element.19), channel_id=1, source_target_pairs={{0,1},{1,2},{2,3},{3,4},{4,5},{5,6},{6,7},{8,9},{9,10},{10,11},{11... | collective-permute-start | bytes 491528 | tf_op jit(solution)/shard_map/ppermute | solution.py:397
  90.3 45.1 %collective-permute-start.6 = (f32[4,80,128]{2,1,0:T(8,128)}, f32[4,80,128]{2,1,0:T(8,128)}, u32[]{:S(2)}, u32[]{:S(2)}) collective-permute-start(f32[4,80,128]{2,1,0:T(8,128)} %get-tuple-element.20), channel_id=1, source_target_pairs={{1,0},{2,1},{3,2},{4,3},{5,4},{6,5},{7,6},{9,8},{10,9},{11,10},{12... | collective-permute-start | bytes 491528 | tf_op jit(solution)/shard_map/ppermute | solution.py:402
  95.0 3.4 %copy-start.1 = (f32[2,16,64,1024]{3,2,1,0:T(8,128)S(1)}, f32[2,16,64,1024]{3,2,1,0:T(8,128)}, u32[]{:S(2)}) copy-start(f32[2,16,64,1024]{3,2,1,0:T(8,128)} %param.19) | copy-start | bytes 25165828
  106.0 3.4 %copy-start.2 = (f32[32,64,1024]{2,1,0:T(8,128)}, f32[32,64,1024]{2,1,0:T(8,128)S(1)}, u32[]{:S(2)}) copy-start(f32[32,64,1024]{2,1,0:T(8,128)S(1)} %tracer_move.1) | copy-start | bytes 25165828
  109.4 1.3 copy-start.5
  125.7 3.4 %copy-start.3 = (f32[32,64,1024]{2,1,0:T(8,128)S(1)}, f32[32,64,1024]{2,1,0:T(8,128)}, u32[]{:S(2)}) copy-start(f32[32,64,1024]{2,1,0:T(8,128)} %copy-done.2) | copy-start | bytes 25165828

commit v2 on v1

--- a/solution.py
+++ b/solution.py
@@ -23,18 +23,22 @@
     return pltpu.CompilerParams(vmem_limit_bytes=mib << 20)
 
 
-def pack_kernel(tile_ref, flux_ref, source_ref, cell_ref, weight_ref, first_ref, second_ref, count_ref):
+def whole(array):
+    return pl.BlockSpec(array.shape, lambda i: (0,) * array.ndim)
+
+
+def pack_kernel(tile_ref, flux_ref, source_ref, cell_ref, weight_ref, out_ref, count_ref, *, beyond):
     blocks = source_ref.shape[0]
-    tiles = first_ref.shape[0]
+    tiles = out_ref.shape[0]
     group = 4
-    first_ref[...] = jnp.zeros_like(first_ref)
-    second_ref[...] = jnp.zeros_like(second_ref)
+    nowhere = jnp.full((4, LANES), beyond, f32)
 
     def clear(t, carry):
         count_ref[t] = 0
+        out_ref[t, 8] = nowhere
         return carry
 
-    lax.fori_loop(0, tiles, clear, 0)
+    lax.fori_loop(0, tiles, clear, 0, unroll=True)
     sub = lax.broadcasted_iota(i32, (8, LANES), 0)
 
     def step(i, carry):
@@ -55,102 +59,109 @@
                 index = jnp.broadcast_to(source_ref[pl.ds(b, 1), :], (8, LANES))
                 picked = jnp.take_along_axis(y, index, axis=1)
                 value = picked * jnp.broadcast_to(weight_ref[pl.ds(b, 1), :], (8, LANES))
-                first_ref[tile, slot] = value[0:4]
-                second_ref[tile, slot] = value[4:8]
-                first_ref[tile, 4, pl.ds(slot, 1), :] = cell_ref[pl.ds(b, 1), :].astype(f32)
+                out_ref[tile, slot] = value[0:4]
+                out_ref[tile, 4 + slot] = value[4:8]
+                out_ref[tile, 8, pl.ds(slot, 1), :] = cell_ref[pl.ds(b, 1), :].astype(f32)
         return carry
 
     lax.fori_loop(0, blocks // (2 * group), step, 0)
 
 
-def pack(tile, flux, source, cell, weight, tiles):
+def pack(tile, flux, source, cell, weight, tiles, beyond):
     return pl.pallas_call(
-        pack_kernel,
+        functools.partial(pack_kernel, beyond=beyond),
         name="pack_margin",
         in_specs=[SM, VM, VM, VM, VM],
-        out_specs=[VM, VM],
-        out_shape=[
-            jax.ShapeDtypeStruct((tiles, 5, 4, LANES), f32),
-            jax.ShapeDtypeStruct((tiles, 4, 4, LANES), f32),
-        ],
+        out_specs=VM,
+        out_shape=jax.ShapeDtypeStruct((tiles, 9, 4, LANES), f32),
         scratch_shapes=[pltpu.SMEM((tiles,), i32)],
         compiler_params=params(24),
         cost_estimate=pl.CostEstimate(flops=1 << 22, bytes_accessed=4 << 20, transcendentals=0),
     )(tile, flux, source, cell, weight)
 
 
-def spread_kernel(cells_ref, value_ref, out_ref, acc_ref, *, group):
-    sources = value_ref.shape[0]
-    rows = out_ref.shape[1]
-    columns = out_ref.shape[2]
+def spread_kernel(load_ref, winds_ref, heats_ref, south_ref, north_ref, acc_ref, *, group):
+    sources = load_ref.shape[0]
+    _, rows, columns = winds_ref.shape
+    fields = 8
     high = columns // LANES
-    depth = 4 * high
-    acc_ref[...] = jnp.zeros_like(acc_ref)
-    sub_high = lax.broadcasted_iota(i32, (high, LANES), 0)
-    sub_low = lax.broadcasted_iota(i32, (LANES, LANES), 0)
-    blank = jnp.zeros((LANES, LANES), jnp.bfloat16)
+    depth = fields * high
+    def clear(i, c):
+        acc_ref[pl.ds(pl.multiple_of(i * 256, 256), 256),:] = jnp.zeros((256, LANES), f32)
+        return c
+    lax.fori_loop(0, rows * depth // 256, clear, 0)
+    low_iota = lax.broadcasted_iota(i32, (LANES, LANES), 0).astype(f32).astype(jnp.bfloat16)
+    pattern = [
+        (2 * i + (lax.broadcasted_iota(i32, (16, LANES), 0) >> 3)).astype(f32).astype(jnp.bfloat16) for i in range(high // 2)
+    ]
+    zero16 = jnp.zeros((16, LANES), jnp.bfloat16)
+    one = jnp.ones((LANES, LANES), jnp.bfloat16)
+    zero = jnp.zeros((LANES, LANES), jnp.bfloat16)
 
     def step(i, carry):
         for g in range(group):
             s = i * group + g
-            cells = cells_ref[s, 4].astype(i32)
-            highs = (cells & (columns - 1)) >> 7
-            lows = cells & (LANES - 1)
-            for pair in range(2):
+            cells = load_ref[s, 8].astype(i32)
+            highs = ((cells & (columns - 1)) >> 7).astype(f32)
+            lows = (cells & (LANES - 1)).astype(f32)
+            for k in range(4):
+                value = jnp.concatenate([load_ref[s, k], load_ref[s, 4 + k]], axis=0)
+                coarse = value.astype(jnp.bfloat16).astype(f32)
+                fine = value - coarse
+                coarse = jnp.concatenate([coarse, coarse], axis=0).astype(jnp.bfloat16)
+                fine = jnp.concatenate([fine, fine], axis=0).astype(jnp.bfloat16)
+                hk = jnp.broadcast_to(highs[k : k + 1], (16, LANES)).astype(jnp.bfloat16)
+                lk = jnp.broadcast_to(lows[k : k + 1], (16, LANES)).astype(jnp.bfloat16)
+                lk = jnp.concatenate([lk] * (LANES // 16), axis=0)
                 left = []
                 right = []
-                for k in (2 * pair, 2 * pair + 1):
-                    value = value_ref[s, k]
-                    coarse = value.astype(jnp.bfloat16).astype(f32)
-                    fine = value - coarse
-                    hit = jnp.broadcast_to(highs[k : k + 1], (high, LANES)) == sub_high
-                    parts = [
-                        jnp.where(hit, jnp.broadcast_to(piece[f : f + 1], (high, LANES)), 0.0)
-                        for piece in (coarse, fine)
-                        for f in range(4)
-                    ]
-                    left.append(jnp.concatenate(parts, axis=0).astype(jnp.bfloat16))
-                    one = jnp.where(jnp.broadcast_to(lows[k : k + 1], (LANES, LANES)) == sub_low, 1.0, 0.0)
-                    right.append(one.astype(jnp.bfloat16))
-                lhs = jnp.concatenate(left, axis=1)
-                rhs = jnp.concatenate(
-                    [
-                        jnp.concatenate([right[0], blank], axis=1),
-                        jnp.concatenate([blank, right[1]], axis=1),
-                    ],
-                    axis=0,
-                )
+                for p in pattern:
+                    hit = hk == p
+                    left.append(jnp.where(hit, coarse, zero16))
+                    right.append(jnp.where(hit, fine, zero16))
+                lhs = jnp.concatenate([jnp.concatenate(left, axis=0), jnp.concatenate(right, axis=0)], axis=1)
+                onehot = jnp.where(lk == low_iota, one, zero)
+                rhs = jnp.concatenate([onehot, onehot], axis=1)
                 both = lax.dot_general(lhs, rhs, (((1,), (1,)), ((), ())), preferred_element_type=f32)
-                both = both[:depth] + both[depth:]
-                for n in range(2):
-                    k = 2 * pair + n
-                    row = cells[k, 0] // columns
-                    place = pl.ds(pl.multiple_of(row * depth, depth), depth)
-                    acc_ref[place, :] += both[:, n * LANES : (n + 1) * LANES]
+                row = cells[k, 0] >> (columns.bit_length() - 1)
+                place = pl.ds(pl.multiple_of(row * depth, depth), depth)
+                acc_ref[place, :] += both
         return carry
 
     lax.fori_loop(0, sources // group, step, 0)
-    for f in range(4):
+
+    def turn(i, carry):
+        r = pl.multiple_of(i * 8, 8)
+        block = acc_ref[pl.ds(pl.multiple_of(r * depth, 8 * depth), 8 * depth), :].reshape(8, depth, LANES)
         for h in range(high):
-            for r in range(0, rows, 8):
-                out_ref[f, r : r + 8, h * LANES : (h + 1) * LANES] = acc_ref[
-                    pl.ds(r * depth + f * high + h, 8, stride=depth), :
-                ]
-
-
-def spread(cells, values, rows, columns, name):
-    depth = 4 * columns // LANES
-    group = 8 if values.shape[0] % 8 == 0 else 1
+            piece = jnp.swapaxes(block[:, h * 8 : h * 8 + 8, :], 0, 1)
+            for f in range(fields):
+                ref = winds_ref if f < 4 else heats_ref
+                ref[f % 4, pl.ds(r, 8), h * LANES : (h + 1) * LANES] = piece[f]
+        return carry
+
+    lax.fori_loop(0, rows // 8, turn, 0)
+    south_ref[...] = winds_ref[:, 0:EDGE, :]
+    north_ref[...] = winds_ref[:, rows - EDGE : rows, :]
+
+def spread(load, rows, columns):
+    depth = 8 * columns // LANES
+    group = 8 if load.shape[0] % 8 == 0 else 1
     return pl.pallas_call(
         functools.partial(spread_kernel, group=group),
-        name=name,
-        in_specs=[VM, VM],
-        out_specs=VM,
-        out_shape=jax.ShapeDtypeStruct((4, rows, columns), f32),
-        scratch_shapes=[pltpu.VMEM((rows * depth, LANES), f32)],
+        name="spread_all",
+        in_specs=[VM],
+        out_specs=[VM] * 4,
+        out_shape=[
+            jax.ShapeDtypeStruct((4, rows, columns), f32),
+            jax.ShapeDtypeStruct((4, rows, columns), f32),
+            jax.ShapeDtypeStruct((4, EDGE, columns), f32),
+            jax.ShapeDtypeStruct((4, EDGE, columns), f32),
+        ],
+        scratch_shapes=[pltpu.VMEM(((rows + 1) * depth, LANES), f32)],
         compiler_params=params(24),
         cost_estimate=pl.CostEstimate(flops=1 << 30, bytes_accessed=4 << 20, transcendentals=0),
-    )(cells, values)
+    )(load)
 
 
 def edges_kernel(low_ref, high_ref, west_ref, east_ref, south_ref, north_ref, columns_ref):
@@ -192,7 +203,7 @@
             jax.ShapeDtypeStruct((levels, columns), f32),
             jax.ShapeDtypeStruct((2, rows, LANES), f32),
         ],
-        compiler_params=params(24),
+        compiler_params=params(56),
         cost_estimate=pl.CostEstimate(flops=1 << 20, bytes_accessed=4 << 20, transcendentals=0),
     )(planes, planes, planes, planes)
 
@@ -261,7 +272,6 @@
 def move(south, north, sides, fixed, side_fixed, planes):
     levels, rows, columns = planes.shape
     per = 4
-    whole = lambda a: pl.BlockSpec(a.shape, lambda i: (0,) * a.ndim)
     return pl.pallas_call(
         functools.partial(move_kernel, per=per),
         name="tracer_move",
@@ -277,7 +287,7 @@
         out_specs=pl.BlockSpec((per, rows, columns), lambda i: (i, 0, 0)),
         out_shape=jax.ShapeDtypeStruct(planes.shape, f32),
         scratch_shapes=[pltpu.VMEM((5, rows, columns), f32)],
-        compiler_params=params(32),
+        compiler_params=params(56),
         cost_estimate=pl.CostEstimate(flops=1 << 25, bytes_accessed=18 << 20, transcendentals=0),
     )(south, north, sides, fixed, side_fixed, planes)
 
@@ -324,35 +334,44 @@
         out_ref[1, k] = salt_last
 
 
-def solve(flux, mask, moved):
+def solve(flux, mask, moved, part, parts):
     count, levels, rows, columns = moved.shape
     depths = np.arange(levels, dtype=np.float64)
     absorb = tuple(float(a) for a in np.exp(-depths / 3.0) - np.exp(-(depths + 1.0) / 3.0))
     decay = tuple(float(a) for a in np.exp(-depths / 2.0))
+    steps = rows // 8 // parts
+    first = part * steps
     return pl.pallas_call(
         functools.partial(solve_kernel, absorb=absorb, decay=decay),
-        name="column_solve",
-        grid=(rows // 8,),
+        name=f"column_solve_{part}",
+        grid=(steps,),
         in_specs=[
-            pl.BlockSpec((4, 8, columns), lambda i: (0, i, 0)),
-            pl.BlockSpec((8, columns), lambda i: (i, 0)),
-            pl.BlockSpec((count, levels, 8, columns), lambda i: (0, 0, i, 0)),
-        ],
-        out_specs=pl.BlockSpec((count, levels, 8, columns), lambda i: (0, 0, i, 0)),
+            pl.BlockSpec((4, 8, columns), lambda i: (0, first + i, 0)),
+            pl.BlockSpec((8, columns), lambda i: (first + i, 0)),
+            pl.BlockSpec((count, levels, 8, columns), lambda i: (0, 0, first + i, 0)),
+        ],
+        out_specs=pl.BlockSpec((count, levels, 8, columns), lambda i: (0, 0, first + i, 0)),
         out_shape=jax.ShapeDtypeStruct(moved.shape, f32),
         scratch_shapes=[pltpu.VMEM((levels, 8, columns), f32)],
-        compiler_params=params(16),
-        cost_estimate=pl.CostEstimate(flops=1 << 25, bytes_accessed=18 << 20, transcendentals=0),
+        input_output_aliases={2: 0},
+        compiler_params=params(56),
+        cost_estimate=pl.CostEstimate(flops=1 << 24, bytes_accessed=(18 << 20) // parts, transcendentals=0),
     )(flux, mask, moved)
 
 
-def barotropic_kernel(fixed_ref, fixed_side_ref, flux_ref, flux_side_ref, height_ref, flow_ref, wide_ref):
+def barotropic_kernel(
+    fixed_ref, fixed_side_ref, flux_ref, south_ref, north_ref, west_ref, east_ref, height_ref, flow_ref, wide_ref
+):
     rows = height_ref.shape[0]
     columns = height_ref.shape[1]
     wide_ref[0:5, :, :columns] = fixed_ref[...]
     wide_ref[0:5, :, columns:] = fixed_side_ref[...]
-    wide_ref[5:9, :, :columns] = flux_ref[...]
-    wide_ref[5:9, :, columns:] = flux_side_ref[...]
+    middle = slice(EDGE, EDGE + rows)
+    wide_ref[5:9, :EDGE, :columns] = south_ref[...]
+    wide_ref[5:9, middle, :columns] = flux_ref[...]
+    wide_ref[5:9, EDGE + rows :, :columns] = north_ref[...]
+    lane = lax.broadcasted_iota(i32, west_ref.shape, 2)
+    wide_ref[5:9, :, columns:] = jnp.where(lane < LANES // 2, east_ref[...], west_ref[...])
     mask = wide_ref[0]
     drag = -0.5 * wide_ref[1]
     height = wide_ref[2]
@@ -368,20 +387,31 @@
         across = mask * (0.95 * across + drag * (beside(level, -1, 0) - beside(level, 1, 0)) + wind_y)
         spread_out = beside(along, -1, 1) - beside(along, 1, 1) + beside(across, -1, 0) - beside(across, 1, 0)
         height = mask * (height - 0.5 * spread_out + source)
-    middle = slice(EDGE, EDGE + rows)
     height_ref[...] = height[middle, :columns]
     flow_ref[0] = along[middle, :columns]
     flow_ref[1] = across[middle, :columns]
 
 
-def barotropic(fixed, fixed_side, flux, flux_side):
+def barotropic(fixed, fixed_side, flux, south, north, west, east):
     _, tall, columns = fixed.shape
     rows = tall - 2 * EDGE
     return pl.pallas_call(
         barotropic_kernel,
         name="barotropic",
-        in_specs=[VM] * 4,
-        out_specs=[VM, VM],
+        grid=(1,),
+        in_specs=[
+            whole(fixed),
+            whole(fixed_side),
+            pl.BlockSpec((4, rows, columns), lambda i: (0, 0, 0)),
+            whole(south),
+            whole(north),
+            whole(west),
+            whole(east),
+        ],
+        out_specs=[
+            pl.BlockSpec((rows, columns), lambda i: (0, 0)),
+            pl.BlockSpec((2, rows, columns), lambda i: (0, 0, 0)),
+        ],
         out_shape=[
             jax.ShapeDtypeStruct((rows, columns), f32),
             jax.ShapeDtypeStruct((2, rows, columns), f32),
@@ -389,7 +419,7 @@
         scratch_shapes=[pltpu.VMEM((9, tall, columns + LANES), f32)],
         compiler_params=params(24),
         cost_estimate=pl.CostEstimate(flops=1 << 24, bytes_accessed=6 << 20, transcendentals=0),
-    )(fixed, fixed_side, flux, flux_side)
+    )(fixed, fixed_side, flux, south, north, west, east)
 
 
 def to_next(array, axes):
@@ -425,9 +455,13 @@
 ):
     tiles = lax.axis_size(EVERY)
     count, levels, rows, columns = tracers.shape
-    first, second = pack(margin_tile.reshape(-1), atm_flux, margin_source, margin_cell, margin_weight, tiles)
-    first = all_to_all(first)
-    second = all_to_all(second)
+    packed = pack(
+        margin_tile.reshape(-1), atm_flux, margin_source, margin_cell, margin_weight, tiles, rows * columns
+    )
+    packed, land_mask, sea_depth, sea_height, transport, tracers = lax.optimization_barrier(
+        (packed, land_mask, sea_depth, sea_height, transport, tracers)
+    )
+    arrived = all_to_all(packed)
 
     mask = land_mask.astype(f32)
     planes = tracers.reshape(count * levels, rows, columns)
@@ -455,17 +489,25 @@
     sides = jnp.stack([from_east[5 * tall :], from_west[5 * tall :]])
     moved = move(from_south[:wide], from_north[:wide], sides, fixed, fixed_side, planes)
 
-    winds = spread(first, first, rows, columns, "spread_first")
-    flux_south = to_next(winds[:, rows - EDGE :], ROWS)
-    flux_north = to_previous(winds[:, :EDGE], ROWS)
-    winds = jnp.concatenate([flux_south, winds, flux_north], axis=1)
-    flux_west = to_next(winds[:, :, -LANES:], "tx")
-    flux_east = to_previous(winds[:, :, :LANES], "tx")
-    winds_side = merge_sides(flux_west, flux_east)
-
-    heats = spread(first, second, rows, columns, "spread_second")
-    solved = solve(heats, mask, moved.reshape(tracers.shape))
-    new_height, new_transport = barotropic(fixed, fixed_side, winds, winds_side)
+    arrived, moved = lax.optimization_barrier((arrived, moved))
+    winds, heats, flux_low, flux_high = spread(arrived, rows, columns)
+    flux_south = to_next(flux_high, ROWS)
+    flux_north = to_previous(flux_low, ROWS)
+    moved = solve(heats, mask, moved.reshape(tracers.shape), 0, 2)
+    flux_south, flux_north, moved = lax.optimization_barrier((flux_south, flux_north, moved))
+    east_edge = jnp.concatenate(
+        [flux_south[:, :, -LANES:], winds[:, :, -LANES:], flux_north[:, :, -LANES:]], axis=1
+    )
+    west_edge = jnp.concatenate(
+        [flux_south[:, :, :LANES], winds[:, :, :LANES], flux_north[:, :, :LANES]], axis=1
+    )
+    flux_west = to_next(east_edge, "tx")
+    flux_east = to_previous(west_edge, "tx")
+    solved = solve(heats, mask, moved, 1, 2)
+    flux_west, flux_east, solved = lax.optimization_barrier((flux_west, flux_east, solved))
+    new_height, new_transport = barotropic(
+        fixed, fixed_side, winds, flux_south, flux_north, flux_west, flux_east
+    )
     return new_height, new_transport, solved
 
 

time: 141 us -> 134 us (0.950)
  waiting for transfers between devices: 12.8 us -> 30.9 us
  local copies, waits for them, and re-layouts: 23.3 us -> 6.97 us
  starting transfers between devices: 46 us -> 38.7 us
  other arithmetic: 4.1 us -> 2.33 us
    ppermute x4, waiting for transfers between devices: 3.93 us -> 30.8 us  [to_previous(): return lax.ppermute(array, axes, [(i + 1, i) for i in range(ends)])]
    pallas_call x4 -> x3, Pallas kernels: 37.2 us -> 24 us  [the longest x1 16.1 us: spread(): pl.pallas_call(functools.partial(spread_kernel, group=group), name='sprea...]
    unnamed x38 -> x32, local copies, waits for them, and re-layouts: 16.8 us -> 5.56 us
    all_to_all x2 -> x1, starting transfers between devices: 20.6 us -> 11 us  [all_to_all(): return lax.all_to_all(array, EVERY, split_axis=0, concat_axis=0, tiled=True)]
    all_to_all x2 -> x1, waiting for transfers between devices: 8.34 us -> 0.01 us  [all_to_all(): return lax.all_to_all(array, EVERY, split_axis=0, concat_axis=0, tiled=True)]
    ppermute x4, starting transfers between devices: 15.7 us -> 21.2 us  [to_previous(): return lax.ppermute(array, axes, [(i + 1, i) for i in range(ends)])]
    pallas_call x1 -> x2, Pallas kernels: 6.28 us -> 11.2 us  [solve(): pl.pallas_call(functools.partial(solve_kernel, absorb=absorb, decay=decay...]
    pallas_call x1, Pallas kernels: 7.6 us -> 12.4 us  [move(): pl.pallas_call(functools.partial(move_kernel, per=per), name='tracer_move...]
  transfers between devices with their start and end apart: 10 -> 9, of which waited for: 3 -> 1; matrix products, arithmetic and copies ran while one was open for 6% -> 3% of each run, Pallas kernels for 35% -> 21%
where the time goes in v2:
time: 134 us; the launch traced here: 131 us
  Pallas kernels  51.2 us (38%)
  starting transfers between devices  38.7 us (29%)
  waiting for transfers between devices  30.9 us (23%)
  local copies, waits for them, and re-layouts  6.97 us (5%)
  other arithmetic  2.33 us (2%)
    ppermute x4, waiting for transfers between devices, to_previous(): return lax.ppermute(array, axes, [(i + 1, i) for i in range(ends)])  30.8 us
    ppermute x4, starting transfers between devices, to_previous(): return lax.ppermute(array, axes, [(i + 1, i) for i in range(ends)])  21.2 us
    pallas_call x1, Pallas kernels, spread(): pl.pallas_call(functools.partial(spread_kernel, group=group), name='sprea...  16.1 us
    pallas_call x1, Pallas kernels, move(): pl.pallas_call(functools.partial(move_kernel, per=per), name='tracer_move...  12.4 us
    pallas_call x2, Pallas kernels, solve(): pl.pallas_call(functools.partial(solve_kernel, absorb=absorb, decay=decay...  11.2 us
    all_to_all x1, starting transfers between devices, all_to_all(): return lax.all_to_all(array, EVERY, split_axis=0, concat_axis=0, tiled=True)  11 us
    ppermute x4, starting transfers between devices, to_next(): return lax.ppermute(array, axes, [(i, i + 1) for i in range(ends)])  6.48 us
    unnamed x32, local copies, waits for them, and re-layouts  5.56 us
  transfers between devices with their start and end apart: 9, of which 1 were waited for; matrix products, arithmetic and copies ran while one was open for 3% of the time, Pallas kernels for 21%

profile of v2, /device:TPU:15, one launch (start us, length us, event | category | flops | bytes accessed | tf_op | source)
XLA Modules:
  0.0 131.0 jit_solution(5921420740763624463)
XLA Ops:
  0.6 0.0 copy-start.4
  0.6 1.0 copy-done.4
  1.7 0.9 copy-done.5
  2.6 0.9 copy-done.6
  3.5 0.9 copy-done.7
  4.4 0.7 copy-done.8
  5.1 5.0 %pack_margin.1 = f32[128,9,4,128]{3,2,1,0:T(4,128)} custom-call(s32[256]{0:T(256)S(1)} %bitcast.28, f32[8,16384]{1,0:T(8,128)S(1)} %copy-done.4, s32[256,128]{1,0:T(8,128)S(1)} %copy-done.5, s32[256,128]{1,0:T(8,128)S(1)} %copy-done.6, f32[256,128]{1,0:T(8,128)S(1)} %copy-done.7), custom_call_target="tpu_custom_call" | custom-call | flops 4194304 | bytes 4194304 | tf_op jit(solution)/shard_map/pack_margin/pallas_call | solution.py:71
  10.1 11.0 %all-to-all-start = ((f32[128,9,4,128]{3,2,1,0:T(4,128)}), f32[128,9,4,128]{3,2,1,0:T(4,128)}, u32[]{:S(2)}, u32[]{:S(2)}) async-start(f32[128,9,4,128]{3,2,1,0:T(4,128)} %pack_margin.1), calls=%async_computation | async-start | bytes 4718592 | tf_op jit(solution)/shard_map/all_to_all | solution.py:441
  21.2 0.0 copy-start.12
  21.2 0.0 copy-start.9
  21.2 0.0 copy-start.10
  21.2 0.0 copy-start.11
  21.2 3.7 %tracer_edges.1 = (f32[32,1024]{1,0:T(8,128)}, f32[32,1024]{1,0:T(8,128)}, f32[2,64,128]{2,1,0:T(8,128)}) custom-call(f32[32,64,1024]{2,1,0:T(8,128)} %bitcast.29, f32[32,64,1024]{2,1,0:T(8,128)} %bitcast.30, f32[32,64,1024]{2,1,0:T(8,128)} %bitcast.31, f32[32,64,1024]{2,1,0:T(8,128)} %bitcast.32), custom_call_target="tpu_custom_call" | custom-call | flops 1048576 | bytes 4194304 | tf_op jit(solution)/shard_map/tracer_edges/pallas_call | solution.py:186
  24.9 0.0 copy-done.12
  24.9 0.7 fusion.3
  25.7 0.1 copy-done.14
  25.8 5.0 %collective-permute-start.1 = (f32[72,1024]{1,0:T(8,128)S(1)}, f32[72,1024]{1,0:T(8,128)S(1)}, u32[]{:S(2)}, u32[]{:S(2)}) collective-permute-start(f32[72,1024]{1,0:T(8,128)S(1)} %pad_maximum_fusion.2), channel_id=1, source_target_pairs={{8,0},{16,8},{24,16},{32,24},{40,32},{48,40},{56,48},{64,56},{72,6... | collective-permute-start | bytes 884744 | tf_op jit(solution)/shard_map/ppermute | solution.py:432
  30.9 2.0 %collective-permute-start = (f32[72,1024]{1,0:T(8,128)S(1)}, f32[72,1024]{1,0:T(8,128)S(1)}, u32[]{:S(2)}, u32[]{:S(2)}) collective-permute-start(f32[72,1024]{1,0:T(8,128)S(1)} %pad_maximum_fusion.1), channel_id=1, source_target_pairs={{0,8},{8,16},{16,24},{24,32},{32,40},{40,48},{48,56},{56,64},{64,7... | collective-permute-start | bytes 884744 | tf_op jit(solution)/shard_map/ppermute | solution.py:427
  32.9 30.8 %collective-permute-done.1 = f32[72,1024]{1,0:T(8,128)S(1)} collective-permute-done((f32[72,1024]{1,0:T(8,128)S(1)}, f32[72,1024]{1,0:T(8,128)S(1)}, u32[]{:S(2)}, u32[]{:S(2)}) %collective-permute-start.1) | collective-permute-done | bytes 294944 | tf_op jit(solution)/shard_map/ppermute | solution.py:432
  63.8 0.0 collective-permute-done
  63.8 0.1 pad_maximum_fusion.fixed_ref
  63.9 0.0 copy-start
  64.0 1.3 collective-permute-start.3
  65.3 3.2 %collective-permute-start.2 = (f32[464,128]{1,0:T(8,128)S(1)}, f32[464,128]{1,0:T(8,128)S(1)}, u32[]{:S(2)}, u32[]{:S(2)}) collective-permute-start(f32[464,128]{1,0:T(8,128)S(1)} %pad_maximum_fusion.3), channel_id=1, source_target_pairs={{1,0},{2,1},{3,2},{4,3},{5,4},{6,5},{7,6},{9,8},{10,9},{11,10},{12... | collective-permute-start | bytes 712712 | tf_op jit(solution)/shard_map/ppermute | solution.py:432
  68.5 0.7 slice.87.north_ref
  69.2 0.7 slice.86.south_ref
  69.8 0.0 collective-permute-done.3
  69.9 0.0 collective-permute-done.2
  69.9 0.6 pad_maximum_fusion.10.sides_ref
  70.5 0.7 slice_select_fusion
  71.2 12.4 %tracer_move.1 = f32[32,64,1024]{2,1,0:T(8,128)} custom-call(f32[32,1024]{1,0:T(8,128)} %slice.86.south_ref, f32[32,1024]{1,0:T(8,128)} %slice.87.north_ref, f32[2,64,128]{2,1,0:T(8,128)} %pad_maximum_fusion.10.sides_ref, f32[5,80,1024]{2,1,0:T(8,128)} %copy-done, f32[5,80,128]{2,1,0:T(8,128)} %bitcast.26, f32[32,64,1024]{2,1,0:T(8,128)} %bitcast.33), custom_call_target="tpu_custom_call" | custom-call | flops 33554432 | bytes 18874368 | tf_op jit(solution)/shard_map/tracer_move/pallas_call | solution.py:275
  83.6 0.0 all-to-all-done.load_ref
  83.6 16.1 %spread_all.1 = (f32[4,64,1024]{2,1,0:T(8,128)S(1)}, f32[4,64,1024]{2,1,0:T(8,128)S(1)}, f32[4,8,1024]{2,1,0:T(8,128)S(1)}, f32[4,8,1024]{2,1,0:T(8,128)S(1)}) custom-call(f32[128,9,4,128]{3,2,1,0:T(4,128)} %all-to-all-done.load_ref), custom_call_target="tpu_custom_call" | custom-call | flops 1073741824 | bytes 4194304 | tf_op jit(solution)/shard_map/spread_all/pallas_call | solution.py:150
  99.7 1.0 copy-done.2
  100.7 1.9 %collective-permute-start.4 = (f32[4,8,1024]{2,1,0:T(8,128)S(1)}, f32[4,8,1024]{2,1,0:T(8,128)S(1)}, u32[]{:S(2)}, u32[]{:S(2)}) collective-permute-start(f32[4,8,1024]{2,1,0:T(8,128)S(1)} %get-tuple-element.37), channel_id=1, source_target_pairs={{0,8},{8,16},{16,24},{24,32},{32,40},{40,48},{48,56},{56,64},{64,7... | collective-permute-start | bytes 393224 | tf_op jit(solution)/shard_map/ppermute | solution.py:427
  102.6 5.8 %collective-permute-start.5 = (f32[4,8,1024]{2,1,0:T(8,128)S(1)}, f32[4,8,1024]{2,1,0:T(8,128)S(1)}, u32[]{:S(2)}, u32[]{:S(2)}) collective-permute-start(f32[4,8,1024]{2,1,0:T(8,128)S(1)} %get-tuple-element.38), channel_id=1, source_target_pairs={{8,0},{16,8},{24,16},{32,24},{40,32},{48,40},{56,48},{64,56},{72,6... | collective-permute-start | bytes 393224 | tf_op jit(solution)/shard_map/ppermute | solution.py:432
  108.4 5.6 %column_solve_0.1.moved_ref = f32[2,16,64,1024]{3,2,1,0:T(8,128)} custom-call(f32[4,64,1024]{2,1,0:T(8,128)} %copy-done.2, f32[64,1024]{1,0:T(8,128)} %get-tuple-element.55.mask_ref, f32[2,16,64,1024]{3,2,1,0:T(8,128)} %bitcast.34), custom_call_target="tpu_custom_call", output_to_operand_aliasing={{}: (2, {})} | custom-call | flops 16777216 | bytes 9437184 | tf_op jit(solution)/shard_map/column_solve_0/pallas_call | solution.py:344
  114.0 0.0 collective-permute-done.4.south_ref
  114.0 0.0 collective-permute-done.5.north_ref
  114.1 1.3 collective-permute-start.6
  115.4 0.0 copy-start.3
  115.4 7.2 %collective-permute-start.7 = (f32[4,80,128]{2,1,0:T(8,128)S(1)}, f32[4,80,128]{2,1,0:T(8,128)S(1)}, u32[]{:S(2)}, u32[]{:S(2)}) collective-permute-start(f32[4,80,128]{2,1,0:T(8,128)S(1)} %pad_maximum_fusion.9), channel_id=1, source_target_pairs={{1,0},{2,1},{3,2},{4,3},{5,4},{6,5},{7,6},{9,8},{10,9},{11,10},{12... | collective-permute-start | bytes 491528 | tf_op jit(solution)/shard_map/ppermute | solution.py:432
  122.6 5.6 %column_solve_1.1 = f32[2,16,64,1024]{3,2,1,0:T(8,128)} custom-call(f32[4,64,1024]{2,1,0:T(8,128)} %copy-done.2, f32[64,1024]{1,0:T(8,128)} %get-tuple-element.55.mask_ref, f32[2,16,64,1024]{3,2,1,0:T(8,128)} %column_solve_0.1.moved_ref), custom_call_target="tpu_custom_call", output_to_operand_aliasing={{}: (2, {})} | custom-call | flops 16777216 | bytes 9437184 | tf_op jit(solution)/shard_map/column_solve_1/pallas_call | solution.py:344
  128.2 0.0 collective-permute-done.6.west_ref
  128.2 0.0 collective-permute-done.7.east_ref
  128.2 0.0 copy-done.1
  128.2 0.0 copy-done.3
  128.2 2.8 %barotropic.1 = (f32[64,1024]{1,0:T(8,128)}, f32[2,64,1024]{2,1,0:T(8,128)}) custom-call(f32[5,80,1024]{2,1,0:T(8,128)S(1)} %copy-done.1, f32[5,80,128]{2,1,0:T(8,128)S(1)} %bitcast.27, f32[4,64,1024]{2,1,0:T(8,128)S(1)} %get-tuple-element.36.flux_ref, f32[4,8,1024]{2,1,0:T(8,128)S(1)} %collective-permute-done.4.south_ref, ...), custom_call_target="tpu_custom_call" | custom-call | flops 16777216 | bytes 6291456 | tf_op jit(solution)/shard_map/barotropic/pallas_call | solution.py:398
  (31 shorter events, 0.3 us)
Async XLA Ops:
  0.6 1.0 copy-start.4
  1.7 0.9 copy-start.5
  2.6 0.9 copy-start.6
  3.5 0.9 copy-start.7
  4.4 0.7 copy-start.8
  10.1 73.5 %all-to-all-start = ((f32[128,9,4,128]{3,2,1,0:T(4,128)}), f32[128,9,4,128]{3,2,1,0:T(4,128)}, u32[]{:S(2)}, u32[]{:S(2)}) async-start(f32[128,9,4,128]{3,2,1,0:T(4,128)} %pack_margin.1), calls=%async_computation | async-start | bytes 4718592 | tf_op jit(solution)/shard_map/all_to_all | solution.py:441
  21.2 3.8 %copy-start.12 = (s32[64,1024]{1,0:T(8,128)S(1)}, s32[64,1024]{1,0:T(8,128)}, u32[]{:S(2)}) copy-start(s32[64,1024]{1,0:T(8,128)} %param.15) | copy-start | bytes 786436
  21.2 4.5 %copy-start.9 = (f32[2,64,1024]{2,1,0:T(8,128)S(1)}, f32[2,64,1024]{2,1,0:T(8,128)}, u32[]{:S(2)}) copy-start(f32[2,64,1024]{2,1,0:T(8,128)} %param.18) | copy-start | bytes 1572868
  21.2 4.5 %copy-start.10 = (f32[64,1024]{1,0:T(8,128)S(1)}, f32[64,1024]{1,0:T(8,128)}, u32[]{:S(2)}) copy-start(f32[64,1024]{1,0:T(8,128)} %param.17) | copy-start | bytes 786436
  21.2 4.5 %copy-start.11 = (f32[64,1024]{1,0:T(8,128)S(1)}, f32[64,1024]{1,0:T(8,128)}, u32[]{:S(2)}) copy-start(f32[64,1024]{1,0:T(8,128)} %param.16) | copy-start | bytes 786436
  24.9 0.9 copy-start.14
  24.9 6.0 %copy-start.13 = (f32[32,1024]{1,0:T(8,128)S(1)}, f32[32,1024]{1,0:T(8,128)}, u32[]{:S(2)}) copy-start(f32[32,1024]{1,0:T(8,128)} %get-tuple-element.27) | copy-start | bytes 393220
  24.9 8.0 %copy-start.15 = (f32[2,64,128]{2,1,0:T(8,128)S(1)}, f32[2,64,128]{2,1,0:T(8,128)}, u32[]{:S(2)}) copy-start(f32[2,64,128]{2,1,0:T(8,128)} %get-tuple-element.33) | copy-start | bytes 196612
  25.8 37.9 %collective-permute-start.1 = (f32[72,1024]{1,0:T(8,128)S(1)}, f32[72,1024]{1,0:T(8,128)S(1)}, u32[]{:S(2)}, u32[]{:S(2)}) collective-permute-start(f32[72,1024]{1,0:T(8,128)S(1)} %pad_maximum_fusion.2), channel_id=1, source_target_pairs={{8,0},{16,8},{24,16},{32,24},{40,32},{48,40},{56,48},{64,56},{72,6... | collective-permute-start | bytes 884744 | tf_op jit(solution)/shard_map/ppermute | solution.py:432
  30.9 32.9 %collective-permute-start = (f32[72,1024]{1,0:T(8,128)S(1)}, f32[72,1024]{1,0:T(8,128)S(1)}, u32[]{:S(2)}, u32[]{:S(2)}) collective-permute-start(f32[72,1024]{1,0:T(8,128)S(1)} %pad_maximum_fusion.1), channel_id=1, source_target_pairs={{0,8},{8,16},{16,24},{24,32},{32,40},{40,48},{48,56},{56,64},{64,7... | collective-permute-start | bytes 884744 | tf_op jit(solution)/shard_map/ppermute | solution.py:427
  63.9 7.3 %copy-start = (f32[5,80,1024]{2,1,0:T(8,128)}, f32[5,80,1024]{2,1,0:T(8,128)S(1)}, u32[]{:S(2)}) copy-start(f32[5,80,1024]{2,1,0:T(8,128)S(1)} %pad_maximum_fusion.fixed_ref) | copy-start | bytes 4915204
  64.0 5.8 %collective-permute-start.3 = (f32[464,128]{1,0:T(8,128)S(1)}, f32[464,128]{1,0:T(8,128)S(1)}, u32[]{:S(2)}, u32[]{:S(2)}) collective-permute-start(f32[464,128]{1,0:T(8,128)S(1)} %pad_maximum_fusion.4), channel_id=1, source_target_pairs={{0,1},{1,2},{2,3},{3,4},{4,5},{5,6},{6,7},{8,9},{9,10},{10,11},{11... | collective-permute-start | bytes 712712 | tf_op jit(solution)/shard_map/ppermute | solution.py:427
  65.3 4.5 %collective-permute-start.2 = (f32[464,128]{1,0:T(8,128)S(1)}, f32[464,128]{1,0:T(8,128)S(1)}, u32[]{:S(2)}, u32[]{:S(2)}) collective-permute-start(f32[464,128]{1,0:T(8,128)S(1)} %pad_maximum_fusion.3), channel_id=1, source_target_pairs={{1,0},{2,1},{3,2},{4,3},{5,4},{6,5},{7,6},{9,8},{10,9},{11,10},{12... | collective-permute-start | bytes 712712 | tf_op jit(solution)/shard_map/ppermute | solution.py:432
  99.7 1.0 copy-start.2
  100.7 13.3 %collective-permute-start.4 = (f32[4,8,1024]{2,1,0:T(8,128)S(1)}, f32[4,8,1024]{2,1,0:T(8,128)S(1)}, u32[]{:S(2)}, u32[]{:S(2)}) collective-permute-start(f32[4,8,1024]{2,1,0:T(8,128)S(1)} %get-tuple-element.37), channel_id=1, source_target_pairs={{0,8},{8,16},{16,24},{24,32},{32,40},{40,48},{48,56},{56,64},{64,7... | collective-permute-start | bytes 393224 | tf_op jit(solution)/shard_map/ppermute | solution.py:427
  102.6 11.4 %collective-permute-start.5 = (f32[4,8,1024]{2,1,0:T(8,128)S(1)}, f32[4,8,1024]{2,1,0:T(8,128)S(1)}, u32[]{:S(2)}, u32[]{:S(2)}) collective-permute-start(f32[4,8,1024]{2,1,0:T(8,128)S(1)} %get-tuple-element.38), channel_id=1, source_target_pairs={{8,0},{16,8},{24,16},{32,24},{40,32},{48,40},{56,48},{64,56},{72,6... | collective-permute-start | bytes 393224 | tf_op jit(solution)/shard_map/ppermute | solution.py:432
  114.1 14.1 %collective-permute-start.6 = (f32[4,80,128]{2,1,0:T(8,128)S(1)}, f32[4,80,128]{2,1,0:T(8,128)S(1)}, u32[]{:S(2)}, u32[]{:S(2)}) collective-permute-start(f32[4,80,128]{2,1,0:T(8,128)S(1)} %pad_maximum_fusion.8), channel_id=1, source_target_pairs={{0,1},{1,2},{2,3},{3,4},{4,5},{5,6},{6,7},{8,9},{9,10},{10,11},{11... | collective-permute-start | bytes 491528 | tf_op jit(solution)/shard_map/ppermute | solution.py:427
  115.4 12.8 %copy-start.1 = (f32[5,80,1024]{2,1,0:T(8,128)S(1)}, f32[5,80,1024]{2,1,0:T(8,128)}, u32[]{:S(2)}) copy-start(f32[5,80,1024]{2,1,0:T(8,128)} %copy-done) | copy-start | bytes 4915204
  115.4 12.8 %copy-start.3 = (f32[400,128]{1,0:T(8,128)S(1)}, f32[400,128]{1,0:T(8,128)}, u32[]{:S(2)}) copy-start(f32[400,128]{1,0:T(8,128)} %slice_select_fusion) | copy-start | bytes 614404
  115.4 12.8 %collective-permute-start.7 = (f32[4,80,128]{2,1,0:T(8,128)S(1)}, f32[4,80,128]{2,1,0:T(8,128)S(1)}, u32[]{:S(2)}, u32[]{:S(2)}) collective-permute-start(f32[4,80,128]{2,1,0:T(8,128)S(1)} %pad_maximum_fusion.9), channel_id=1, source_target_pairs={{1,0},{2,1},{3,2},{4,3},{5,4},{6,5},{7,6},{9,8},{10,9},{11,10},{12... | collective-permute-start | bytes 491528 | tf_op jit(solution)/shard_map/ppermute | solution.py:432

commit v3 on v2

--- a/solution.py
+++ b/solution.py
@@ -27,15 +27,15 @@
     return pl.BlockSpec(array.shape, lambda i: (0,) * array.ndim)
 
 
-def pack_kernel(tile_ref, flux_ref, source_ref, cell_ref, weight_ref, out_ref, count_ref, *, beyond):
+def pack_kernel(tile_ref, flux_ref, source_ref, cell_ref, weight_ref, first_ref, second_ref, count_ref, *, beyond):
     blocks = source_ref.shape[0]
-    tiles = out_ref.shape[0]
+    tiles = first_ref.shape[0]
     group = 4
     nowhere = jnp.full((4, LANES), beyond, f32)
 
     def clear(t, carry):
         count_ref[t] = 0
-        out_ref[t, 8] = nowhere
+        first_ref[t, 4] = nowhere
         return carry
 
     lax.fori_loop(0, tiles, clear, 0, unroll=True)
@@ -59,9 +59,9 @@
                 index = jnp.broadcast_to(source_ref[pl.ds(b, 1), :], (8, LANES))
                 picked = jnp.take_along_axis(y, index, axis=1)
                 value = picked * jnp.broadcast_to(weight_ref[pl.ds(b, 1), :], (8, LANES))
-                out_ref[tile, slot] = value[0:4]
-                out_ref[tile, 4 + slot] = value[4:8]
-                out_ref[tile, 8, pl.ds(slot, 1), :] = cell_ref[pl.ds(b, 1), :].astype(f32)
+                first_ref[tile, slot] = value[0:4]
+                second_ref[tile, slot] = value[4:8]
+                first_ref[tile, 4, pl.ds(slot, 1), :] = cell_ref[pl.ds(b, 1), :].astype(f32)
         return carry
 
     lax.fori_loop(0, blocks // (2 * group), step, 0)
@@ -71,29 +71,36 @@
     return pl.pallas_call(
         functools.partial(pack_kernel, beyond=beyond),
         name="pack_margin",
-        in_specs=[SM, VM, VM, VM, VM],
-        out_specs=VM,
-        out_shape=jax.ShapeDtypeStruct((tiles, 9, 4, LANES), f32),
+        grid=(1,),
+        in_specs=[SM, whole(flux), whole(source), whole(cell), whole(weight)],
+        out_specs=[
+            pl.BlockSpec((tiles, 5, 4, LANES), lambda i: (0, 0, 0, 0)),
+            pl.BlockSpec((tiles, 4, 4, LANES), lambda i: (0, 0, 0, 0)),
+        ],
+        out_shape=[
+            jax.ShapeDtypeStruct((tiles, 5, 4, LANES), f32),
+            jax.ShapeDtypeStruct((tiles, 4, 4, LANES), f32),
+        ],
         scratch_shapes=[pltpu.SMEM((tiles,), i32)],
-        compiler_params=params(24),
+        compiler_params=params(56),
         cost_estimate=pl.CostEstimate(flops=1 << 22, bytes_accessed=4 << 20, transcendentals=0),
     )(tile, flux, source, cell, weight)
 
 
-def spread_kernel(load_ref, winds_ref, heats_ref, south_ref, north_ref, acc_ref, *, group):
-    sources = load_ref.shape[0]
-    _, rows, columns = winds_ref.shape
-    fields = 8
+def spread_kernel(cells_ref, value_ref, out_ref, acc_ref, *, group):
+    sources = value_ref.shape[0]
+    fields, rows, columns = out_ref.shape
     high = columns // LANES
     depth = fields * high
+
     def clear(i, c):
-        acc_ref[pl.ds(pl.multiple_of(i * 256, 256), 256),:] = jnp.zeros((256, LANES), f32)
+        acc_ref[pl.ds(pl.multiple_of(i * 256, 256), 256), :] = jnp.zeros((256, LANES), f32)
         return c
+
     lax.fori_loop(0, rows * depth // 256, clear, 0)
-    low_iota = lax.broadcasted_iota(i32, (LANES, LANES), 0).astype(f32).astype(jnp.bfloat16)
-    pattern = [
-        (2 * i + (lax.broadcasted_iota(i32, (16, LANES), 0) >> 3)).astype(f32).astype(jnp.bfloat16) for i in range(high // 2)
-    ]
+    lane = lax.broadcasted_iota(i32, (LANES, LANES), 0).astype(f32).astype(jnp.bfloat16)
+    sub = lax.broadcasted_iota(i32, (16, LANES), 0) >> 2
+    pattern = [(4 * i + sub).astype(f32).astype(jnp.bfloat16) for i in range(high // 4)]
     zero16 = jnp.zeros((16, LANES), jnp.bfloat16)
     one = jnp.ones((LANES, LANES), jnp.bfloat16)
     zero = jnp.zeros((LANES, LANES), jnp.bfloat16)
@@ -101,18 +108,16 @@
     def step(i, carry):
         for g in range(group):
             s = i * group + g
-            cells = load_ref[s, 8].astype(i32)
+            cells = cells_ref[s, 4].astype(i32)
             highs = ((cells & (columns - 1)) >> 7).astype(f32)
             lows = (cells & (LANES - 1)).astype(f32)
             for k in range(4):
-                value = jnp.concatenate([load_ref[s, k], load_ref[s, 4 + k]], axis=0)
+                value = value_ref[s, k]
                 coarse = value.astype(jnp.bfloat16).astype(f32)
                 fine = value - coarse
-                coarse = jnp.concatenate([coarse, coarse], axis=0).astype(jnp.bfloat16)
-                fine = jnp.concatenate([fine, fine], axis=0).astype(jnp.bfloat16)
+                coarse = jnp.concatenate([coarse] * 4, axis=0).astype(jnp.bfloat16)
+                fine = jnp.concatenate([fine] * 4, axis=0).astype(jnp.bfloat16)
                 hk = jnp.broadcast_to(highs[k : k + 1], (16, LANES)).astype(jnp.bfloat16)
-                lk = jnp.broadcast_to(lows[k : k + 1], (16, LANES)).astype(jnp.bfloat16)
-                lk = jnp.concatenate([lk] * (LANES // 16), axis=0)
                 left = []
                 right = []
                 for p in pattern:
@@ -120,7 +125,8 @@
                     left.append(jnp.where(hit, coarse, zero16))
                     right.append(jnp.where(hit, fine, zero16))
                 lhs = jnp.concatenate([jnp.concatenate(left, axis=0), jnp.concatenate(right, axis=0)], axis=1)
-                onehot = jnp.where(lk == low_iota, one, zero)
+                low = jnp.concatenate([jnp.broadcast_to(lows[k : k + 1], (16, LANES)).astype(jnp.bfloat16)] * (LANES // 16), axis=0)
+                onehot = jnp.where(low == lane, one, zero)
                 rhs = jnp.concatenate([onehot, onehot], axis=1)
                 both = lax.dot_general(lhs, rhs, (((1,), (1,)), ((), ())), preferred_element_type=f32)
                 row = cells[k, 0] >> (columns.bit_length() - 1)
@@ -133,35 +139,28 @@
     def turn(i, carry):
         r = pl.multiple_of(i * 8, 8)
         block = acc_ref[pl.ds(pl.multiple_of(r * depth, 8 * depth), 8 * depth), :].reshape(8, depth, LANES)
-        for h in range(high):
-            piece = jnp.swapaxes(block[:, h * 8 : h * 8 + 8, :], 0, 1)
-            for f in range(fields):
-                ref = winds_ref if f < 4 else heats_ref
-                ref[f % 4, pl.ds(r, 8), h * LANES : (h + 1) * LANES] = piece[f]
+        for n in range(depth // 8):
+            piece = jnp.swapaxes(block[:, n * 8 : n * 8 + 8, :], 0, 1)
+            for e in range(8):
+                h = 2 * n + e // 4
+                out_ref[e % 4, pl.ds(r, 8), h * LANES : (h + 1) * LANES] = piece[e]
         return carry
 
     lax.fori_loop(0, rows // 8, turn, 0)
-    south_ref[...] = winds_ref[:, 0:EDGE, :]
-    north_ref[...] = winds_ref[:, rows - EDGE : rows, :]
-
-def spread(load, rows, columns):
-    depth = 8 * columns // LANES
-    group = 8 if load.shape[0] % 8 == 0 else 1
+
+def spread(cells, load, rows, columns, name):
+    depth = 4 * columns // LANES
+    group = 8
     return pl.pallas_call(
         functools.partial(spread_kernel, group=group),
-        name="spread_all",
-        in_specs=[VM],
-        out_specs=[VM] * 4,
-        out_shape=[
-            jax.ShapeDtypeStruct((4, rows, columns), f32),
-            jax.ShapeDtypeStruct((4, rows, columns), f32),
-            jax.ShapeDtypeStruct((4, EDGE, columns), f32),
-            jax.ShapeDtypeStruct((4, EDGE, columns), f32),
-        ],
+        name=name,
+        in_specs=[VM, VM],
+        out_specs=VM,
+        out_shape=jax.ShapeDtypeStruct((4, rows, columns), f32),
         scratch_shapes=[pltpu.VMEM(((rows + 1) * depth, LANES), f32)],
         compiler_params=params(24),
         cost_estimate=pl.CostEstimate(flops=1 << 30, bytes_accessed=4 << 20, transcendentals=0),
-    )(load)
+    )(cells, load)
 
 
 def edges_kernel(low_ref, high_ref, west_ref, east_ref, south_ref, north_ref, columns_ref):
@@ -212,52 +211,41 @@
     return pltpu.roll(array, amount % array.shape[axis], axis)
 
 
-def move_kernel(south_ref, north_ref, sides_ref, fixed_ref, side_fixed_ref, planes_ref, out_ref, coef_ref, *, per):
+def drift(speed, toward):
+    return 0.1 + 0.15 * jnp.maximum(-toward * speed, 0.0)
+
+
+def move_kernel(mask_ref, depth_ref, flow_ref, planes_ref, out_ref, coef_ref, *, per):
     step = pl.program_id(0)
     rows = planes_ref.shape[1]
     columns = planes_ref.shape[2]
 
     @pl.when(step == 0)
     def _():
-        middle = slice(EDGE, EDGE + rows)
-        mask = fixed_ref[0, middle, :]
+        mask = mask_ref[...].astype(f32)
         lane = lax.broadcasted_iota(i32, (rows, columns), 1)
-        beyond = side_fixed_ref[0, middle, :]
-        east = jnp.where(lane == columns - 1, beyond[:, 0:1], beside(mask, -1, 1))
-        west = jnp.where(lane == 0, beyond[:, LANES - 1 : LANES], beside(mask, 1, 1))
-        tall = fixed_ref[0]
-        north = beside(tall, -1, 0)[middle]
-        south = beside(tall, 1, 0)[middle]
-        depth = fixed_ref[1, middle, :]
-        u = fixed_ref[3, middle, :] / depth
-        v = fixed_ref[4, middle, :] / depth
-        east = mask * east * (0.1 - 0.15 * jnp.minimum(u, 0.0))
-        west = mask * west * (0.1 + 0.15 * jnp.maximum(u, 0.0))
-        north = mask * north * (0.1 - 0.15 * jnp.minimum(v, 0.0))
-        south = mask * south * (0.1 + 0.15 * jnp.maximum(v, 0.0))
+        sub = lax.broadcasted_iota(i32, (rows, columns), 0)
+        u = flow_ref[0] / depth_ref[...]
+        v = flow_ref[1] / depth_ref[...]
+        east = mask * jnp.where(lane == columns - 1, 0.0, beside(mask, -1, 1)) * drift(u, 1.0)
+        west = mask * jnp.where(lane == 0, 0.0, beside(mask, 1, 1)) * drift(u, -1.0)
+        north = mask * jnp.where(sub == rows - 1, 0.0, beside(mask, -1, 0)) * drift(v, 1.0)
+        south = mask * jnp.where(sub == 0, 0.0, beside(mask, 1, 0)) * drift(v, -1.0)
         coef_ref[0] = 1.0 - (east + west + north + south)
         coef_ref[1] = east
         coef_ref[2] = west
         coef_ref[3] = north
         coef_ref[4] = south
 
-    lane_side = lax.broadcasted_iota(i32, (rows, LANES), 1)
     for n in range(per):
-        p = step * per + n
-        chosen = lane_side == p
-        first = jnp.sum(jnp.where(chosen, sides_ref[0], 0.0), axis=1, keepdims=True)
-        last = jnp.sum(jnp.where(chosen, sides_ref[1], 0.0), axis=1, keepdims=True)
-        south_row = south_ref[pl.ds(p, 1), :]
-        north_row = north_ref[pl.ds(p, 1), :]
         for r in range(0, rows, 8):
             span = slice(r, r + 8)
             q = planes_ref[n, span, :]
-            lane = lax.broadcasted_iota(i32, (8, columns), 1)
             sub = lax.broadcasted_iota(i32, (8, columns), 0)
-            east = jnp.where(lane == columns - 1, first[span], beside(q, -1, 1))
-            west = jnp.where(lane == 0, last[span], beside(q, 1, 1))
-            below = south_row if r == 0 else planes_ref[n, r - 1 : r, :]
-            above = north_row if r + 8 == rows else planes_ref[n, r + 8 : r + 9, :]
+            east = beside(q, -1, 1)
+            west = beside(q, 1, 1)
+            below = planes_ref[n, max(r - 1, 0) : max(r - 1, 0) + 1, :]
+            above = planes_ref[n, min(r + 8, rows - 1) : min(r + 8, rows - 1) + 1, :]
             north = jnp.where(sub == 7, above, beside(q, -1, 0))
             south = jnp.where(sub == 0, below, beside(q, 1, 0))
             out_ref[n, span, :] = (
@@ -269,7 +257,7 @@
             )
 
 
-def move(south, north, sides, fixed, side_fixed, planes):
+def move(mask, depth, flow, planes):
     levels, rows, columns = planes.shape
     per = 4
     return pl.pallas_call(
@@ -277,11 +265,9 @@
         name="tracer_move",
         grid=(levels // per,),
         in_specs=[
-            whole(south),
-            whole(north),
-            whole(sides),
-            whole(fixed),
-            whole(side_fixed),
+            whole(mask),
+            whole(depth),
+            whole(flow),
             pl.BlockSpec((per, rows, columns), lambda i: (i, 0, 0)),
         ],
         out_specs=pl.BlockSpec((per, rows, columns), lambda i: (i, 0, 0)),
@@ -289,7 +275,91 @@
         scratch_shapes=[pltpu.VMEM((5, rows, columns), f32)],
         compiler_params=params(56),
         cost_estimate=pl.CostEstimate(flops=1 << 25, bytes_accessed=18 << 20, transcendentals=0),
-    )(south, north, sides, fixed, side_fixed, planes)
+    )(mask, depth, flow, planes)
+
+
+def patch_rows_kernel(south_ref, north_ref, low_ref, high_ref, fixed_ref, moved_ref, out_ref):
+    step = pl.program_id(0)
+    levels = moved_ref.shape[0]
+    columns = moved_ref.shape[2]
+    upper = step == 1
+    row = jnp.where(upper, fixed_ref.shape[1] - EDGE - 1, EDGE)
+    other = jnp.where(upper, row + 1, row - 1)
+    toward = jnp.where(upper, 1.0, -1.0)
+    mask = fixed_ref[0, pl.ds(row, 1), :]
+    beyond = fixed_ref[0, pl.ds(other, 1), :]
+    v = fixed_ref[4, pl.ds(row, 1), :] / fixed_ref[1, pl.ds(row, 1), :]
+    coef = mask * beyond * drift(v, toward)
+    near = jnp.where(upper, north_ref[0:levels, :], south_ref[0:levels, :])
+    own = jnp.where(upper, high_ref[...], low_ref[...])
+    extra = coef * (near - own)
+    hit = lax.broadcasted_iota(i32, (EDGE, columns), 0) == jnp.where(upper, EDGE - 1, 0)
+    for p in range(levels):
+        out_ref[p] = moved_ref[p] + jnp.where(hit, extra[p : p + 1, :], 0.0)
+
+
+def patch_rows(south, north, low, high, fixed, moved):
+    levels, rows, columns = moved.shape
+    last = rows // EDGE - 1
+    block = pl.BlockSpec((levels, EDGE, columns), lambda i: (0, i * last, 0))
+    return pl.pallas_call(
+        patch_rows_kernel,
+        name="patch_rows",
+        grid=(2,),
+        in_specs=[whole(south), whole(north), whole(low), whole(high), whole(fixed), block],
+        out_specs=block,
+        out_shape=jax.ShapeDtypeStruct(moved.shape, f32),
+        input_output_aliases={5: 0},
+        compiler_params=params(56),
+        cost_estimate=pl.CostEstimate(flops=1 << 20, bytes_accessed=4 << 20, transcendentals=0),
+    )(south, north, low, high, fixed, moved)
+
+
+def patch_columns_kernel(near_ref, own_ref, side_ref, fixed_ref, moved_ref, out_ref):
+    step = pl.program_id(0)
+    levels, rows, _ = moved_ref.shape
+    upper = step == 1
+    edge = jnp.where(upper, LANES - 1, 0)
+    toward = jnp.where(upper, 1.0, -1.0)
+    lane = lax.broadcasted_iota(i32, (rows, LANES), 1)
+    hit = lane == edge
+    middle = slice(EDGE, EDGE + rows)
+
+    def column(value, chosen):
+        return jnp.sum(jnp.where(chosen, value, 0.0), axis=1, keepdims=True)
+
+    mask = column(fixed_ref[0, middle, :], hit)
+    depth = column(fixed_ref[1, middle, :], hit)
+    flow = column(fixed_ref[3, middle, :], hit)
+    beyond = column(side_ref[0, middle, :], lane == LANES - 1 - edge)
+    coef = mask * beyond * drift(flow / depth, toward)
+    extra = coef * (near_ref[0] - own_ref[0])
+    for p in range(levels):
+        out_ref[p] = moved_ref[p] + jnp.where(hit, extra[:, p : p + 1], 0.0)
+
+
+def patch_columns(near, own, side, fixed, moved):
+    levels, rows, columns = moved.shape
+    last = columns // LANES - 1
+    block = pl.BlockSpec((levels, rows, LANES), lambda i: (0, 0, i * last))
+    one = pl.BlockSpec((1, rows, LANES), lambda i: (i, 0, 0))
+    return pl.pallas_call(
+        patch_columns_kernel,
+        name="patch_columns",
+        grid=(2,),
+        in_specs=[
+            one,
+            one,
+            whole(side),
+            pl.BlockSpec((5, fixed.shape[1], LANES), lambda i: (0, 0, i * last)),
+            block,
+        ],
+        out_specs=block,
+        out_shape=jax.ShapeDtypeStruct(moved.shape, f32),
+        input_output_aliases={4: 0},
+        compiler_params=params(56),
+        cost_estimate=pl.CostEstimate(flops=1 << 20, bytes_accessed=4 << 20, transcendentals=0),
+    )(near, own, side, fixed, moved)
 
 
 def solve_kernel(flux_ref, mask_ref, moved_ref, out_ref, ratio_ref, *, absorb, decay):
@@ -334,28 +404,26 @@
         out_ref[1, k] = salt_last
 
 
-def solve(flux, mask, moved, part, parts):
+def solve(flux, mask, moved):
     count, levels, rows, columns = moved.shape
     depths = np.arange(levels, dtype=np.float64)
     absorb = tuple(float(a) for a in np.exp(-depths / 3.0) - np.exp(-(depths + 1.0) / 3.0))
     decay = tuple(float(a) for a in np.exp(-depths / 2.0))
-    steps = rows // 8 // parts
-    first = part * steps
     return pl.pallas_call(
         functools.partial(solve_kernel, absorb=absorb, decay=decay),
-        name=f"column_solve_{part}",
-        grid=(steps,),
+        name="column_solve",
+        grid=(rows // 8,),
         in_specs=[
-            pl.BlockSpec((4, 8, columns), lambda i: (0, first + i, 0)),
-            pl.BlockSpec((8, columns), lambda i: (first + i, 0)),
-            pl.BlockSpec((count, levels, 8, columns), lambda i: (0, 0, first + i, 0)),
-        ],
-        out_specs=pl.BlockSpec((count, levels, 8, columns), lambda i: (0, 0, first + i, 0)),
+            pl.BlockSpec((4, 8, columns), lambda i: (0, i, 0)),
+            pl.BlockSpec((8, columns), lambda i: (i, 0)),
+            pl.BlockSpec((count, levels, 8, columns), lambda i: (0, 0, i, 0)),
+        ],
+        out_specs=pl.BlockSpec((count, levels, 8, columns), lambda i: (0, 0, i, 0)),
         out_shape=jax.ShapeDtypeStruct(moved.shape, f32),
         scratch_shapes=[pltpu.VMEM((levels, 8, columns), f32)],
         input_output_aliases={2: 0},
         compiler_params=params(56),
-        cost_estimate=pl.CostEstimate(flops=1 << 24, bytes_accessed=(18 << 20) // parts, transcendentals=0),
+        cost_estimate=pl.CostEstimate(flops=1 << 25, bytes_accessed=18 << 20, transcendentals=0),
     )(flux, mask, moved)
 
 
@@ -455,23 +523,28 @@
 ):
     tiles = lax.axis_size(EVERY)
     count, levels, rows, columns = tracers.shape
-    packed = pack(
+    first, second = pack(
         margin_tile.reshape(-1), atm_flux, margin_source, margin_cell, margin_weight, tiles, rows * columns
     )
-    packed, land_mask, sea_depth, sea_height, transport, tracers = lax.optimization_barrier(
-        (packed, land_mask, sea_depth, sea_height, transport, tracers)
+    first, second, land_mask, sea_depth, sea_height, transport, tracers = lax.optimization_barrier(
+        (first, second, land_mask, sea_depth, sea_height, transport, tracers)
     )
-    arrived = all_to_all(packed)
-
+    arrived = all_to_all(first)
+
+    planes = tracers.reshape(count * levels, rows, columns)
+    wide = count * levels
+    low, high, own_sides = edges(planes)
     mask = land_mask.astype(f32)
-    planes = tracers.reshape(count * levels, rows, columns)
-    tracer_south, tracer_north, tracer_sides = edges(planes)
     fixed = jnp.concatenate([jnp.stack([mask, sea_depth, sea_height]), transport], axis=0)
     tops = fixed[:, rows - EDGE :].reshape(5 * EDGE, columns)
     bottoms = fixed[:, :EDGE].reshape(5 * EDGE, columns)
-    from_south = to_next(jnp.concatenate([tracer_north, tops], axis=0), ROWS)
-    from_north = to_previous(jnp.concatenate([tracer_south, bottoms], axis=0), ROWS)
-    wide = count * levels
+    from_south = to_next(jnp.concatenate([high, tops], axis=0), ROWS)
+    from_north = to_previous(jnp.concatenate([low, bottoms], axis=0), ROWS)
+    moved = move(land_mask, sea_depth, transport, planes)
+    arrived, second, moved = lax.optimization_barrier((arrived, second, moved))
+    arrived_second = all_to_all(second)
+
+    from_south, from_north, arrived = lax.optimization_barrier((from_south, from_north, arrived))
     fixed = jnp.concatenate(
         [
             from_south[wide:].reshape(5, EDGE, columns),
@@ -481,19 +554,18 @@
         axis=1,
     )
     tall = rows + 2 * EDGE
-    east_edge = jnp.concatenate([fixed[:, :, -LANES:].reshape(5 * tall, LANES), tracer_sides[1]], axis=0)
-    west_edge = jnp.concatenate([fixed[:, :, :LANES].reshape(5 * tall, LANES), tracer_sides[0]], axis=0)
+    east_edge = jnp.concatenate([fixed[:, :, -LANES:].reshape(5 * tall, LANES), own_sides[1]], axis=0)
+    west_edge = jnp.concatenate([fixed[:, :, :LANES].reshape(5 * tall, LANES), own_sides[0]], axis=0)
     from_west = to_next(east_edge, "tx")
     from_east = to_previous(west_edge, "tx")
+    moved = patch_rows(from_south, from_north, low, high, fixed, moved)
+    winds = spread(arrived, arrived, rows, columns, "spread_winds")
+    from_west, from_east, winds, moved = lax.optimization_barrier((from_west, from_east, winds, moved))
+    flux_south = to_next(winds[:, rows - EDGE :], ROWS)
+    flux_north = to_previous(winds[:, :EDGE], ROWS)
     fixed_side = merge_sides(from_west[: 5 * tall], from_east[: 5 * tall]).reshape(5, tall, LANES)
-    sides = jnp.stack([from_east[5 * tall :], from_west[5 * tall :]])
-    moved = move(from_south[:wide], from_north[:wide], sides, fixed, fixed_side, planes)
-
-    arrived, moved = lax.optimization_barrier((arrived, moved))
-    winds, heats, flux_low, flux_high = spread(arrived, rows, columns)
-    flux_south = to_next(flux_high, ROWS)
-    flux_north = to_previous(flux_low, ROWS)
-    moved = solve(heats, mask, moved.reshape(tracers.shape), 0, 2)
+    near_sides = jnp.stack([from_west[5 * tall :], from_east[5 * tall :]])
+    moved = patch_columns(near_sides, own_sides, fixed_side, fixed, moved)
     flux_south, flux_north, moved = lax.optimization_barrier((flux_south, flux_north, moved))
     east_edge = jnp.concatenate(
         [flux_south[:, :, -LANES:], winds[:, :, -LANES:], flux_north[:, :, -LANES:]], axis=1
@@ -503,8 +575,8 @@
     )
     flux_west = to_next(east_edge, "tx")
     flux_east = to_previous(west_edge, "tx")
-    solved = solve(heats, mask, moved, 1, 2)
-    flux_west, flux_east, solved = lax.optimization_barrier((flux_west, flux_east, solved))
+    heats = spread(arrived, arrived_second, rows, columns, "spread_heats")
+    solved = solve(heats, mask, moved.reshape(tracers.shape))
     new_height, new_transport = barotropic(
         fixed, fixed_side, winds, flux_south, flux_north, flux_west, flux_east
     )

time: 134 us -> 140 us (1.045)
  the two profiles are of different devices: /device:TPU:15 before, /device:TPU:33 now
where the time goes in v3:
time: 140 us; the launch traced here: 139 us
  Pallas kernels  70.6 us (50%)
  starting transfers between devices  44.3 us (32%)
  waiting for transfers between devices  14.6 us (10%)
  other arithmetic  4.49 us (3%)
  local copies, waits for them, and re-layouts  4.07 us (3%)
    pallas_call x2, Pallas kernels, spread(): pl.pallas_call(functools.partial(spread_kernel, group=group), name=name,...  29.6 us
    all_to_all x2, starting transfers between devices, all_to_all(): return lax.all_to_all(array, EVERY, split_axis=0, concat_axis=0, tiled=True)  17.4 us
    ppermute x4, starting transfers between devices, to_next(): return lax.ppermute(array, axes, [(i, i + 1) for i in range(ends)])  13.9 us
    ppermute x4, starting transfers between devices, to_previous(): return lax.ppermute(array, axes, [(i + 1, i) for i in range(ends)])  13 us
    pallas_call x1, Pallas kernels, move(): pl.pallas_call(functools.partial(move_kernel, per=per), name='tracer_move...  11.3 us
    pallas_call x1, Pallas kernels, solve(): pl.pallas_call(functools.partial(solve_kernel, absorb=absorb, decay=decay...  10.5 us
    ppermute x4, waiting for transfers between devices, to_previous(): return lax.ppermute(array, axes, [(i + 1, i) for i in range(ends)])  8.44 us
    ppermute x4, waiting for transfers between devices, to_next(): return lax.ppermute(array, axes, [(i, i + 1) for i in range(ends)])  6.18 us
  transfers between devices with their start and end apart: 10, of which 5 were waited for; matrix products, arithmetic and copies ran while one was open for 4% of the time, Pallas kernels for 28%

profile of v3, /device:TPU:33, one launch (start us, length us, event | category | flops | bytes accessed | tf_op | source)
XLA Modules:
  0.0 139.1 jit_solution(6116002403272850171)
XLA Ops:
  0.6 5.7 %pack_margin.1 = (f32[128,5,4,128]{3,2,1,0:T(4,128)}, f32[128,4,4,128]{3,2,1,0:T(4,128)}) custom-call(s32[256]{0:T(256)} %bitcast.40, f32[8,16384]{1,0:T(8,128)} %flux_ref.1, s32[256,128]{1,0:T(8,128)} %source_ref.1, s32[256,128]{1,0:T(8,128)} %cell_ref.1, f32[256,128]{1,0:T(8,128)} %weight_ref.1), custom_call_target="tpu_custom_call" | custom-call | flops 4194304 | bytes 4194304 | tf_op jit(solution)/shard_map/pack_margin/pallas_call | solution.py:71
  6.3 10.5 %all-to-all-start = ((f32[128,5,4,128]{3,2,1,0:T(4,128)}), f32[128,5,4,128]{3,2,1,0:T(4,128)S(1)}, u32[]{:S(2)}, u32[]{:S(2)}) async-start(f32[128,5,4,128]{3,2,1,0:T(4,128)} %get-tuple-element.39), calls=%async_computation | async-start | bytes 2621440 | tf_op jit(solution)/shard_map/all_to_all | solution.py:509
  16.8 0.0 copy-start.8
  16.8 0.0 copy-start.4
  16.9 0.0 copy-start.6
  16.9 0.0 copy-start.9
  16.9 3.7 %tracer_edges.1 = (f32[32,1024]{1,0:T(8,128)}, f32[32,1024]{1,0:T(8,128)}, f32[2,64,128]{2,1,0:T(8,128)}) custom-call(f32[32,64,1024]{2,1,0:T(8,128)} %bitcast.28, f32[32,64,1024]{2,1,0:T(8,128)} %bitcast.29, f32[32,64,1024]{2,1,0:T(8,128)} %bitcast.30, f32[32,64,1024]{2,1,0:T(8,128)} %bitcast.31), custom_call_target="tpu_custom_call" | custom-call | flops 1048576 | bytes 4194304 | tf_op jit(solution)/shard_map/tracer_edges/pallas_call | solution.py:185
  20.6 0.7 fusion.4
  21.4 0.1 copy-done.13
  21.5 4.2 %collective-permute-start = (f32[72,1024]{1,0:T(8,128)S(1)}, f32[72,1024]{1,0:T(8,128)S(1)}, u32[]{:S(2)}, u32[]{:S(2)}) collective-permute-start(f32[72,1024]{1,0:T(8,128)S(1)} %pad_maximum_fusion.1), channel_id=1, source_target_pairs={{0,8},{8,16},{16,24},{24,32},{32,40},{40,48},{48,56},{56,64},{64,7... | collective-permute-start | bytes 884744 | tf_op jit(solution)/shard_map/ppermute | solution.py:495
  25.8 0.0 copy-start.5
  25.8 3.5 %collective-permute-start.1 = (f32[72,1024]{1,0:T(8,128)S(1)}, f32[72,1024]{1,0:T(8,128)S(1)}, u32[]{:S(2)}, u32[]{:S(2)}) collective-permute-start(f32[72,1024]{1,0:T(8,128)S(1)} %pad_maximum_fusion.2), channel_id=1, source_target_pairs={{8,0},{16,8},{24,16},{32,24},{40,32},{48,40},{56,48},{64,56},{72,6... | collective-permute-start | bytes 884744 | tf_op jit(solution)/shard_map/ppermute | solution.py:500
  29.3 11.3 %tracer_move.1.moved_ref = f32[32,64,1024]{2,1,0:T(8,128)} custom-call(s32[64,1024]{1,0:T(8,128)} %mask_ref, f32[64,1024]{1,0:T(8,128)} %depth_ref, f32[2,64,1024]{2,1,0:T(8,128)} %flow_ref, f32[32,64,1024]{2,1,0:T(8,128)} %bitcast.32), custom_call_target="tpu_custom_call" | custom-call | flops 33554432 | bytes 18874368 | tf_op jit(solution)/shard_map/tracer_move/pallas_call | solution.py:263
  40.7 0.0 copy-done.7
  40.7 0.6 slice_bitcast_fusion.4
  41.3 0.0 all-to-all-done.cells_ref.value_ref
  41.3 3.7 %collective-permute-done.south_ref = f32[72,1024]{1,0:T(8,128)S(1)} collective-permute-done((f32[72,1024]{1,0:T(8,128)S(1)}, f32[72,1024]{1,0:T(8,128)S(1)}, u32[]{:S(2)}, u32[]{:S(2)}) %collective-permute-start) | collective-permute-done | bytes 294944 | tf_op jit(solution)/shard_map/ppermute | solution.py:495
  45.0 4.0 %collective-permute-done.1.north_ref = f32[72,1024]{1,0:T(8,128)S(1)} collective-permute-done((f32[72,1024]{1,0:T(8,128)S(1)}, f32[72,1024]{1,0:T(8,128)S(1)}, u32[]{:S(2)}, u32[]{:S(2)}) %collective-permute-start.1) | collective-permute-done | bytes 294944 | tf_op jit(solution)/shard_map/ppermute | solution.py:500
  49.1 0.7 copy-done.11
  49.8 1.3 pad_maximum_fusion.fixed_ref
  51.0 0.0 copy-start
  51.1 0.0 copy-done.16
  51.1 3.3 %collective-permute-start.2 = (f32[464,128]{1,0:T(8,128)S(1)}, f32[464,128]{1,0:T(8,128)}, u32[]{:S(2)}, u32[]{:S(2)}) collective-permute-start(f32[464,128]{1,0:T(8,128)S(1)} %pad_maximum_fusion.3), channel_id=1, source_target_pairs={{0,1},{1,2},{2,3},{3,4},{4,5},{5,6},{6,7},{8,9},{9,10},{10,11},{11... | collective-permute-start | bytes 712712 | tf_op jit(solution)/shard_map/ppermute | solution.py:495
  54.4 1.9 %collective-permute-start.3 = (f32[464,128]{1,0:T(8,128)S(1)}, f32[464,128]{1,0:T(8,128)}, u32[]{:S(2)}, u32[]{:S(2)}) collective-permute-start(f32[464,128]{1,0:T(8,128)S(1)} %pad_maximum_fusion.4), channel_id=1, source_target_pairs={{1,0},{2,1},{3,2},{4,3},{5,4},{6,5},{7,6},{9,8},{10,9},{11,10},{12... | collective-permute-start | bytes 712712 | tf_op jit(solution)/shard_map/ppermute | solution.py:500
  56.4 6.9 %all-to-all-start.1 = ((f32[128,4,4,128]{3,2,1,0:T(4,128)}), f32[128,4,4,128]{3,2,1,0:T(4,128)}, u32[]{:S(2)}, u32[]{:S(2)}) async-start(f32[128,4,4,128]{3,2,1,0:T(4,128)} %get-tuple-element.55), calls=%async_computation.1 | async-start | bytes 2097152 | tf_op jit(solution)/shard_map/all_to_all | solution.py:509
  63.3 3.5 %patch_rows.1.moved_ref = f32[32,64,1024]{2,1,0:T(8,128)} custom-call(f32[72,1024]{1,0:T(8,128)} %copy-done.10, f32[72,1024]{1,0:T(8,128)} %copy-done.11, f32[32,1024]{1,0:T(8,128)} %get-tuple-element.38.low_ref, f32[32,1024]{1,0:T(8,128)} %get-tuple-element.33.high_ref, f32[5,80,1024]{2,1,0:T(8,128)} %copy-done, ...), custom_call_target="tpu_custom_call", output_to_operand_aliasing={{}: (5, {})} | custom-call | flops 1048576 | bytes 4194304 | tf_op jit(solution)/shard_map/patch_rows/pallas_call | solution.py:305
  66.8 14.1 %spread_winds.1.flux_ref = f32[4,64,1024]{2,1,0:T(8,128)S(1)} custom-call(f32[128,5,4,128]{3,2,1,0:T(4,128)S(1)} %all-to-all-done.cells_ref.value_ref, f32[128,5,4,128]{3,2,1,0:T(4,128)S(1)} %all-to-all-done.cells_ref.value_ref), custom_call_target="tpu_custom_call" | custom-call | flops 1073741824 | bytes 4194304 | tf_op jit(solution)/shard_map/spread_winds/pallas_call | solution.py:154
  80.9 0.0 collective-permute-done.2
  80.9 0.0 collective-permute-done.3
  81.0 0.8 slice_bitcast_fusion.2
  81.7 0.8 slice_bitcast_fusion.3
  82.5 1.7 %slice_select_fusion = f32[400,128]{1,0:T(8,128)} fusion(f32[464,128]{1,0:T(8,128)} %collective-permute-done.2, f32[464,128]{1,0:T(8,128)} %collective-permute-done.3, pred[128]{0:T(512)(128)(4,1)S(1)} %iota_compare_fusion), kind=kLoop, calls=%fused_computation.5 | loop fusion | flops 51200 | bytes 614528 | tf_op jit(solution)/shard_map/jit(_where)/select_n | solution.py:505
  84.2 5.7 %collective-permute-start.5 = (f32[4,8,1024]{2,1,0:T(8,128)S(1)}, f32[4,8,1024]{2,1,0:T(8,128)S(1)}, u32[]{:S(2)}, u32[]{:S(2)}) collective-permute-start(f32[4,8,1024]{2,1,0:T(8,128)S(1)} %get-tuple-element.63), channel_id=1, source_target_pairs={{8,0},{16,8},{24,16},{32,24},{40,32},{48,40},{56,48},{64,56},{72,6... | collective-permute-start | bytes 393224 | tf_op jit(solution)/shard_map/ppermute | solution.py:500
  89.9 1.9 %collective-permute-start.4 = (f32[4,8,1024]{2,1,0:T(8,128)S(1)}, f32[4,8,1024]{2,1,0:T(8,128)S(1)}, u32[]{:S(2)}, u32[]{:S(2)}) collective-permute-start(f32[4,8,1024]{2,1,0:T(8,128)S(1)} %get-tuple-element.64), channel_id=1, source_target_pairs={{0,8},{8,16},{16,24},{24,32},{32,40},{40,48},{48,56},{56,64},{64,7... | collective-permute-start | bytes 393224 | tf_op jit(solution)/shard_map/ppermute | solution.py:495
  91.8 0.6 pad_maximum_fusion.10.near_ref
  92.5 3.6 %patch_columns.1 = f32[32,64,1024]{2,1,0:T(8,128)} custom-call(f32[2,64,128]{2,1,0:T(8,128)} %pad_maximum_fusion.10.near_ref, f32[2,64,128]{2,1,0:T(8,128)} %get-tuple-element.44.own_ref, f32[5,80,128]{2,1,0:T(8,128)} %bitcast.26, f32[5,80,1024]{2,1,0:T(8,128)} %copy-done, f32[32,64,1024]{2,1,0:T(8,128)} %patch_rows.1.moved_ref), custom_call_target="tpu_custom_call", output_to_operand_aliasing={{}: (4, {})} | custom-call | flops 1048576 | bytes 4194304 | tf_op jit(solution)/shard_map/patch_columns/pallas_call | solution.py:346
  96.2 0.0 collective-permute-done.5.north_ref
  96.2 2.1 %collective-permute-done.4.south_ref = f32[4,8,1024]{2,1,0:T(8,128)S(1)} collective-permute-done((f32[4,8,1024]{2,1,0:T(8,128)S(1)}, f32[4,8,1024]{2,1,0:T(8,128)S(1)}, u32[]{:S(2)}, u32[]{:S(2)}) %collective-permute-start.4) | collective-permute-done | bytes 131104 | tf_op jit(solution)/shard_map/ppermute | solution.py:495
  98.3 4.5 %collective-permute-start.6 = (f32[4,80,128]{2,1,0:T(8,128)S(1)}, f32[4,80,128]{2,1,0:T(8,128)S(1)}, u32[]{:S(2)}, u32[]{:S(2)}) collective-permute-start(f32[4,80,128]{2,1,0:T(8,128)S(1)} %pad_maximum_fusion.8), channel_id=1, source_target_pairs={{0,1},{1,2},{2,3},{3,4},{4,5},{5,6},{6,7},{8,9},{9,10},{10,11},{11... | collective-permute-start | bytes 491528 | tf_op jit(solution)/shard_map/ppermute | solution.py:495
  102.9 1.9 %collective-permute-start.7 = (f32[4,80,128]{2,1,0:T(8,128)S(1)}, f32[4,80,128]{2,1,0:T(8,128)S(1)}, u32[]{:S(2)}, u32[]{:S(2)}) collective-permute-start(f32[4,80,128]{2,1,0:T(8,128)S(1)} %pad_maximum_fusion.9), channel_id=1, source_target_pairs={{1,0},{2,1},{3,2},{4,3},{5,4},{6,5},{7,6},{9,8},{10,9},{11,10},{12... | collective-permute-start | bytes 491528 | tf_op jit(solution)/shard_map/ppermute | solution.py:500
  104.8 0.3 collective-permute-done.6.west_ref
  105.1 4.4 %collective-permute-done.7.east_ref = f32[4,80,128]{2,1,0:T(8,128)S(1)} collective-permute-done((f32[4,80,128]{2,1,0:T(8,128)S(1)}, f32[4,80,128]{2,1,0:T(8,128)S(1)}, u32[]{:S(2)}, u32[]{:S(2)}) %collective-permute-start.7) | collective-permute-done | bytes 163872 | tf_op jit(solution)/shard_map/ppermute | solution.py:500
  109.5 0.0 copy-done.1
  109.5 2.7 %barotropic.1 = (f32[64,1024]{1,0:T(8,128)}, f32[2,64,1024]{2,1,0:T(8,128)}) custom-call(f32[5,80,1024]{2,1,0:T(8,128)S(1)} %copy-done.1, f32[5,80,128]{2,1,0:T(8,128)S(1)} %bitcast.27, f32[4,64,1024]{2,1,0:T(8,128)S(1)} %spread_winds.1.flux_ref, f32[4,8,1024]{2,1,0:T(8,128)S(1)} %collective-permute-done.4.south_ref, ...), custom_call_target="tpu_custom_call" | custom-call | flops 16777216 | bytes 6291456 | tf_op jit(solution)/shard_map/barotropic/pallas_call | solution.py:466
  112.2 0.0 all-to-all-done.1.value_ref
  112.2 15.4 %spread_heats.1.flux_ref = f32[4,64,1024]{2,1,0:T(8,128)S(1)} custom-call(f32[128,5,4,128]{3,2,1,0:T(4,128)S(1)} %all-to-all-done.cells_ref.value_ref, f32[128,4,4,128]{3,2,1,0:T(4,128)} %all-to-all-done.1.value_ref), custom_call_target="tpu_custom_call" | custom-call | flops 1073741824 | bytes 4194304 | tf_op jit(solution)/shard_map/spread_heats/pallas_call | solution.py:154
  127.7 1.0 copy-done.3
  128.7 10.5 %column_solve.1 = f32[2,16,64,1024]{3,2,1,0:T(8,128)} custom-call(f32[4,64,1024]{2,1,0:T(8,128)} %copy-done.3, f32[64,1024]{1,0:T(8,128)} %get-tuple-element.65.mask_ref, f32[2,16,64,1024]{3,2,1,0:T(8,128)} %bitcast.33), custom_call_target="tpu_custom_call", output_to_operand_aliasing={{}: (2, {})} | custom-call | flops 33554432 | bytes 18874368 | tf_op jit(solution)/shard_map/column_solve/pallas_call | solution.py:412
  (36 shorter events, 0.3 us)
Async XLA Ops:
  6.3 35.0 %all-to-all-start = ((f32[128,5,4,128]{3,2,1,0:T(4,128)}), f32[128,5,4,128]{3,2,1,0:T(4,128)S(1)}, u32[]{:S(2)}, u32[]{:S(2)}) async-start(f32[128,5,4,128]{3,2,1,0:T(4,128)} %get-tuple-element.39), calls=%async_computation | async-start | bytes 2621440 | tf_op jit(solution)/shard_map/all_to_all | solution.py:509
  16.8 3.8 %copy-start.8 = (s32[64,1024]{1,0:T(8,128)S(1)}, s32[64,1024]{1,0:T(8,128)}, u32[]{:S(2)}) copy-start(s32[64,1024]{1,0:T(8,128)} %mask_ref) | copy-start | bytes 786436
  16.8 4.5 %copy-start.4 = (f32[2,64,1024]{2,1,0:T(8,128)S(1)}, f32[2,64,1024]{2,1,0:T(8,128)}, u32[]{:S(2)}) copy-start(f32[2,64,1024]{2,1,0:T(8,128)} %flow_ref) | copy-start | bytes 1572868
  16.9 4.5 %copy-start.6 = (f32[64,1024]{1,0:T(8,128)S(1)}, f32[64,1024]{1,0:T(8,128)}, u32[]{:S(2)}) copy-start(f32[64,1024]{1,0:T(8,128)} %depth_ref) | copy-start | bytes 786436
  16.9 4.5 %copy-start.9 = (f32[64,1024]{1,0:T(8,128)S(1)}, f32[64,1024]{1,0:T(8,128)}, u32[]{:S(2)}) copy-start(f32[64,1024]{1,0:T(8,128)} %param.17) | copy-start | bytes 786436
  20.6 0.9 copy-start.13
  20.6 5.2 %copy-start.12 = (f32[32,1024]{1,0:T(8,128)S(1)}, f32[32,1024]{1,0:T(8,128)}, u32[]{:S(2)}) copy-start(f32[32,1024]{1,0:T(8,128)} %get-tuple-element.38.low_ref) | copy-start | bytes 393220
  21.4 19.3 %copy-start.7 = (f32[1,64,1024]{2,1,0:T(8,128)}, f32[1,64,1024]{2,1,0:T(8,128)S(1)}, u32[]{:S(2)}) copy-start(f32[1,64,1024]{2,1,0:T(8,128)S(1)} %get-tuple-element.66) | copy-start | bytes 786436
  21.5 23.5 %collective-permute-start = (f32[72,1024]{1,0:T(8,128)S(1)}, f32[72,1024]{1,0:T(8,128)S(1)}, u32[]{:S(2)}, u32[]{:S(2)}) collective-permute-start(f32[72,1024]{1,0:T(8,128)S(1)} %pad_maximum_fusion.1), channel_id=1, source_target_pairs={{0,8},{8,16},{16,24},{24,32},{32,40},{40,48},{48,56},{56,64},{64,7... | collective-permute-start | bytes 884744 | tf_op jit(solution)/shard_map/ppermute | solution.py:495
  25.8 14.9 %copy-start.14 = (f32[2,64,128]{2,1,0:T(8,128)S(1)}, f32[2,64,128]{2,1,0:T(8,128)}, u32[]{:S(2)}) copy-start(f32[2,64,128]{2,1,0:T(8,128)} %get-tuple-element.44.own_ref) | copy-start | bytes 196612
  25.8 23.9 %copy-start.5 = (f32[2,64,1024]{2,1,0:T(8,128)S(1)}, f32[2,64,1024]{2,1,0:T(8,128)}, u32[]{:S(2)}) copy-start(f32[2,64,1024]{2,1,0:T(8,128)} %flow_ref) | copy-start | bytes 1572868
  25.8 23.2 %collective-permute-start.1 = (f32[72,1024]{1,0:T(8,128)S(1)}, f32[72,1024]{1,0:T(8,128)S(1)}, u32[]{:S(2)}, u32[]{:S(2)}) collective-permute-start(f32[72,1024]{1,0:T(8,128)S(1)} %pad_maximum_fusion.2), channel_id=1, source_target_pairs={{8,0},{16,8},{24,16},{32,24},{40,32},{48,40},{56,48},{64,56},{72,6... | collective-permute-start | bytes 884744 | tf_op jit(solution)/shard_map/ppermute | solution.py:500
  45.0 4.0 %copy-start.10 = (f32[72,1024]{1,0:T(8,128)}, f32[72,1024]{1,0:T(8,128)S(1)}, u32[]{:S(2)}) copy-start(f32[72,1024]{1,0:T(8,128)S(1)} %collective-permute-done.south_ref) | copy-start | bytes 884740
  49.0 0.7 copy-start.11
  49.8 1.3 copy-start.16
  49.8 4.6 %copy-start.15 = (f32[64,128]{1,0:T(8,128)S(1)}, f32[64,128]{1,0:T(8,128)}, u32[]{:S(2)}) copy-start(f32[64,128]{1,0:T(8,128)} %get-tuple-element.71) | copy-start | bytes 98308
  51.0 5.3 %copy-start = (f32[5,80,1024]{2,1,0:T(8,128)}, f32[5,80,1024]{2,1,0:T(8,128)S(1)}, u32[]{:S(2)}) copy-start(f32[5,80,1024]{2,1,0:T(8,128)S(1)} %pad_maximum_fusion.fixed_ref) | copy-start | bytes 4915204
  51.1 29.8 %collective-permute-start.2 = (f32[464,128]{1,0:T(8,128)S(1)}, f32[464,128]{1,0:T(8,128)}, u32[]{:S(2)}, u32[]{:S(2)}) collective-permute-start(f32[464,128]{1,0:T(8,128)S(1)} %pad_maximum_fusion.3), channel_id=1, source_target_pairs={{0,1},{1,2},{2,3},{3,4},{4,5},{5,6},{6,7},{8,9},{9,10},{10,11},{11... | collective-permute-start | bytes 712712 | tf_op jit(solution)/shard_map/ppermute | solution.py:495
  54.4 26.5 %collective-permute-start.3 = (f32[464,128]{1,0:T(8,128)S(1)}, f32[464,128]{1,0:T(8,128)}, u32[]{:S(2)}, u32[]{:S(2)}) collective-permute-start(f32[464,128]{1,0:T(8,128)S(1)} %pad_maximum_fusion.4), channel_id=1, source_target_pairs={{1,0},{2,1},{3,2},{4,3},{5,4},{6,5},{7,6},{9,8},{10,9},{11,10},{12... | collective-permute-start | bytes 712712 | tf_op jit(solution)/shard_map/ppermute | solution.py:500
  56.4 55.9 %all-to-all-start.1 = ((f32[128,4,4,128]{3,2,1,0:T(4,128)}), f32[128,4,4,128]{3,2,1,0:T(4,128)}, u32[]{:S(2)}, u32[]{:S(2)}) async-start(f32[128,4,4,128]{3,2,1,0:T(4,128)} %get-tuple-element.55), calls=%async_computation.1 | async-start | bytes 2097152 | tf_op jit(solution)/shard_map/all_to_all | solution.py:509
  84.2 11.9 %collective-permute-start.5 = (f32[4,8,1024]{2,1,0:T(8,128)S(1)}, f32[4,8,1024]{2,1,0:T(8,128)S(1)}, u32[]{:S(2)}, u32[]{:S(2)}) collective-permute-start(f32[4,8,1024]{2,1,0:T(8,128)S(1)} %get-tuple-element.63), channel_id=1, source_target_pairs={{8,0},{16,8},{24,16},{32,24},{40,32},{48,40},{56,48},{64,56},{72,6... | collective-permute-start | bytes 393224 | tf_op jit(solution)/shard_map/ppermute | solution.py:500
  89.9 8.4 %collective-permute-start.4 = (f32[4,8,1024]{2,1,0:T(8,128)S(1)}, f32[4,8,1024]{2,1,0:T(8,128)S(1)}, u32[]{:S(2)}, u32[]{:S(2)}) collective-permute-start(f32[4,8,1024]{2,1,0:T(8,128)S(1)} %get-tuple-element.64), channel_id=1, source_target_pairs={{0,8},{8,16},{16,24},{24,32},{32,40},{40,48},{48,56},{56,64},{64,7... | collective-permute-start | bytes 393224 | tf_op jit(solution)/shard_map/ppermute | solution.py:495
  92.5 17.0 %copy-start.1 = (f32[5,80,1024]{2,1,0:T(8,128)S(1)}, f32[5,80,1024]{2,1,0:T(8,128)}, u32[]{:S(2)}) copy-start(f32[5,80,1024]{2,1,0:T(8,128)} %copy-done) | copy-start | bytes 4915204
  92.5 17.0 %copy-start.2 = (f32[400,128]{1,0:T(8,128)S(1)}, f32[400,128]{1,0:T(8,128)}, u32[]{:S(2)}) copy-start(f32[400,128]{1,0:T(8,128)} %slice_select_fusion) | copy-start | bytes 614404
  98.3 6.8 %collective-permute-start.6 = (f32[4,80,128]{2,1,0:T(8,128)S(1)}, f32[4,80,128]{2,1,0:T(8,128)S(1)}, u32[]{:S(2)}, u32[]{:S(2)}) collective-permute-start(f32[4,80,128]{2,1,0:T(8,128)S(1)} %pad_maximum_fusion.8), channel_id=1, source_target_pairs={{0,1},{1,2},{2,3},{3,4},{4,5},{5,6},{6,7},{8,9},{9,10},{10,11},{11... | collective-permute-start | bytes 491528 | tf_op jit(solution)/shard_map/ppermute | solution.py:495
  102.9 6.6 %collective-permute-start.7 = (f32[4,80,128]{2,1,0:T(8,128)S(1)}, f32[4,80,128]{2,1,0:T(8,128)S(1)}, u32[]{:S(2)}, u32[]{:S(2)}) collective-permute-start(f32[4,80,128]{2,1,0:T(8,128)S(1)} %pad_maximum_fusion.9), channel_id=1, source_target_pairs={{1,0},{2,1},{3,2},{4,3},{5,4},{6,5},{7,6},{9,8},{10,9},{11,10},{12... | collective-permute-start | bytes 491528 | tf_op jit(solution)/shard_map/ppermute | solution.py:500
  127.7 1.0 copy-start.3

commit v4 on v2

--- a/solution.py
+++ b/solution.py
@@ -71,11 +71,12 @@
     return pl.pallas_call(
         functools.partial(pack_kernel, beyond=beyond),
         name="pack_margin",
-        in_specs=[SM, VM, VM, VM, VM],
-        out_specs=VM,
+        grid=(1,),
+        in_specs=[SM, whole(flux), whole(source), whole(cell), whole(weight)],
+        out_specs=pl.BlockSpec((tiles, 9, 4, LANES), lambda i: (0, 0, 0, 0)),
         out_shape=jax.ShapeDtypeStruct((tiles, 9, 4, LANES), f32),
         scratch_shapes=[pltpu.SMEM((tiles,), i32)],
-        compiler_params=params(24),
+        compiler_params=params(56),
         cost_estimate=pl.CostEstimate(flops=1 << 22, bytes_accessed=4 << 20, transcendentals=0),
     )(tile, flux, source, cell, weight)
 
@@ -164,100 +165,97 @@
     )(load)
 
 
-def edges_kernel(low_ref, high_ref, west_ref, east_ref, south_ref, north_ref, columns_ref):
+def edges_kernel(
+    low_ref, high_ref, left_ref, right_ref, mask_ref, depth_ref, height_ref, flow_ref, south_ref, north_ref, west_ref, east_ref
+):
     levels = low_ref.shape[0]
-    rows = west_ref.shape[1]
+    rows, columns = mask_ref.shape
     lane = lax.broadcasted_iota(i32, (rows, LANES), 1)
     lasts = jnp.zeros((rows, LANES), f32)
     firsts = jnp.zeros((rows, LANES), f32)
     for p in range(levels):
         south_ref[p : p + 1, :] = low_ref[p, 0:1, :]
         north_ref[p : p + 1, :] = high_ref[p, EDGE - 1 : EDGE, :]
-        firsts = jnp.where(lane == p, west_ref[p, :, 0:1], firsts)
-        lasts = jnp.where(lane == p, east_ref[p, :, LANES - 1 : LANES], lasts)
-    columns_ref[0] = firsts
-    columns_ref[1] = lasts
-
-
-def edges(planes):
+        firsts = jnp.where(lane == p, left_ref[p, :, 0:1], firsts)
+        lasts = jnp.where(lane == p, right_ref[p, :, LANES - 1 : LANES], lasts)
+    fields = [mask_ref, depth_ref, height_ref, flow_ref.at[0], flow_ref.at[1]]
+    for f, ref in enumerate(fields):
+        place = slice(levels + f * EDGE, levels + (f + 1) * EDGE)
+        south_ref[place, :] = ref[0:EDGE, :].astype(f32)
+        north_ref[place, :] = ref[rows - EDGE : rows, :].astype(f32)
+        place = slice(f * rows, (f + 1) * rows)
+        west_ref[place, :] = ref[:, 0:LANES].astype(f32)
+        east_ref[place, :] = ref[:, columns - LANES : columns].astype(f32)
+    west_ref[5 * rows : 6 * rows, :] = firsts
+    east_ref[5 * rows : 6 * rows, :] = lasts
+
+
+def edges(planes, mask, depth, height, flow):
     levels, rows, columns = planes.shape
     last_row = rows // EDGE - 1
     last_lane = columns // LANES - 1
+    tall = jax.ShapeDtypeStruct((levels + 5 * EDGE, columns), f32)
+    thin = jax.ShapeDtypeStruct((6 * rows, LANES), f32)
     return pl.pallas_call(
         edges_kernel,
-        name="tracer_edges",
+        name="tile_edges",
         grid=(1,),
         in_specs=[
             pl.BlockSpec((levels, EDGE, columns), lambda i: (0, 0, 0)),
             pl.BlockSpec((levels, EDGE, columns), lambda i: (0, last_row, 0)),
             pl.BlockSpec((levels, rows, LANES), lambda i: (0, 0, 0)),
             pl.BlockSpec((levels, rows, LANES), lambda i: (0, 0, last_lane)),
+            whole(mask),
+            whole(depth),
+            whole(height),
+            whole(flow),
         ],
-        out_specs=[
-            pl.BlockSpec((levels, columns), lambda i: (0, 0)),
-            pl.BlockSpec((levels, columns), lambda i: (0, 0)),
-            pl.BlockSpec((2, rows, LANES), lambda i: (0, 0, 0)),
-        ],
-        out_shape=[
-            jax.ShapeDtypeStruct((levels, columns), f32),
-            jax.ShapeDtypeStruct((levels, columns), f32),
-            jax.ShapeDtypeStruct((2, rows, LANES), f32),
-        ],
+        out_specs=[whole(tall), whole(tall), whole(thin), whole(thin)],
+        out_shape=[tall, tall, thin, thin],
         compiler_params=params(56),
-        cost_estimate=pl.CostEstimate(flops=1 << 20, bytes_accessed=4 << 20, transcendentals=0),
-    )(planes, planes, planes, planes)
+        cost_estimate=pl.CostEstimate(flops=1 << 20, bytes_accessed=6 << 20, transcendentals=0),
+    )(planes, planes, planes, planes, mask, depth, height, flow)
 
 
 def beside(array, amount, axis):
     return pltpu.roll(array, amount % array.shape[axis], axis)
 
 
-def move_kernel(south_ref, north_ref, sides_ref, fixed_ref, side_fixed_ref, planes_ref, out_ref, coef_ref, *, per):
+def drift(speed, toward):
+    return 0.1 + 0.15 * jnp.maximum(-toward * speed, 0.0)
+
+
+def move_kernel(mask_ref, depth_ref, flow_ref, planes_ref, out_ref, coef_ref, *, per):
     step = pl.program_id(0)
     rows = planes_ref.shape[1]
     columns = planes_ref.shape[2]
 
     @pl.when(step == 0)
     def _():
-        middle = slice(EDGE, EDGE + rows)
-        mask = fixed_ref[0, middle, :]
+        mask = mask_ref[...].astype(f32)
         lane = lax.broadcasted_iota(i32, (rows, columns), 1)
-        beyond = side_fixed_ref[0, middle, :]
-        east = jnp.where(lane == columns - 1, beyond[:, 0:1], beside(mask, -1, 1))
-        west = jnp.where(lane == 0, beyond[:, LANES - 1 : LANES], beside(mask, 1, 1))
-        tall = fixed_ref[0]
-        north = beside(tall, -1, 0)[middle]
-        south = beside(tall, 1, 0)[middle]
-        depth = fixed_ref[1, middle, :]
-        u = fixed_ref[3, middle, :] / depth
-        v = fixed_ref[4, middle, :] / depth
-        east = mask * east * (0.1 - 0.15 * jnp.minimum(u, 0.0))
-        west = mask * west * (0.1 + 0.15 * jnp.maximum(u, 0.0))
-        north = mask * north * (0.1 - 0.15 * jnp.minimum(v, 0.0))
-        south = mask * south * (0.1 + 0.15 * jnp.maximum(v, 0.0))
+        sub = lax.broadcasted_iota(i32, (rows, columns), 0)
+        u = flow_ref[0] / depth_ref[...]
+        v = flow_ref[1] / depth_ref[...]
+        east = mask * jnp.where(lane == columns - 1, 0.0, beside(mask, -1, 1)) * drift(u, 1.0)
+        west = mask * jnp.where(lane == 0, 0.0, beside(mask, 1, 1)) * drift(u, -1.0)
+        north = mask * jnp.where(sub == rows - 1, 0.0, beside(mask, -1, 0)) * drift(v, 1.0)
+        south = mask * jnp.where(sub == 0, 0.0, beside(mask, 1, 0)) * drift(v, -1.0)
         coef_ref[0] = 1.0 - (east + west + north + south)
         coef_ref[1] = east
         coef_ref[2] = west
         coef_ref[3] = north
         coef_ref[4] = south
 
-    lane_side = lax.broadcasted_iota(i32, (rows, LANES), 1)
     for n in range(per):
-        p = step * per + n
-        chosen = lane_side == p
-        first = jnp.sum(jnp.where(chosen, sides_ref[0], 0.0), axis=1, keepdims=True)
-        last = jnp.sum(jnp.where(chosen, sides_ref[1], 0.0), axis=1, keepdims=True)
-        south_row = south_ref[pl.ds(p, 1), :]
-        north_row = north_ref[pl.ds(p, 1), :]
         for r in range(0, rows, 8):
             span = slice(r, r + 8)
             q = planes_ref[n, span, :]
-            lane = lax.broadcasted_iota(i32, (8, columns), 1)
             sub = lax.broadcasted_iota(i32, (8, columns), 0)
-            east = jnp.where(lane == columns - 1, first[span], beside(q, -1, 1))
-            west = jnp.where(lane == 0, last[span], beside(q, 1, 1))
-            below = south_row if r == 0 else planes_ref[n, r - 1 : r, :]
-            above = north_row if r + 8 == rows else planes_ref[n, r + 8 : r + 9, :]
+            east = beside(q, -1, 1)
+            west = beside(q, 1, 1)
+            below = planes_ref[n, max(r - 1, 0) : max(r - 1, 0) + 1, :]
+            above = planes_ref[n, min(r + 8, rows - 1) : min(r + 8, rows - 1) + 1, :]
             north = jnp.where(sub == 7, above, beside(q, -1, 0))
             south = jnp.where(sub == 0, below, beside(q, 1, 0))
             out_ref[n, span, :] = (
@@ -269,7 +267,7 @@
             )
 
 
-def move(south, north, sides, fixed, side_fixed, planes):
+def move(mask, depth, flow, planes):
     levels, rows, columns = planes.shape
     per = 4
     return pl.pallas_call(
@@ -277,11 +275,9 @@
         name="tracer_move",
         grid=(levels // per,),
         in_specs=[
-            whole(south),
-            whole(north),
-            whole(sides),
-            whole(fixed),
-            whole(side_fixed),
+            whole(mask),
+            whole(depth),
+            whole(flow),
             pl.BlockSpec((per, rows, columns), lambda i: (i, 0, 0)),
         ],
         out_specs=pl.BlockSpec((per, rows, columns), lambda i: (i, 0, 0)),
@@ -289,12 +285,93 @@
         scratch_shapes=[pltpu.VMEM((5, rows, columns), f32)],
         compiler_params=params(56),
         cost_estimate=pl.CostEstimate(flops=1 << 25, bytes_accessed=18 << 20, transcendentals=0),
-    )(south, north, sides, fixed, side_fixed, planes)
-
-
-def solve_kernel(flux_ref, mask_ref, moved_ref, out_ref, ratio_ref, *, absorb, decay):
+    )(mask, depth, flow, planes)
+
+
+def patch_columns_kernel(west_ref, east_ref, own_west_ref, own_east_ref, moved_ref, out_ref):
+    upper = pl.program_id(0) == 1
+    levels, rows, _ = moved_ref.shape
+    edge = jnp.where(upper, LANES - 1, 0)
+    toward = jnp.where(upper, 1.0, -1.0)
+    lane = lax.broadcasted_iota(i32, (rows, LANES), 1)
+    hit = lane == edge
+
+    def column(field, chosen, low_ref, high_ref):
+        place = slice(field * rows, (field + 1) * rows)
+        value = jnp.where(upper, high_ref[place, :], low_ref[place, :])
+        return jnp.sum(jnp.where(chosen, value, 0.0), axis=1, keepdims=True)
+
+    mask = column(0, hit, own_west_ref, own_east_ref)
+    depth = column(1, hit, own_west_ref, own_east_ref)
+    flow = column(3, hit, own_west_ref, own_east_ref)
+    beyond = column(0, lane == LANES - 1 - edge, west_ref, east_ref)
+    coef = mask * beyond * drift(flow / depth, toward)
+    place = slice(5 * rows, 6 * rows)
+    near = jnp.where(upper, east_ref[place, :], west_ref[place, :])
+    own = jnp.where(upper, own_east_ref[place, :], own_west_ref[place, :])
+    extra = coef * (near - own)
+    for p in range(levels):
+        out_ref[p] = moved_ref[p] + jnp.where(hit, extra[:, p : p + 1], 0.0)
+
+
+def patch_columns(west, east, own_west, own_east, moved):
+    levels, rows, columns = moved.shape
+    last = columns // LANES - 1
+    block = pl.BlockSpec((levels, rows, LANES), lambda i: (0, 0, i * last))
+    return pl.pallas_call(
+        patch_columns_kernel,
+        name="patch_columns",
+        grid=(2,),
+        in_specs=[whole(west), whole(east), whole(own_west), whole(own_east), block],
+        out_specs=block,
+        out_shape=jax.ShapeDtypeStruct(moved.shape, f32),
+        input_output_aliases={4: 0},
+        compiler_params=params(56),
+        cost_estimate=pl.CostEstimate(flops=1 << 20, bytes_accessed=4 << 20, transcendentals=0),
+    )(west, east, own_west, own_east, moved)
+
+
+def solve_kernel(
+    flux_ref, mask_ref, depth_ref, flow_ref, near_ref, own_ref, moved_ref, out_ref, ratio_ref, *, part, parts, absorb, decay
+):
+    step = pl.program_id(0)
+    at_edge = step == (0 if part == 0 else pl.num_programs(0) - 1)
+    run = functools.partial(
+        solve_rows, flux_ref, mask_ref, depth_ref, flow_ref, near_ref, own_ref, moved_ref, out_ref, ratio_ref, absorb, decay
+    )
+    toward = -1.0 if part == 0 else 1.0
+
+    @pl.when(at_edge)
+    def _():
+        run(toward)
+
+    @pl.when(jnp.logical_not(at_edge))
+    def _():
+        run(None)
+
+
+def solve_rows(
+    flux_ref, mask_ref, depth_ref, flow_ref, near_ref, own_ref, moved_ref, out_ref, ratio_ref, absorb, decay, toward
+):
     levels = moved_ref.shape[1]
-    mask = mask_ref[...]
+    columns = mask_ref.shape[1]
+    planes = 2 * levels
+    mask = mask_ref[...].astype(f32)
+    if toward is not None:
+        row = 0 if toward < 0 else EDGE - 1
+        other = planes + (EDGE - 1 if toward < 0 else 0)
+        line = slice(row, row + 1)
+        coef = mask[line] * near_ref[other : other + 1, :] * drift(flow_ref[0, line, :] / depth_ref[line, :], toward)
+        hit = lax.broadcasted_iota(i32, (EDGE, columns), 0) == row
+
+    def moved(tracer, k):
+        value = moved_ref[tracer, k]
+        if toward is not None:
+            p = tracer * levels + k
+            extra = coef * (near_ref[p : p + 1, :] - own_ref[p : p + 1, :])
+            value = value + jnp.where(hit, extra, 0.0)
+        return value
+
     heat_top = 0.5 * mask * flux_ref[0]
     sun = 0.5 * mask * flux_ref[1]
     salt_top = mask * flux_ref[2]
@@ -306,8 +383,8 @@
     heat_last = None
     salt_last = None
     for k in range(levels):
-        heat = moved_ref[0, k] + absorb[k] * sun
-        salt = moved_ref[1, k]
+        heat = moved(0, k) + absorb[k] * sun
+        salt = moved(1, k)
         if k == 0:
             heat = heat + heat_top
             salt = salt + salt_top
@@ -334,44 +411,110 @@
         out_ref[1, k] = salt_last
 
 
-def solve(flux, mask, moved, part, parts):
+def solve(flux, mask, depth, flow, near, own, moved, part, parts):
     count, levels, rows, columns = moved.shape
     depths = np.arange(levels, dtype=np.float64)
     absorb = tuple(float(a) for a in np.exp(-depths / 3.0) - np.exp(-(depths + 1.0) / 3.0))
     decay = tuple(float(a) for a in np.exp(-depths / 2.0))
-    steps = rows // 8 // parts
+    steps = rows // EDGE // parts
     first = part * steps
-    return pl.pallas_call(
-        functools.partial(solve_kernel, absorb=absorb, decay=decay),
+    line = pl.BlockSpec((EDGE, columns), lambda i: (first + i, 0))
+    return pl.pallas_call(
+        functools.partial(solve_kernel, part=part, parts=parts, absorb=absorb, decay=decay),
         name=f"column_solve_{part}",
         grid=(steps,),
         in_specs=[
-            pl.BlockSpec((4, 8, columns), lambda i: (0, first + i, 0)),
-            pl.BlockSpec((8, columns), lambda i: (first + i, 0)),
-            pl.BlockSpec((count, levels, 8, columns), lambda i: (0, 0, first + i, 0)),
+            pl.BlockSpec((4, EDGE, columns), lambda i: (0, first + i, 0)),
+            line,
+            line,
+            pl.BlockSpec((1, EDGE, columns), lambda i: (1, first + i, 0)),
+            whole(near),
+            whole(own),
+            pl.BlockSpec((count, levels, EDGE, columns), lambda i: (0, 0, first + i, 0)),
         ],
-        out_specs=pl.BlockSpec((count, levels, 8, columns), lambda i: (0, 0, first + i, 0)),
+        out_specs=pl.BlockSpec((count, levels, EDGE, columns), lambda i: (0, 0, first + i, 0)),
         out_shape=jax.ShapeDtypeStruct(moved.shape, f32),
-        scratch_shapes=[pltpu.VMEM((levels, 8, columns), f32)],
-        input_output_aliases={2: 0},
+        scratch_shapes=[pltpu.VMEM((levels, EDGE, columns), f32)],
+        input_output_aliases={6: 0},
         compiler_params=params(56),
-        cost_estimate=pl.CostEstimate(flops=1 << 24, bytes_accessed=(18 << 20) // parts, transcendentals=0),
-    )(flux, mask, moved)
+        cost_estimate=pl.CostEstimate(flops=1 << 24, bytes_accessed=9 << 20, transcendentals=0),
+    )(flux, mask, depth, flow, near, own, moved)
+
+
+def sides_kernel(left_ref, right_ref, south_ref, north_ref, low_ref, high_ref, west_ref, east_ref):
+    rows = left_ref.shape[1]
+    columns = south_ref.shape[2]
+    levels = low_ref.shape[0] - 5 * EDGE
+    tall = rows + 2 * EDGE
+    for ref, part_ref, lanes in (
+        (west_ref, left_ref, slice(0, LANES)),
+        (east_ref, right_ref, slice(columns - LANES, columns)),
+    ):
+        for f in range(4):
+            start = f * tall
+            ref[start : start + EDGE, :] = south_ref[f, :, lanes]
+            ref[start + EDGE : start + EDGE + rows, :] = part_ref[f]
+            ref[start + EDGE + rows : start + tall, :] = north_ref[f, :, lanes]
+        for f in range(5):
+            start = 4 * tall + 2 * EDGE * f
+            place = slice(levels + f * EDGE, levels + (f + 1) * EDGE)
+            ref[start : start + EDGE, :] = low_ref[place, lanes]
+            ref[start + EDGE : start + 2 * EDGE, :] = high_ref[place, lanes]
+
+
+def sides(winds, south, north, low, high):
+    _, rows, columns = winds.shape
+    last = columns // LANES - 1
+    shape = jax.ShapeDtypeStruct((4 * (rows + 2 * EDGE) + 10 * EDGE, LANES), f32)
+    return pl.pallas_call(
+        sides_kernel,
+        name="tile_sides",
+        grid=(1,),
+        in_specs=[
+            pl.BlockSpec((4, rows, LANES), lambda i: (0, 0, 0)),
+            pl.BlockSpec((4, rows, LANES), lambda i: (0, 0, last)),
+            whole(south),
+            whole(north),
+            whole(low),
+            whole(high),
+        ],
+        out_specs=[whole(shape), whole(shape)],
+        out_shape=[shape, shape],
+        compiler_params=params(16),
+        cost_estimate=pl.CostEstimate(flops=1 << 16, bytes_accessed=2 << 20, transcendentals=0),
+    )(winds, winds, south, north, low, high)
 
 
 def barotropic_kernel(
-    fixed_ref, fixed_side_ref, flux_ref, south_ref, north_ref, west_ref, east_ref, height_ref, flow_ref, wide_ref
+    mask_ref, depth_ref, begin_ref, stream_ref, low_ref, high_ref, left_ref, right_ref,
+    flux_ref, south_ref, north_ref, west_ref, east_ref, height_ref, flow_ref, wide_ref,
 ):
-    rows = height_ref.shape[0]
-    columns = height_ref.shape[1]
-    wide_ref[0:5, :, :columns] = fixed_ref[...]
-    wide_ref[0:5, :, columns:] = fixed_side_ref[...]
+    rows, columns = begin_ref.shape
+    levels = low_ref.shape[0] - 5 * EDGE
+    tall = rows + 2 * EDGE
     middle = slice(EDGE, EDGE + rows)
-    wide_ref[5:9, :EDGE, :columns] = south_ref[...]
-    wide_ref[5:9, middle, :columns] = flux_ref[...]
-    wide_ref[5:9, EDGE + rows :, :columns] = north_ref[...]
-    lane = lax.broadcasted_iota(i32, west_ref.shape, 2)
-    wide_ref[5:9, :, columns:] = jnp.where(lane < LANES // 2, east_ref[...], west_ref[...])
+
+    def merge(low, high):
+        lane = lax.broadcasted_iota(i32, low.shape, 1)
+        return jnp.where(lane < LANES // 2, high, low)
+
+    for f, ref in enumerate([mask_ref, depth_ref, begin_ref, stream_ref.at[0], stream_ref.at[1]]):
+        place = slice(levels + f * EDGE, levels + (f + 1) * EDGE)
+        wide_ref[f, 0:EDGE, 0:columns] = low_ref[place, :]
+        wide_ref[f, middle, 0:columns] = ref[...].astype(f32)
+        wide_ref[f, EDGE + rows : tall, 0:columns] = high_ref[place, :]
+        place = slice(f * rows, (f + 1) * rows)
+        wide_ref[f, middle, columns : columns + LANES] = merge(left_ref[place, :], right_ref[place, :])
+        start = 4 * tall + 2 * EDGE * f
+        corner = merge(west_ref[start : start + 2 * EDGE, :], east_ref[start : start + 2 * EDGE, :])
+        wide_ref[f, 0:EDGE, columns : columns + LANES] = corner[0:EDGE]
+        wide_ref[f, EDGE + rows : tall, columns : columns + LANES] = corner[EDGE : 2 * EDGE]
+    for f in range(4):
+        wide_ref[5 + f, 0:EDGE, 0:columns] = south_ref[f]
+        wide_ref[5 + f, middle, 0:columns] = flux_ref[f]
+        wide_ref[5 + f, EDGE + rows : tall, 0:columns] = north_ref[f]
+        place = slice(f * tall, (f + 1) * tall)
+        wide_ref[5 + f, :, columns : columns + LANES] = merge(west_ref[place, :], east_ref[place, :])
     mask = wide_ref[0]
     drag = -0.5 * wide_ref[1]
     height = wide_ref[2]
@@ -392,34 +535,20 @@
     flow_ref[1] = across[middle, :columns]
 
 
-def barotropic(fixed, fixed_side, flux, south, north, west, east):
-    _, tall, columns = fixed.shape
-    rows = tall - 2 * EDGE
+def barotropic(*arrays):
+    rows, columns = arrays[2].shape
+    outs = [jax.ShapeDtypeStruct((rows, columns), f32), jax.ShapeDtypeStruct((2, rows, columns), f32)]
     return pl.pallas_call(
         barotropic_kernel,
         name="barotropic",
         grid=(1,),
-        in_specs=[
-            whole(fixed),
-            whole(fixed_side),
-            pl.BlockSpec((4, rows, columns), lambda i: (0, 0, 0)),
-            whole(south),
-            whole(north),
-            whole(west),
-            whole(east),
-        ],
-        out_specs=[
-            pl.BlockSpec((rows, columns), lambda i: (0, 0)),
-            pl.BlockSpec((2, rows, columns), lambda i: (0, 0, 0)),
-        ],
-        out_shape=[
-            jax.ShapeDtypeStruct((rows, columns), f32),
-            jax.ShapeDtypeStruct((2, rows, columns), f32),
-        ],
-        scratch_shapes=[pltpu.VMEM((9, tall, columns + LANES), f32)],
-        compiler_params=params(24),
+        in_specs=[whole(array) for array in arrays],
+        out_specs=[whole(out) for out in outs],
+        out_shape=outs,
+        scratch_shapes=[pltpu.VMEM((9, rows + 2 * EDGE, columns + LANES), f32)],
+        compiler_params=params(32),
         cost_estimate=pl.CostEstimate(flops=1 << 24, bytes_accessed=6 << 20, transcendentals=0),
-    )(fixed, fixed_side, flux, south, north, west, east)
+    )(*arrays)
 
 
 def to_next(array, axes):
@@ -430,11 +559,6 @@
 def to_previous(array, axes):
     ends = lax.axis_size(axes) - 1
     return lax.ppermute(array, axes, [(i + 1, i) for i in range(ends)])
-
-
-def merge_sides(from_west, from_east):
-    lane = lax.broadcasted_iota(i32, from_west.shape, from_west.ndim - 1)
-    return jnp.where(lane < LANES // 2, from_east, from_west)
 
 
 def all_to_all(array):
@@ -463,50 +587,29 @@
     )
     arrived = all_to_all(packed)
 
-    mask = land_mask.astype(f32)
     planes = tracers.reshape(count * levels, rows, columns)
-    tracer_south, tracer_north, tracer_sides = edges(planes)
-    fixed = jnp.concatenate([jnp.stack([mask, sea_depth, sea_height]), transport], axis=0)
-    tops = fixed[:, rows - EDGE :].reshape(5 * EDGE, columns)
-    bottoms = fixed[:, :EDGE].reshape(5 * EDGE, columns)
-    from_south = to_next(jnp.concatenate([tracer_north, tops], axis=0), ROWS)
-    from_north = to_previous(jnp.concatenate([tracer_south, bottoms], axis=0), ROWS)
-    wide = count * levels
-    fixed = jnp.concatenate(
-        [
-            from_south[wide:].reshape(5, EDGE, columns),
-            fixed,
-            from_north[wide:].reshape(5, EDGE, columns),
-        ],
-        axis=1,
-    )
-    tall = rows + 2 * EDGE
-    east_edge = jnp.concatenate([fixed[:, :, -LANES:].reshape(5 * tall, LANES), tracer_sides[1]], axis=0)
-    west_edge = jnp.concatenate([fixed[:, :, :LANES].reshape(5 * tall, LANES), tracer_sides[0]], axis=0)
-    from_west = to_next(east_edge, "tx")
-    from_east = to_previous(west_edge, "tx")
-    fixed_side = merge_sides(from_west[: 5 * tall], from_east[: 5 * tall]).reshape(5, tall, LANES)
-    sides = jnp.stack([from_east[5 * tall :], from_west[5 * tall :]])
-    moved = move(from_south[:wide], from_north[:wide], sides, fixed, fixed_side, planes)
-
+    own_south, own_north, own_west, own_east = edges(planes, land_mask, sea_depth, sea_height, transport)
+    from_west = to_next(own_east, "tx")
+    from_east = to_previous(own_west, "tx")
+    from_south = to_next(own_north, ROWS)
+    from_north = to_previous(own_south, ROWS)
+    moved = move(land_mask, sea_depth, transport, planes)
+    moved = patch_columns(from_west, from_east, own_west, own_east, moved).reshape(tracers.shape)
     arrived, moved = lax.optimization_barrier((arrived, moved))
+
     winds, heats, flux_low, flux_high = spread(arrived, rows, columns)
     flux_south = to_next(flux_high, ROWS)
     flux_north = to_previous(flux_low, ROWS)
-    moved = solve(heats, mask, moved.reshape(tracers.shape), 0, 2)
+    moved = solve(heats, land_mask, sea_depth, transport, from_south, own_south, moved, 0, 2)
     flux_south, flux_north, moved = lax.optimization_barrier((flux_south, flux_north, moved))
-    east_edge = jnp.concatenate(
-        [flux_south[:, :, -LANES:], winds[:, :, -LANES:], flux_north[:, :, -LANES:]], axis=1
-    )
-    west_edge = jnp.concatenate(
-        [flux_south[:, :, :LANES], winds[:, :, :LANES], flux_north[:, :, :LANES]], axis=1
-    )
-    flux_west = to_next(east_edge, "tx")
-    flux_east = to_previous(west_edge, "tx")
-    solved = solve(heats, mask, moved, 1, 2)
+    side_west, side_east = sides(winds, flux_south, flux_north, from_south, from_north)
+    flux_west = to_next(side_east, "tx")
+    flux_east = to_previous(side_west, "tx")
+    solved = solve(heats, land_mask, sea_depth, transport, from_north, own_north, moved, 1, 2)
     flux_west, flux_east, solved = lax.optimization_barrier((flux_west, flux_east, solved))
     new_height, new_transport = barotropic(
-        fixed, fixed_side, winds, flux_south, flux_north, flux_west, flux_east
+        land_mask, sea_depth, sea_height, transport, from_south, from_north, from_west, from_east,
+        winds, flux_south, flux_north, flux_west, flux_east,
     )
     return new_height, new_transport, solved
 

time: 134 us -> 100 us (0.75); the launches traced: 131 us -> 99.2 us
  waiting for transfers between devices: 30.9 us -> 4.18 us
  starting transfers between devices: 38.7 us -> 34.8 us
  Pallas kernels: 51.2 us -> 54.2 us
  other arithmetic: 2.33 us -> 0 us
  local copies, waits for them, and re-layouts: 6.97 us -> 5.12 us
    ppermute x4, waiting for transfers between devices: 30.8 us -> 0.01 us  [to_previous(): return lax.ppermute(array, axes, [(i + 1, i) for i in range(ends)])]
    ppermute x4, starting transfers between devices: 21.2 us -> 12.5 us  [to_previous(): return lax.ppermute(array, axes, [(i + 1, i) for i in range(ends)])]
    pallas_call x3 -> x5, Pallas kernels: 14.9 us -> 20.1 us  [the longest x2 12.3 us: solve(): pl.pallas_call(functools.partial(solve_kernel, part=part, parts=parts, ab...]
    ppermute x4, starting transfers between devices: 6.48 us -> 11.6 us  [to_next(): return lax.ppermute(array, axes, [(i, i + 1) for i in range(ends)])]
    all_to_all x1, waiting for transfers between devices: 0.01 us -> 4.16 us  [all_to_all(): return lax.all_to_all(array, EVERY, split_axis=0, concat_axis=0, tiled=True)]
    pallas_call x1, Pallas kernels: 16.1 us -> 14.3 us  [spread(): pl.pallas_call(functools.partial(spread_kernel, group=group), name='sprea...]
    slice x5 -> x0, local copies, waits for them, and re-layouts: 1.37 us -> none  [the longest x1 0.66 us: local(): from_south[:wide]]
    unnamed x32 -> x28, local copies, waits for them, and re-layouts: 5.56 us -> 5.12 us
  transfers between devices with their start and end apart: 9 -> 9, of which waited for: 1 -> 1; matrix products, arithmetic and copies ran while one was open for 3% -> 0% of each run, Pallas kernels for 21% -> 46%
where the time goes in v4:
time: 100 us; the launch traced here: 99.2 us
  Pallas kernels  54.2 us (54%)
  starting transfers between devices  34.8 us (35%)
  local copies, waits for them, and re-layouts  5.12 us (5%)
  waiting for transfers between devices  4.18 us (4%)
    pallas_call x1, Pallas kernels, spread(): pl.pallas_call(functools.partial(spread_kernel, group=group), name='sprea...  14.3 us
    ppermute x4, starting transfers between devices, to_previous(): return lax.ppermute(array, axes, [(i + 1, i) for i in range(ends)])  12.5 us
    pallas_call x2, Pallas kernels, solve(): pl.pallas_call(functools.partial(solve_kernel, part=part, parts=parts, ab...  12.3 us
    ppermute x4, starting transfers between devices, to_next(): return lax.ppermute(array, axes, [(i, i + 1) for i in range(ends)])  11.6 us
    pallas_call x1, Pallas kernels, move(): pl.pallas_call(functools.partial(move_kernel, per=per), name='tracer_move...  11.3 us
    all_to_all x1, starting transfers between devices, all_to_all(): return lax.all_to_all(array, EVERY, split_axis=0, concat_axis=0, tiled=True)  10.6 us
    pallas_call x1, Pallas kernels, pack(): pl.pallas_call(functools.partial(pack_kernel, beyond=beyond), name='pack_...  5.7 us
    unnamed x28, local copies, waits for them, and re-layouts  5.12 us
  transfers between devices with their start and end apart: 9, of which 1 were waited for; matrix products, arithmetic and copies ran while one was open for 0% of the time, Pallas kernels for 46%

profile of v4, /device:TPU:15, one launch (start us, length us, event | category | flops | bytes accessed | tf_op | source)
XLA Modules:
  0.0 99.2 jit_solution(1821284420745523815)
XLA Ops:
  0.6 5.7 %pack_margin.1 = f32[128,9,4,128]{3,2,1,0:T(4,128)} custom-call(s32[256]{0:T(256)} %bitcast.9, f32[8,16384]{1,0:T(8,128)} %flux_ref.1, s32[256,128]{1,0:T(8,128)} %source_ref.1, s32[256,128]{1,0:T(8,128)} %cell_ref.1, f32[256,128]{1,0:T(8,128)} %weight_ref.1), custom_call_target="tpu_custom_call" | custom-call | flops 4194304 | bytes 4194304 | tf_op jit(solution)/shard_map/pack_margin/pallas_call | solution.py:71
  6.3 10.6 %all-to-all-start = ((f32[128,9,4,128]{3,2,1,0:T(4,128)}), f32[128,9,4,128]{3,2,1,0:T(4,128)S(1)}, u32[]{:S(2)}, u32[]{:S(2)}) async-start(f32[128,9,4,128]{3,2,1,0:T(4,128)} %pack_margin.1), calls=%async_computation | async-start | bytes 4718592 | tf_op jit(solution)/shard_map/all_to_all | solution.py:565
  17.0 4.2 %tile_edges.1 = (f32[72,1024]{1,0:T(8,128)}, f32[72,1024]{1,0:T(8,128)}, f32[384,128]{1,0:T(8,128)}, f32[384,128]{1,0:T(8,128)}) custom-call(f32[32,64,1024]{2,1,0:T(8,128)} %bitcast.3, f32[32,64,1024]{2,1,0:T(8,128)} %bitcast.4, f32[32,64,1024]{2,1,0:T(8,128)} %bitcast.5, f32[32,64,1024]{2,1,0:T(8,128)} %bitcast.6, s32[64,1024]{1,0:T(8,128)} %mask_ref.4, ...), custom_call_target="tpu_custom_call" | custom-call | flops 1048576 | bytes 6291456 | tf_op jit(solution)/shard_map/tile_edges/pallas_call | solution.py:199
  21.2 1.3 %collective-permute-start.2 = (f32[384,128]{1,0:T(8,128)}, f32[384,128]{1,0:T(8,128)S(1)}, u32[]{:S(2)}, u32[]{:S(2)}) collective-permute-start(f32[384,128]{1,0:T(8,128)} %get-tuple-element.36.own_east_ref), channel_id=1, source_target_pairs={{0,1},{1,2},{2,3},{3,4},{4,5},{5,6},{6,7},{8,9},{9,10},{10,11},{11... | collective-permute-start | bytes 589832 | tf_op jit(solution)/shard_map/ppermute | solution.py:556
  22.5 3.0 %collective-permute-start.3 = (f32[384,128]{1,0:T(8,128)}, f32[384,128]{1,0:T(8,128)S(1)}, u32[]{:S(2)}, u32[]{:S(2)}) collective-permute-start(f32[384,128]{1,0:T(8,128)} %get-tuple-element.37.own_west_ref), channel_id=1, source_target_pairs={{1,0},{2,1},{3,2},{4,3},{5,4},{6,5},{7,6},{9,8},{10,9},{11,10},{12... | collective-permute-start | bytes 589832 | tf_op jit(solution)/shard_map/ppermute | solution.py:561
  25.5 5.1 %collective-permute-start = (f32[72,1024]{1,0:T(8,128)}, f32[72,1024]{1,0:T(8,128)S(1)}, u32[]{:S(2)}, u32[]{:S(2)}) collective-permute-start(f32[72,1024]{1,0:T(8,128)} %get-tuple-element.34.own_ref), channel_id=1, source_target_pairs={{0,8},{8,16},{16,24},{24,32},{32,40},{40,48},{48,56},{56,64},{64,7... | collective-permute-start | bytes 884744 | tf_op jit(solution)/shard_map/ppermute | solution.py:556
  30.7 2.6 %collective-permute-start.1 = (f32[72,1024]{1,0:T(8,128)}, f32[72,1024]{1,0:T(8,128)S(1)}, u32[]{:S(2)}, u32[]{:S(2)}) collective-permute-start(f32[72,1024]{1,0:T(8,128)} %get-tuple-element.35.own_ref), channel_id=1, source_target_pairs={{8,0},{16,8},{24,16},{32,24},{40,32},{48,40},{56,48},{64,56},{72,6... | collective-permute-start | bytes 884744 | tf_op jit(solution)/shard_map/ppermute | solution.py:561
  33.2 11.3 %tracer_move.1.moved_ref = f32[32,64,1024]{2,1,0:T(8,128)} custom-call(s32[64,1024]{1,0:T(8,128)} %mask_ref.4, f32[64,1024]{1,0:T(8,128)} %depth_ref.4, f32[2,64,1024]{2,1,0:T(8,128)} %stream_ref, f32[32,64,1024]{2,1,0:T(8,128)} %bitcast.7), custom_call_target="tpu_custom_call" | custom-call | flops 33554432 | bytes 18874368 | tf_op jit(solution)/shard_map/tracer_move/pallas_call | solution.py:273
  44.6 0.0 collective-permute-done.2.west_ref.left_ref
  44.6 0.0 collective-permute-done.3.east_ref.right_ref
  44.6 0.7 copy-done.10
  45.3 0.7 copy-done.12
  45.9 3.5 %patch_columns.1 = f32[32,64,1024]{2,1,0:T(8,128)} custom-call(f32[384,128]{1,0:T(8,128)} %copy-done.10, f32[384,128]{1,0:T(8,128)} %copy-done.12, f32[384,128]{1,0:T(8,128)} %get-tuple-element.37.own_west_ref, f32[384,128]{1,0:T(8,128)} %get-tuple-element.36.own_east_ref, f32[32,64,1024]{2,1,0:T(8,128)} %tracer_move.1.moved_ref), custom_call_target="tpu_custom_call", output_to_operand_aliasing={{}: (4, {})} | custom-call | flops 1048576 | bytes 4194304 | tf_op jit(solution)/shard_map/patch_columns/pallas_call | solution.py:321
  49.4 4.2 %all-to-all-done.load_ref = f32[128,9,4,128]{3,2,1,0:T(4,128)S(1)} async-done(((f32[128,9,4,128]{3,2,1,0:T(4,128)}), f32[128,9,4,128]{3,2,1,0:T(4,128)S(1)}, u32[]{:S(2)}, u32[]{:S(2)}) %all-to-all-start) | async-done | bytes 2359328 | tf_op jit(solution)/shard_map/all_to_all | solution.py:565
  53.6 14.3 %spread_all.1 = (f32[4,64,1024]{2,1,0:T(8,128)S(1)}, f32[4,64,1024]{2,1,0:T(8,128)S(1)}, f32[4,8,1024]{2,1,0:T(8,128)S(1)}, f32[4,8,1024]{2,1,0:T(8,128)S(1)}) custom-call(f32[128,9,4,128]{3,2,1,0:T(4,128)S(1)} %all-to-all-done.load_ref), custom_call_target="tpu_custom_call" | custom-call | flops 1073741824 | bytes 4194304 | tf_op jit(solution)/shard_map/spread_all/pallas_call | solution.py:151
  68.0 0.0 copy-start.3
  68.0 1.0 %copy-done.3 = f32[4,64,1024]{2,1,0:T(8,128)} copy-done((f32[4,64,1024]{2,1,0:T(8,128)}, f32[4,64,1024]{2,1,0:T(8,128)S(1)}, u32[]{:S(2)}) %copy-start.3) | copy-done | bytes 1048600
  69.0 3.9 %collective-permute-start.4 = (f32[4,8,1024]{2,1,0:T(8,128)S(1)}, f32[4,8,1024]{2,1,0:T(8,128)S(1)}, u32[]{:S(2)}, u32[]{:S(2)}) collective-permute-start(f32[4,8,1024]{2,1,0:T(8,128)S(1)} %get-tuple-element.41), channel_id=1, source_target_pairs={{0,8},{8,16},{16,24},{24,32},{32,40},{40,48},{48,56},{56,64},{64,7... | collective-permute-start | bytes 393224 | tf_op jit(solution)/shard_map/ppermute | solution.py:556
  72.9 3.7 %collective-permute-start.5 = (f32[4,8,1024]{2,1,0:T(8,128)S(1)}, f32[4,8,1024]{2,1,0:T(8,128)S(1)}, u32[]{:S(2)}, u32[]{:S(2)}) collective-permute-start(f32[4,8,1024]{2,1,0:T(8,128)S(1)} %get-tuple-element.42), channel_id=1, source_target_pairs={{8,0},{16,8},{24,16},{32,24},{40,32},{48,40},{56,48},{64,56},{72,6... | collective-permute-start | bytes 393224 | tf_op jit(solution)/shard_map/ppermute | solution.py:561
  76.7 0.0 collective-permute-done.near_ref.low_ref
  76.7 0.0 copy-start.4
  76.7 0.7 copy-done.4
  77.4 6.2 %column_solve_0.1.moved_ref = f32[2,16,64,1024]{3,2,1,0:T(8,128)} custom-call(f32[4,64,1024]{2,1,0:T(8,128)} %copy-done.3, s32[64,1024]{1,0:T(8,128)} %mask_ref.4, f32[64,1024]{1,0:T(8,128)} %depth_ref.4, f32[2,64,1024]{2,1,0:T(8,128)} %stream_ref, f32[72,1024]{1,0:T(8,128)} %copy-done.4, ...), custom_call_target="tpu_custom_call", output_to_operand_aliasing={{}: (6, {})} | custom-call | flops 16777216 | bytes 9437184 | tf_op jit(solution)/shard_map/column_solve_0/pallas_call | solution.py:422
  83.5 0.0 collective-permute-done.4.south_ref
  83.5 0.0 collective-permute-done.5.north_ref
  83.5 0.0 collective-permute-done.1.high_ref.near_ref
  83.6 0.0 copy-start.7
  83.6 0.0 copy-start.5
  83.6 1.1 %copy-done.5 = f32[72,1024]{1,0:T(8,128)S(1)} copy-done((f32[72,1024]{1,0:T(8,128)S(1)}, f32[72,1024]{1,0:T(8,128)}, u32[]{:S(2)}) %copy-start.5) | copy-done | bytes 294936
  84.7 1.3 %collective-permute-start.6 = (f32[400,128]{1,0:T(8,128)S(1)}, f32[400,128]{1,0:T(8,128)S(1)}, u32[]{:S(2)}, u32[]{:S(2)}) collective-permute-start(f32[400,128]{1,0:T(8,128)S(1)} %get-tuple-element.47), channel_id=1, source_target_pairs={{0,1},{1,2},{2,3},{3,4},{4,5},{5,6},{6,7},{8,9},{9,10},{10,11},{11... | collective-permute-start | bytes 614408 | tf_op jit(solution)/shard_map/ppermute | solution.py:556
  86.0 0.0 copy-start
  86.0 0.0 copy-start.1
  86.0 0.0 copy-start.2
  86.0 0.0 copy-start.6
  86.0 0.0 copy-start.9
  86.0 0.0 copy-start.11
  86.0 0.0 copy-start.13
  86.0 3.2 %collective-permute-start.7 = (f32[400,128]{1,0:T(8,128)S(1)}, f32[400,128]{1,0:T(8,128)S(1)}, u32[]{:S(2)}, u32[]{:S(2)}) collective-permute-start(f32[400,128]{1,0:T(8,128)S(1)} %get-tuple-element.48), channel_id=1, source_target_pairs={{1,0},{2,1},{3,2},{4,3},{5,4},{6,5},{7,6},{9,8},{10,9},{11,10},{12... | collective-permute-start | bytes 614408 | tf_op jit(solution)/shard_map/ppermute | solution.py:561
  89.2 0.0 copy-done.7
  89.2 6.2 %column_solve_1.1 = f32[2,16,64,1024]{3,2,1,0:T(8,128)} custom-call(f32[4,64,1024]{2,1,0:T(8,128)} %copy-done.3, s32[64,1024]{1,0:T(8,128)} %mask_ref.4, f32[64,1024]{1,0:T(8,128)} %depth_ref.4, f32[2,64,1024]{2,1,0:T(8,128)} %stream_ref, f32[72,1024]{1,0:T(8,128)} %copy-done.7, ...), custom_call_target="tpu_custom_call", output_to_operand_aliasing={{}: (6, {})} | custom-call | flops 16777216 | bytes 9437184 | tf_op jit(solution)/shard_map/column_solve_1/pallas_call | solution.py:422
  95.4 0.0 collective-permute-done.6.west_ref
  95.4 0.0 collective-permute-done.7.east_ref
  95.4 0.0 copy-done
  95.4 0.0 copy-done.1
  95.4 0.0 copy-done.2
  95.5 0.0 copy-start.8
  95.5 1.0 copy-done.8
  96.5 2.8 %barotropic.1 = (f32[64,1024]{1,0:T(8,128)}, f32[2,64,1024]{2,1,0:T(8,128)}) custom-call(s32[64,1024]{1,0:T(8,128)S(1)} %copy-done.1, f32[64,1024]{1,0:T(8,128)S(1)} %copy-done.2, f32[64,1024]{1,0:T(8,128)S(1)} %copy-done.9, f32[2,64,1024]{2,1,0:T(8,128)S(1)} %copy-done, f32[72,1024]{1,0:T(8,128)S(1)} %copy-done.6, f32[72,1024]{1,0:T(8,128)S(1)} %copy-done.8, ...), custom_call_target="tpu_custom_call" | custom-call | flops 16777216 | bytes 6291456 | tf_op jit(solution)/shard_map/barotropic/pallas_call | solution.py:541
  (7 shorter events, 0.0 us)
Async XLA Ops:
  6.3 47.3 %all-to-all-start = ((f32[128,9,4,128]{3,2,1,0:T(4,128)}), f32[128,9,4,128]{3,2,1,0:T(4,128)S(1)}, u32[]{:S(2)}, u32[]{:S(2)}) async-start(f32[128,9,4,128]{3,2,1,0:T(4,128)} %pack_margin.1), calls=%async_computation | async-start | bytes 4718592 | tf_op jit(solution)/shard_map/all_to_all | solution.py:565
  21.2 23.4 %collective-permute-start.2 = (f32[384,128]{1,0:T(8,128)}, f32[384,128]{1,0:T(8,128)S(1)}, u32[]{:S(2)}, u32[]{:S(2)}) collective-permute-start(f32[384,128]{1,0:T(8,128)} %get-tuple-element.36.own_east_ref), channel_id=1, source_target_pairs={{0,1},{1,2},{2,3},{3,4},{4,5},{5,6},{6,7},{8,9},{9,10},{10,11},{11... | collective-permute-start | bytes 589832 | tf_op jit(solution)/shard_map/ppermute | solution.py:556
  22.5 22.1 %collective-permute-start.3 = (f32[384,128]{1,0:T(8,128)}, f32[384,128]{1,0:T(8,128)S(1)}, u32[]{:S(2)}, u32[]{:S(2)}) collective-permute-start(f32[384,128]{1,0:T(8,128)} %get-tuple-element.37.own_west_ref), channel_id=1, source_target_pairs={{1,0},{2,1},{3,2},{4,3},{5,4},{6,5},{7,6},{9,8},{10,9},{11,10},{12... | collective-permute-start | bytes 589832 | tf_op jit(solution)/shard_map/ppermute | solution.py:561
  25.5 51.1 %collective-permute-start = (f32[72,1024]{1,0:T(8,128)}, f32[72,1024]{1,0:T(8,128)S(1)}, u32[]{:S(2)}, u32[]{:S(2)}) collective-permute-start(f32[72,1024]{1,0:T(8,128)} %get-tuple-element.34.own_ref), channel_id=1, source_target_pairs={{0,8},{8,16},{16,24},{24,32},{32,40},{40,48},{48,56},{56,64},{64,7... | collective-permute-start | bytes 884744 | tf_op jit(solution)/shard_map/ppermute | solution.py:556
  30.7 52.9 %collective-permute-start.1 = (f32[72,1024]{1,0:T(8,128)}, f32[72,1024]{1,0:T(8,128)S(1)}, u32[]{:S(2)}, u32[]{:S(2)}) collective-permute-start(f32[72,1024]{1,0:T(8,128)} %get-tuple-element.35.own_ref), channel_id=1, source_target_pairs={{8,0},{16,8},{24,16},{32,24},{40,32},{48,40},{56,48},{64,56},{72,6... | collective-permute-start | bytes 884744 | tf_op jit(solution)/shard_map/ppermute | solution.py:561
  44.6 0.7 copy-start.10
  45.3 0.7 copy-start.12
  68.0 1.0 %copy-start.3 = (f32[4,64,1024]{2,1,0:T(8,128)}, f32[4,64,1024]{2,1,0:T(8,128)S(1)}, u32[]{:S(2)}) copy-start(f32[4,64,1024]{2,1,0:T(8,128)S(1)} %get-tuple-element.43.flux_ref) | copy-start | bytes 3145732
  69.0 14.6 %collective-permute-start.4 = (f32[4,8,1024]{2,1,0:T(8,128)S(1)}, f32[4,8,1024]{2,1,0:T(8,128)S(1)}, u32[]{:S(2)}, u32[]{:S(2)}) collective-permute-start(f32[4,8,1024]{2,1,0:T(8,128)S(1)} %get-tuple-element.41), channel_id=1, source_target_pairs={{0,8},{8,16},{16,24},{24,32},{32,40},{40,48},{48,56},{56,64},{64,7... | collective-permute-start | bytes 393224 | tf_op jit(solution)/shard_map/ppermute | solution.py:556
  72.9 10.6 %collective-permute-start.5 = (f32[4,8,1024]{2,1,0:T(8,128)S(1)}, f32[4,8,1024]{2,1,0:T(8,128)S(1)}, u32[]{:S(2)}, u32[]{:S(2)}) collective-permute-start(f32[4,8,1024]{2,1,0:T(8,128)S(1)} %get-tuple-element.42), channel_id=1, source_target_pairs={{8,0},{16,8},{24,16},{32,24},{40,32},{48,40},{56,48},{64,56},{72,6... | collective-permute-start | bytes 393224 | tf_op jit(solution)/shard_map/ppermute | solution.py:561
  76.7 0.7 copy-start.4
  83.6 5.7 %copy-start.7 = (f32[72,1024]{1,0:T(8,128)}, f32[72,1024]{1,0:T(8,128)S(1)}, u32[]{:S(2)}) copy-start(f32[72,1024]{1,0:T(8,128)S(1)} %collective-permute-done.1.high_ref.near_ref) | copy-start | bytes 884740
  83.6 1.1 %copy-start.5 = (f32[72,1024]{1,0:T(8,128)S(1)}, f32[72,1024]{1,0:T(8,128)}, u32[]{:S(2)}) copy-start(f32[72,1024]{1,0:T(8,128)} %copy-done.4) | copy-start | bytes 884740
  84.7 10.7 %collective-permute-start.6 = (f32[400,128]{1,0:T(8,128)S(1)}, f32[400,128]{1,0:T(8,128)S(1)}, u32[]{:S(2)}, u32[]{:S(2)}) collective-permute-start(f32[400,128]{1,0:T(8,128)S(1)} %get-tuple-element.47), channel_id=1, source_target_pairs={{0,1},{1,2},{2,3},{3,4},{4,5},{5,6},{6,7},{8,9},{9,10},{10,11},{11... | collective-permute-start | bytes 614408 | tf_op jit(solution)/shard_map/ppermute | solution.py:556
  86.0 9.5 %copy-start = (f32[2,64,1024]{2,1,0:T(8,128)S(1)}, f32[2,64,1024]{2,1,0:T(8,128)}, u32[]{:S(2)}) copy-start(f32[2,64,1024]{2,1,0:T(8,128)} %stream_ref) | copy-start | bytes 1572868
  86.0 9.5 %copy-start.1 = (s32[64,1024]{1,0:T(8,128)S(1)}, s32[64,1024]{1,0:T(8,128)}, u32[]{:S(2)}) copy-start(s32[64,1024]{1,0:T(8,128)} %mask_ref.4) | copy-start | bytes 786436
  86.0 9.5 %copy-start.2 = (f32[64,1024]{1,0:T(8,128)S(1)}, f32[64,1024]{1,0:T(8,128)}, u32[]{:S(2)}) copy-start(f32[64,1024]{1,0:T(8,128)} %depth_ref.4) | copy-start | bytes 786436
  86.0 9.4 %copy-start.6 = (f32[72,1024]{1,0:T(8,128)S(1)}, f32[72,1024]{1,0:T(8,128)}, u32[]{:S(2)}) copy-start(f32[72,1024]{1,0:T(8,128)} %copy-done.4) | copy-start | bytes 884740
  86.0 9.4 %copy-start.9 = (f32[64,1024]{1,0:T(8,128)S(1)}, f32[64,1024]{1,0:T(8,128)}, u32[]{:S(2)}) copy-start(f32[64,1024]{1,0:T(8,128)} %begin_ref) | copy-start | bytes 786436
  86.0 9.4 %copy-start.11 = (f32[384,128]{1,0:T(8,128)S(1)}, f32[384,128]{1,0:T(8,128)}, u32[]{:S(2)}) copy-start(f32[384,128]{1,0:T(8,128)} %copy-done.10) | copy-start | bytes 589828
  86.0 9.4 %copy-start.13 = (f32[384,128]{1,0:T(8,128)S(1)}, f32[384,128]{1,0:T(8,128)}, u32[]{:S(2)}) copy-start(f32[384,128]{1,0:T(8,128)} %copy-done.12) | copy-start | bytes 589828
  86.0 9.4 %collective-permute-start.7 = (f32[400,128]{1,0:T(8,128)S(1)}, f32[400,128]{1,0:T(8,128)S(1)}, u32[]{:S(2)}, u32[]{:S(2)}) collective-permute-start(f32[400,128]{1,0:T(8,128)S(1)} %get-tuple-element.48), channel_id=1, source_target_pairs={{1,0},{2,1},{3,2},{4,3},{5,4},{6,5},{7,6},{9,8},{10,9},{11,10},{12... | collective-permute-start | bytes 614408 | tf_op jit(solution)/shard_map/ppermute | solution.py:561
  95.5 1.0 copy-start.8

commit v5 on v4

--- a/solution.py
+++ b/solution.py
@@ -82,7 +82,6 @@
 
 
 def spread_kernel(load_ref, winds_ref, heats_ref, south_ref, north_ref, acc_ref, *, group):
-    sources = load_ref.shape[0]
     _, rows, columns = winds_ref.shape
     fields = 8
     high = columns // LANES
@@ -90,7 +89,10 @@
     def clear(i, c):
         acc_ref[pl.ds(pl.multiple_of(i * 256, 256), 256),:] = jnp.zeros((256, LANES), f32)
         return c
-    lax.fori_loop(0, rows * depth // 256, clear, 0)
+    @pl.when(pl.program_id(0) == 0)
+    def _():
+        lax.fori_loop(0, rows * depth // 256, clear, 0)
+
     low_iota = lax.broadcasted_iota(i32, (LANES, LANES), 0).astype(f32).astype(jnp.bfloat16)
     pattern = [
         (2 * i + (lax.broadcasted_iota(i32, (16, LANES), 0) >> 3)).astype(f32).astype(jnp.bfloat16) for i in range(high // 2)
@@ -99,37 +101,32 @@
     one = jnp.ones((LANES, LANES), jnp.bfloat16)
     zero = jnp.zeros((LANES, LANES), jnp.bfloat16)
 
-    def step(i, carry):
-        for g in range(group):
-            s = i * group + g
-            cells = load_ref[s, 8].astype(i32)
-            highs = ((cells & (columns - 1)) >> 7).astype(f32)
-            lows = (cells & (LANES - 1)).astype(f32)
-            for k in range(4):
-                value = jnp.concatenate([load_ref[s, k], load_ref[s, 4 + k]], axis=0)
-                coarse = value.astype(jnp.bfloat16).astype(f32)
-                fine = value - coarse
-                coarse = jnp.concatenate([coarse, coarse], axis=0).astype(jnp.bfloat16)
-                fine = jnp.concatenate([fine, fine], axis=0).astype(jnp.bfloat16)
-                hk = jnp.broadcast_to(highs[k : k + 1], (16, LANES)).astype(jnp.bfloat16)
-                lk = jnp.broadcast_to(lows[k : k + 1], (16, LANES)).astype(jnp.bfloat16)
-                lk = jnp.concatenate([lk] * (LANES // 16), axis=0)
-                left = []
-                right = []
-                for p in pattern:
-                    hit = hk == p
-                    left.append(jnp.where(hit, coarse, zero16))
-                    right.append(jnp.where(hit, fine, zero16))
-                lhs = jnp.concatenate([jnp.concatenate(left, axis=0), jnp.concatenate(right, axis=0)], axis=1)
-                onehot = jnp.where(lk == low_iota, one, zero)
-                rhs = jnp.concatenate([onehot, onehot], axis=1)
-                both = lax.dot_general(lhs, rhs, (((1,), (1,)), ((), ())), preferred_element_type=f32)
-                row = cells[k, 0] >> (columns.bit_length() - 1)
-                place = pl.ds(pl.multiple_of(row * depth, depth), depth)
-                acc_ref[place, :] += both
-        return carry
-
-    lax.fori_loop(0, sources // group, step, 0)
+    for s in range(group):
+        cells = load_ref[s, 8].astype(i32)
+        highs = ((cells & (columns - 1)) >> 7).astype(f32)
+        lows = (cells & (LANES - 1)).astype(f32)
+        for k in range(4):
+            value = jnp.concatenate([load_ref[s, k], load_ref[s, 4 + k]], axis=0)
+            coarse = value.astype(jnp.bfloat16).astype(f32)
+            fine = value - coarse
+            coarse = jnp.concatenate([coarse, coarse], axis=0).astype(jnp.bfloat16)
+            fine = jnp.concatenate([fine, fine], axis=0).astype(jnp.bfloat16)
+            hk = jnp.broadcast_to(highs[k : k + 1], (16, LANES)).astype(jnp.bfloat16)
+            lk = jnp.broadcast_to(lows[k : k + 1], (16, LANES)).astype(jnp.bfloat16)
+            lk = jnp.concatenate([lk] * (LANES // 16), axis=0)
+            left = []
+            right = []
+            for p in pattern:
+                hit = hk == p
+                left.append(jnp.where(hit, coarse, zero16))
+                right.append(jnp.where(hit, fine, zero16))
+            lhs = jnp.concatenate([jnp.concatenate(left, axis=0), jnp.concatenate(right, axis=0)], axis=1)
+            onehot = jnp.where(lk == low_iota, one, zero)
+            rhs = jnp.concatenate([onehot, onehot], axis=1)
+            both = lax.dot_general(lhs, rhs, (((1,), (1,)), ((), ())), preferred_element_type=f32)
+            row = cells[k, 0] >> (columns.bit_length() - 1)
+            place = pl.ds(pl.multiple_of(row * depth, depth), depth)
+            acc_ref[place, :] += both
 
     def turn(i, carry):
         r = pl.multiple_of(i * 8, 8)
@@ -141,24 +138,30 @@
                 ref[f % 4, pl.ds(r, 8), h * LANES : (h + 1) * LANES] = piece[f]
         return carry
 
-    lax.fori_loop(0, rows // 8, turn, 0)
-    south_ref[...] = winds_ref[:, 0:EDGE, :]
-    north_ref[...] = winds_ref[:, rows - EDGE : rows, :]
+    @pl.when(pl.program_id(0) == pl.num_programs(0) - 1)
+    def _():
+        lax.fori_loop(0, rows // 8, turn, 0)
+        south_ref[...] = winds_ref[:, 0:EDGE, :]
+        north_ref[...] = winds_ref[:, rows - EDGE : rows, :]
+
 
 def spread(load, rows, columns):
     depth = 8 * columns // LANES
-    group = 8 if load.shape[0] % 8 == 0 else 1
+    sources = load.shape[0]
+    group = 16 if sources % 16 == 0 else 1
+    outs = [
+        jax.ShapeDtypeStruct((4, rows, columns), f32),
+        jax.ShapeDtypeStruct((4, rows, columns), f32),
+        jax.ShapeDtypeStruct((4, EDGE, columns), f32),
+        jax.ShapeDtypeStruct((4, EDGE, columns), f32),
+    ]
     return pl.pallas_call(
         functools.partial(spread_kernel, group=group),
         name="spread_all",
-        in_specs=[VM],
-        out_specs=[VM] * 4,
-        out_shape=[
-            jax.ShapeDtypeStruct((4, rows, columns), f32),
-            jax.ShapeDtypeStruct((4, rows, columns), f32),
-            jax.ShapeDtypeStruct((4, EDGE, columns), f32),
-            jax.ShapeDtypeStruct((4, EDGE, columns), f32),
-        ],
+        grid=(sources // group,),
+        in_specs=[pl.BlockSpec((group, *load.shape[1:]), lambda i: (i, 0, 0, 0))],
+        out_specs=[whole(out) for out in outs],
+        out_shape=outs,
         scratch_shapes=[pltpu.VMEM(((rows + 1) * depth, LANES), f32)],
         compiler_params=params(24),
         cost_estimate=pl.CostEstimate(flops=1 << 30, bytes_accessed=4 << 20, transcendentals=0),
@@ -326,7 +329,7 @@
         out_specs=block,
         out_shape=jax.ShapeDtypeStruct(moved.shape, f32),
         input_output_aliases={4: 0},
-        compiler_params=params(56),
+        compiler_params=params(40),
         cost_estimate=pl.CostEstimate(flops=1 << 20, bytes_accessed=4 << 20, transcendentals=0),
     )(west, east, own_west, own_east, moved)
 
@@ -436,7 +439,7 @@
         out_shape=jax.ShapeDtypeStruct(moved.shape, f32),
         scratch_shapes=[pltpu.VMEM((levels, EDGE, columns), f32)],
         input_output_aliases={6: 0},
-        compiler_params=params(56),
+        compiler_params=params(48),
         cost_estimate=pl.CostEstimate(flops=1 << 24, bytes_accessed=9 << 20, transcendentals=0),
     )(flux, mask, depth, flow, near, own, moved)
 
@@ -591,10 +594,11 @@
     own_south, own_north, own_west, own_east = edges(planes, land_mask, sea_depth, sea_height, transport)
     from_west = to_next(own_east, "tx")
     from_east = to_previous(own_west, "tx")
+    moved = move(land_mask, sea_depth, transport, planes)
+    moved = patch_columns(from_west, from_east, own_west, own_east, moved).reshape(tracers.shape)
+    own_south, own_north, moved = lax.optimization_barrier((own_south, own_north, moved))
     from_south = to_next(own_north, ROWS)
     from_north = to_previous(own_south, ROWS)
-    moved = move(land_mask, sea_depth, transport, planes)
-    moved = patch_columns(from_west, from_east, own_west, own_east, moved).reshape(tracers.shape)
     arrived, moved = lax.optimization_barrier((arrived, moved))
 
     winds, heats, flux_low, flux_high = spread(arrived, rows, columns)

time: 100 us -> 100 us (level)
  starting transfers between devices: 34.8 us -> 44.3 us
  local copies, waits for them, and re-layouts: 5.12 us -> 0.04 us
  waiting for transfers between devices: 4.18 us -> 0.02 us
  Pallas kernels: 54.2 us -> 53.2 us
    ppermute x4, starting transfers between devices: 12.5 us -> 21.3 us  [to_previous(): return lax.ppermute(array, axes, [(i + 1, i) for i in range(ends)])]
    unnamed x28 -> x16, local copies, waits for them, and re-layouts: 5.12 us -> 0.04 us
    all_to_all x1, waiting for transfers between devices: 4.16 us -> 0.01 us  [all_to_all(): return lax.all_to_all(array, EVERY, split_axis=0, concat_axis=0, tiled=True)]
  transfers between devices with their start and end apart: 9 -> 9, of which waited for: 1 -> 0; matrix products, arithmetic and copies ran while one was open for 0% -> 0% of each run, Pallas kernels for 46% -> 46%
where the time goes in v5:
time: 100 us; the launch traced here: 98.4 us
  Pallas kernels  53.2 us (53%)
  starting transfers between devices  44.3 us (44%)
    ppermute x4, starting transfers between devices, to_previous(): return lax.ppermute(array, axes, [(i + 1, i) for i in range(ends)])  21.3 us
    pallas_call x1, Pallas kernels, spread(): pl.pallas_call(functools.partial(spread_kernel, group=group), name='sprea...  14.4 us
    ppermute x4, starting transfers between devices, to_next(): return lax.ppermute(array, axes, [(i, i + 1) for i in range(ends)])  11.9 us
    pallas_call x2, Pallas kernels, solve(): pl.pallas_call(functools.partial(solve_kernel, part=part, parts=parts, ab...  11.5 us
    pallas_call x1, Pallas kernels, move(): pl.pallas_call(functools.partial(move_kernel, per=per), name='tracer_move...  11.3 us
    all_to_all x1, starting transfers between devices, all_to_all(): return lax.all_to_all(array, EVERY, split_axis=0, concat_axis=0, tiled=True)  11 us
    pallas_call x1, Pallas kernels, pack(): pl.pallas_call(functools.partial(pack_kernel, beyond=beyond), name='pack_...  5.69 us
    pallas_call x1, Pallas kernels, edges(): pl.pallas_call(edges_kernel, name='tile_edges', grid=(1,), in_specs=[pl.B...  4.23 us
  transfers between devices with their start and end apart: 9, of which 0 were waited for; matrix products, arithmetic and copies ran while one was open for 0% of the time, Pallas kernels for 46%

profile of v5, /device:TPU:15, one launch (start us, length us, event | category | flops | bytes accessed | tf_op | source)
XLA Modules:
  0.0 98.4 jit_solution(12031261277517295696)
XLA Ops:
  0.6 5.7 %pack_margin.1 = f32[128,9,4,128]{3,2,1,0:T(4,128)} custom-call(s32[256]{0:T(256)} %bitcast.9, f32[8,16384]{1,0:T(8,128)} %flux_ref.1, s32[256,128]{1,0:T(8,128)} %source_ref.1, s32[256,128]{1,0:T(8,128)} %cell_ref.1, f32[256,128]{1,0:T(8,128)} %weight_ref.1), custom_call_target="tpu_custom_call" | custom-call | flops 4194304 | bytes 4194304 | tf_op jit(solution)/shard_map/pack_margin/pallas_call | solution.py:71
  6.3 11.0 %all-to-all-start = ((f32[128,9,4,128]{3,2,1,0:T(4,128)}), f32[128,9,4,128]{3,2,1,0:T(4,128)}, u32[]{:S(2)}, u32[]{:S(2)}) async-start(f32[128,9,4,128]{3,2,1,0:T(4,128)} %pack_margin.1), calls=%async_computation | async-start | bytes 4718592 | tf_op jit(solution)/shard_map/all_to_all | solution.py:568
  17.4 4.2 %tile_edges.1 = (f32[72,1024]{1,0:T(8,128)}, f32[72,1024]{1,0:T(8,128)}, f32[384,128]{1,0:T(8,128)}, f32[384,128]{1,0:T(8,128)}) custom-call(f32[32,64,1024]{2,1,0:T(8,128)} %bitcast.3, f32[32,64,1024]{2,1,0:T(8,128)} %bitcast.4, f32[32,64,1024]{2,1,0:T(8,128)} %bitcast.5, f32[32,64,1024]{2,1,0:T(8,128)} %bitcast.6, s32[64,1024]{1,0:T(8,128)} %mask_ref.4, ...), custom_call_target="tpu_custom_call" | custom-call | flops 1048576 | bytes 6291456 | tf_op jit(solution)/shard_map/tile_edges/pallas_call | solution.py:202
  21.6 1.3 %collective-permute-start = (f32[384,128]{1,0:T(8,128)}, f32[384,128]{1,0:T(8,128)S(1)}, u32[]{:S(2)}, u32[]{:S(2)}) collective-permute-start(f32[384,128]{1,0:T(8,128)} %get-tuple-element.39.own_east_ref), channel_id=1, source_target_pairs={{0,1},{1,2},{2,3},{3,4},{4,5},{5,6},{6,7},{8,9},{9,10},{10,11},{11... | collective-permute-start | bytes 589832 | tf_op jit(solution)/shard_map/ppermute | solution.py:559
  22.9 0.0 copy-start.6
  22.9 0.0 copy-start.7
  22.9 3.2 %collective-permute-start.1 = (f32[384,128]{1,0:T(8,128)}, f32[384,128]{1,0:T(8,128)S(1)}, u32[]{:S(2)}, u32[]{:S(2)}) collective-permute-start(f32[384,128]{1,0:T(8,128)} %get-tuple-element.40.own_west_ref), channel_id=1, source_target_pairs={{1,0},{2,1},{3,2},{4,3},{5,4},{6,5},{7,6},{9,8},{10,9},{11,10},{12... | collective-permute-start | bytes 589832 | tf_op jit(solution)/shard_map/ppermute | solution.py:564
  26.1 11.3 %tracer_move.1.moved_ref = f32[32,64,1024]{2,1,0:T(8,128)} custom-call(s32[64,1024]{1,0:T(8,128)} %mask_ref.4, f32[64,1024]{1,0:T(8,128)} %depth_ref.4, f32[2,64,1024]{2,1,0:T(8,128)} %stream_ref, f32[32,64,1024]{2,1,0:T(8,128)} %bitcast.7), custom_call_target="tpu_custom_call" | custom-call | flops 33554432 | bytes 18874368 | tf_op jit(solution)/shard_map/tracer_move/pallas_call | solution.py:276
  37.4 0.0 copy-start.4
  37.4 0.0 copy-start.5
  37.4 0.0 copy-start
  37.4 0.0 copy-start.1
  37.4 0.0 copy-start.2
  37.5 0.0 collective-permute-done.west_ref.left_ref
  37.5 0.0 collective-permute-done.1.east_ref.right_ref
  37.5 0.0 copy-done.6
  37.5 0.0 copy-done.7
  37.5 3.4 %patch_columns.1 = f32[32,64,1024]{2,1,0:T(8,128)} custom-call(f32[384,128]{1,0:T(8,128)S(1)} %collective-permute-done.west_ref.left_ref, f32[384,128]{1,0:T(8,128)S(1)} %collective-permute-done.1.east_ref.right_ref, f32[384,128]{1,0:T(8,128)S(1)} %copy-done.6, f32[384,128]{1,0:T(8,128)S(1)} %copy-done.7, ...), custom_call_target="tpu_custom_call", output_to_operand_aliasing={{}: (4, {})} | custom-call | flops 1048576 | bytes 4194304 | tf_op jit(solution)/shard_map/patch_columns/pallas_call | solution.py:324
  40.9 0.0 copy-done.4
  40.9 5.1 %collective-permute-start.2 = (f32[72,1024]{1,0:T(8,128)S(1)}, f32[72,1024]{1,0:T(8,128)S(1)}, u32[]{:S(2)}, u32[]{:S(2)}) collective-permute-start(f32[72,1024]{1,0:T(8,128)S(1)} %copy-done.4), channel_id=1, source_target_pairs={{0,8},{8,16},{16,24},{24,32},{32,40},{40,48},{48,56},{56,64},{64,7... | collective-permute-start | bytes 884744 | tf_op jit(solution)/shard_map/ppermute | solution.py:559
  46.0 0.0 copy-done.5
  46.0 2.6 %collective-permute-start.3 = (f32[72,1024]{1,0:T(8,128)S(1)}, f32[72,1024]{1,0:T(8,128)S(1)}, u32[]{:S(2)}, u32[]{:S(2)}) collective-permute-start(f32[72,1024]{1,0:T(8,128)S(1)} %copy-done.5), channel_id=1, source_target_pairs={{8,0},{16,8},{24,16},{32,24},{40,32},{48,40},{56,48},{64,56},{72,6... | collective-permute-start | bytes 884744 | tf_op jit(solution)/shard_map/ppermute | solution.py:564
  48.6 0.0 all-to-all-done.load_ref
  48.6 14.4 %spread_all.1 = (f32[4,64,1024]{2,1,0:T(8,128)S(1)}, f32[4,64,1024]{2,1,0:T(8,128)S(1)}, f32[4,8,1024]{2,1,0:T(8,128)S(1)}, f32[4,8,1024]{2,1,0:T(8,128)S(1)}) custom-call(f32[128,9,4,128]{3,2,1,0:T(4,128)} %all-to-all-done.load_ref), custom_call_target="tpu_custom_call" | custom-call | flops 1073741824 | bytes 4194304 | tf_op jit(solution)/shard_map/spread_all/pallas_call | solution.py:158
  63.0 4.2 %collective-permute-start.4 = (f32[4,8,1024]{2,1,0:T(8,128)S(1)}, f32[4,8,1024]{2,1,0:T(8,128)S(1)}, u32[]{:S(2)}, u32[]{:S(2)}) collective-permute-start(f32[4,8,1024]{2,1,0:T(8,128)S(1)} %get-tuple-element.47), channel_id=1, source_target_pairs={{0,8},{8,16},{16,24},{24,32},{32,40},{40,48},{48,56},{56,64},{64,7... | collective-permute-start | bytes 393224 | tf_op jit(solution)/shard_map/ppermute | solution.py:559
  67.2 3.4 %collective-permute-start.5 = (f32[4,8,1024]{2,1,0:T(8,128)S(1)}, f32[4,8,1024]{2,1,0:T(8,128)S(1)}, u32[]{:S(2)}, u32[]{:S(2)}) collective-permute-start(f32[4,8,1024]{2,1,0:T(8,128)S(1)} %get-tuple-element.48), channel_id=1, source_target_pairs={{8,0},{16,8},{24,16},{32,24},{40,32},{48,40},{56,48},{64,56},{72,6... | collective-permute-start | bytes 393224 | tf_op jit(solution)/shard_map/ppermute | solution.py:564
  70.7 0.0 collective-permute-done.2.near_ref.low_ref
  70.7 0.0 copy-done
  70.7 0.0 copy-done.1
  70.7 0.0 copy-done.2
  70.7 5.7 %column_solve_0.1.moved_ref = f32[2,16,64,1024]{3,2,1,0:T(8,128)} custom-call(f32[4,64,1024]{2,1,0:T(8,128)S(1)} %get-tuple-element.49.flux_ref, s32[64,1024]{1,0:T(8,128)S(1)} %copy-done.1, f32[64,1024]{1,0:T(8,128)S(1)} %copy-done.2, f32[2,64,1024]{2,1,0:T(8,128)S(1)} %copy-done, ...), custom_call_target="tpu_custom_call", output_to_operand_aliasing={{}: (6, {})} | custom-call | flops 16777216 | bytes 9437184 | tf_op jit(solution)/shard_map/column_solve_0/pallas_call | solution.py:425
  76.5 0.0 collective-permute-done.4.south_ref
  76.5 0.0 collective-permute-done.5.north_ref
  76.5 0.0 collective-permute-done.3.high_ref.near_ref
  76.5 1.3 %collective-permute-start.6 = (f32[400,128]{1,0:T(8,128)S(1)}, f32[400,128]{1,0:T(8,128)S(1)}, u32[]{:S(2)}, u32[]{:S(2)}) collective-permute-start(f32[400,128]{1,0:T(8,128)S(1)} %get-tuple-element.53), channel_id=1, source_target_pairs={{0,1},{1,2},{2,3},{3,4},{4,5},{5,6},{6,7},{8,9},{9,10},{10,11},{11... | collective-permute-start | bytes 614408 | tf_op jit(solution)/shard_map/ppermute | solution.py:559
  77.8 0.0 copy-start.3
  77.8 12.1 %collective-permute-start.7 = (f32[400,128]{1,0:T(8,128)S(1)}, f32[400,128]{1,0:T(8,128)S(1)}, u32[]{:S(2)}, u32[]{:S(2)}) collective-permute-start(f32[400,128]{1,0:T(8,128)S(1)} %get-tuple-element.54), channel_id=1, source_target_pairs={{1,0},{2,1},{3,2},{4,3},{5,4},{6,5},{7,6},{9,8},{10,9},{11,10},{12... | collective-permute-start | bytes 614408 | tf_op jit(solution)/shard_map/ppermute | solution.py:564
  90.0 5.7 %column_solve_1.1 = f32[2,16,64,1024]{3,2,1,0:T(8,128)} custom-call(f32[4,64,1024]{2,1,0:T(8,128)S(1)} %get-tuple-element.49.flux_ref, s32[64,1024]{1,0:T(8,128)S(1)} %copy-done.1, f32[64,1024]{1,0:T(8,128)S(1)} %copy-done.2, f32[2,64,1024]{2,1,0:T(8,128)S(1)} %copy-done, ...), custom_call_target="tpu_custom_call", output_to_operand_aliasing={{}: (6, {})} | custom-call | flops 16777216 | bytes 9437184 | tf_op jit(solution)/shard_map/column_solve_1/pallas_call | solution.py:425
  95.7 0.0 collective-permute-done.6.west_ref
  95.7 0.0 collective-permute-done.7.east_ref
  95.7 0.0 copy-done.3
  95.7 2.7 %barotropic.1 = (f32[64,1024]{1,0:T(8,128)}, f32[2,64,1024]{2,1,0:T(8,128)}) custom-call(s32[64,1024]{1,0:T(8,128)S(1)} %copy-done.1, f32[64,1024]{1,0:T(8,128)S(1)} %copy-done.2, f32[64,1024]{1,0:T(8,128)S(1)} %copy-done.3, f32[2,64,1024]{2,1,0:T(8,128)S(1)} %copy-done, f32[72,1024]{1,0:T(8,128)S(1)} %collective-permute-done.2.near_ref.low_ref, ...), custom_call_target="tpu_custom_call" | custom-call | flops 16777216 | bytes 6291456 | tf_op jit(solution)/shard_map/barotropic/pallas_call | solution.py:544
  (1 shorter events, 0.0 us)
Async XLA Ops:
  6.3 42.3 %all-to-all-start = ((f32[128,9,4,128]{3,2,1,0:T(4,128)}), f32[128,9,4,128]{3,2,1,0:T(4,128)}, u32[]{:S(2)}, u32[]{:S(2)}) async-start(f32[128,9,4,128]{3,2,1,0:T(4,128)} %pack_margin.1), calls=%async_computation | async-start | bytes 4718592 | tf_op jit(solution)/shard_map/all_to_all | solution.py:568
  21.6 15.9 %collective-permute-start = (f32[384,128]{1,0:T(8,128)}, f32[384,128]{1,0:T(8,128)S(1)}, u32[]{:S(2)}, u32[]{:S(2)}) collective-permute-start(f32[384,128]{1,0:T(8,128)} %get-tuple-element.39.own_east_ref), channel_id=1, source_target_pairs={{0,1},{1,2},{2,3},{3,4},{4,5},{5,6},{6,7},{8,9},{9,10},{10,11},{11... | collective-permute-start | bytes 589832 | tf_op jit(solution)/shard_map/ppermute | solution.py:559
  22.9 14.6 %copy-start.6 = (f32[384,128]{1,0:T(8,128)S(1)}, f32[384,128]{1,0:T(8,128)}, u32[]{:S(2)}) copy-start(f32[384,128]{1,0:T(8,128)} %get-tuple-element.40.own_west_ref) | copy-start | bytes 589828
  22.9 14.6 %copy-start.7 = (f32[384,128]{1,0:T(8,128)S(1)}, f32[384,128]{1,0:T(8,128)}, u32[]{:S(2)}) copy-start(f32[384,128]{1,0:T(8,128)} %get-tuple-element.39.own_east_ref) | copy-start | bytes 589828
  22.9 14.6 %collective-permute-start.1 = (f32[384,128]{1,0:T(8,128)}, f32[384,128]{1,0:T(8,128)S(1)}, u32[]{:S(2)}, u32[]{:S(2)}) collective-permute-start(f32[384,128]{1,0:T(8,128)} %get-tuple-element.40.own_west_ref), channel_id=1, source_target_pairs={{1,0},{2,1},{3,2},{4,3},{5,4},{6,5},{7,6},{9,8},{10,9},{11,10},{12... | collective-permute-start | bytes 589832 | tf_op jit(solution)/shard_map/ppermute | solution.py:564
  37.4 3.5 %copy-start.4 = (f32[72,1024]{1,0:T(8,128)S(1)}, f32[72,1024]{1,0:T(8,128)}, u32[]{:S(2)}) copy-start(f32[72,1024]{1,0:T(8,128)} %get-tuple-element.41.own_ref) | copy-start | bytes 884740
  37.4 8.6 %copy-start.5 = (f32[72,1024]{1,0:T(8,128)S(1)}, f32[72,1024]{1,0:T(8,128)}, u32[]{:S(2)}) copy-start(f32[72,1024]{1,0:T(8,128)} %get-tuple-element.42.own_ref) | copy-start | bytes 884740
  37.4 33.3 %copy-start = (f32[2,64,1024]{2,1,0:T(8,128)S(1)}, f32[2,64,1024]{2,1,0:T(8,128)}, u32[]{:S(2)}) copy-start(f32[2,64,1024]{2,1,0:T(8,128)} %stream_ref) | copy-start | bytes 1572868
  37.4 33.3 %copy-start.1 = (s32[64,1024]{1,0:T(8,128)S(1)}, s32[64,1024]{1,0:T(8,128)}, u32[]{:S(2)}) copy-start(s32[64,1024]{1,0:T(8,128)} %mask_ref.4) | copy-start | bytes 786436
  37.4 33.3 %copy-start.2 = (f32[64,1024]{1,0:T(8,128)S(1)}, f32[64,1024]{1,0:T(8,128)}, u32[]{:S(2)}) copy-start(f32[64,1024]{1,0:T(8,128)} %depth_ref.4) | copy-start | bytes 786436
  40.9 29.8 %collective-permute-start.2 = (f32[72,1024]{1,0:T(8,128)S(1)}, f32[72,1024]{1,0:T(8,128)S(1)}, u32[]{:S(2)}, u32[]{:S(2)}) collective-permute-start(f32[72,1024]{1,0:T(8,128)S(1)} %copy-done.4), channel_id=1, source_target_pairs={{0,8},{8,16},{16,24},{24,32},{32,40},{40,48},{48,56},{56,64},{64,7... | collective-permute-start | bytes 884744 | tf_op jit(solution)/shard_map/ppermute | solution.py:559
  46.0 30.5 %collective-permute-start.3 = (f32[72,1024]{1,0:T(8,128)S(1)}, f32[72,1024]{1,0:T(8,128)S(1)}, u32[]{:S(2)}, u32[]{:S(2)}) collective-permute-start(f32[72,1024]{1,0:T(8,128)S(1)} %copy-done.5), channel_id=1, source_target_pairs={{8,0},{16,8},{24,16},{32,24},{40,32},{48,40},{56,48},{64,56},{72,6... | collective-permute-start | bytes 884744 | tf_op jit(solution)/shard_map/ppermute | solution.py:564
  63.0 13.5 %collective-permute-start.4 = (f32[4,8,1024]{2,1,0:T(8,128)S(1)}, f32[4,8,1024]{2,1,0:T(8,128)S(1)}, u32[]{:S(2)}, u32[]{:S(2)}) collective-permute-start(f32[4,8,1024]{2,1,0:T(8,128)S(1)} %get-tuple-element.47), channel_id=1, source_target_pairs={{0,8},{8,16},{16,24},{24,32},{32,40},{40,48},{48,56},{56,64},{64,7... | collective-permute-start | bytes 393224 | tf_op jit(solution)/shard_map/ppermute | solution.py:559
  67.2 9.2 %collective-permute-start.5 = (f32[4,8,1024]{2,1,0:T(8,128)S(1)}, f32[4,8,1024]{2,1,0:T(8,128)S(1)}, u32[]{:S(2)}, u32[]{:S(2)}) collective-permute-start(f32[4,8,1024]{2,1,0:T(8,128)S(1)} %get-tuple-element.48), channel_id=1, source_target_pairs={{8,0},{16,8},{24,16},{32,24},{40,32},{48,40},{56,48},{64,56},{72,6... | collective-permute-start | bytes 393224 | tf_op jit(solution)/shard_map/ppermute | solution.py:564
  76.5 19.2 %collective-permute-start.6 = (f32[400,128]{1,0:T(8,128)S(1)}, f32[400,128]{1,0:T(8,128)S(1)}, u32[]{:S(2)}, u32[]{:S(2)}) collective-permute-start(f32[400,128]{1,0:T(8,128)S(1)} %get-tuple-element.53), channel_id=1, source_target_pairs={{0,1},{1,2},{2,3},{3,4},{4,5},{5,6},{6,7},{8,9},{9,10},{10,11},{11... | collective-permute-start | bytes 614408 | tf_op jit(solution)/shard_map/ppermute | solution.py:559
  77.8 17.9 %copy-start.3 = (f32[64,1024]{1,0:T(8,128)S(1)}, f32[64,1024]{1,0:T(8,128)}, u32[]{:S(2)}) copy-start(f32[64,1024]{1,0:T(8,128)} %begin_ref) | copy-start | bytes 786436
  77.8 17.9 %collective-permute-start.7 = (f32[400,128]{1,0:T(8,128)S(1)}, f32[400,128]{1,0:T(8,128)S(1)}, u32[]{:S(2)}, u32[]{:S(2)}) collective-permute-start(f32[400,128]{1,0:T(8,128)S(1)} %get-tuple-element.54), channel_id=1, source_target_pairs={{1,0},{2,1},{3,2},{4,3},{5,4},{6,5},{7,6},{9,8},{10,9},{11,10},{12... | collective-permute-start | bytes 614408 | tf_op jit(solution)/shard_map/ppermute | solution.py:564

commit v6 on v5

--- a/solution.py
+++ b/solution.py
@@ -291,53 +291,37 @@
     )(mask, depth, flow, planes)
 
 
-def patch_columns_kernel(west_ref, east_ref, own_west_ref, own_east_ref, moved_ref, out_ref):
-    upper = pl.program_id(0) == 1
-    levels, rows, _ = moved_ref.shape
-    edge = jnp.where(upper, LANES - 1, 0)
-    toward = jnp.where(upper, 1.0, -1.0)
-    lane = lax.broadcasted_iota(i32, (rows, LANES), 1)
-    hit = lane == edge
-
-    def column(field, chosen, low_ref, high_ref):
-        place = slice(field * rows, (field + 1) * rows)
-        value = jnp.where(upper, high_ref[place, :], low_ref[place, :])
-        return jnp.sum(jnp.where(chosen, value, 0.0), axis=1, keepdims=True)
-
-    mask = column(0, hit, own_west_ref, own_east_ref)
-    depth = column(1, hit, own_west_ref, own_east_ref)
-    flow = column(3, hit, own_west_ref, own_east_ref)
-    beyond = column(0, lane == LANES - 1 - edge, west_ref, east_ref)
-    coef = mask * beyond * drift(flow / depth, toward)
-    place = slice(5 * rows, 6 * rows)
-    near = jnp.where(upper, east_ref[place, :], west_ref[place, :])
-    own = jnp.where(upper, own_east_ref[place, :], own_west_ref[place, :])
-    extra = coef * (near - own)
-    for p in range(levels):
-        out_ref[p] = moved_ref[p] + jnp.where(hit, extra[:, p : p + 1], 0.0)
-
-
-def patch_columns(west, east, own_west, own_east, moved):
-    levels, rows, columns = moved.shape
-    last = columns // LANES - 1
-    block = pl.BlockSpec((levels, rows, LANES), lambda i: (0, 0, i * last))
-    return pl.pallas_call(
-        patch_columns_kernel,
-        name="patch_columns",
-        grid=(2,),
-        in_specs=[whole(west), whole(east), whole(own_west), whole(own_east), block],
-        out_specs=block,
-        out_shape=jax.ShapeDtypeStruct(moved.shape, f32),
-        input_output_aliases={4: 0},
-        compiler_params=params(40),
-        cost_estimate=pl.CostEstimate(flops=1 << 20, bytes_accessed=4 << 20, transcendentals=0),
-    )(west, east, own_west, own_east, moved)
-
-
 def solve_kernel(
-    flux_ref, mask_ref, depth_ref, flow_ref, near_ref, own_ref, moved_ref, out_ref, ratio_ref, *, part, parts, absorb, decay
+    flux_ref, mask_ref, depth_ref, flow_ref, near_ref, own_ref, west_ref, east_ref, own_west_ref, own_east_ref, *refs,
+    part, parts, absorb, decay,
 ):
+    moved_ref, out_ref, ratio_ref = refs[0], refs[-2], refs[-1]
     step = pl.program_id(0)
+    levels = moved_ref.shape[1]
+    rows = west_ref.shape[0] // 6
+    columns = mask_ref.shape[1]
+    start = (part * (rows // EDGE // parts) + step) * EDGE
+    lane = lax.broadcasted_iota(i32, (EDGE, LANES), 1)
+    sides = (
+        (west_ref, own_west_ref, 0, -1.0, slice(0, LANES)),
+        (east_ref, own_east_ref, LANES - 1, 1.0, slice(columns - LANES, columns)),
+    )
+    for beyond_ref, inside_ref, edge, toward, lanes in sides:
+
+        def take(ref, field):
+            return ref[pl.ds(pl.multiple_of(field * rows + start, EDGE), EDGE), :]
+
+        there = LANES - 1 - edge
+        land = take(inside_ref, 0)[:, edge : edge + 1] * take(beyond_ref, 0)[:, there : there + 1]
+        speed = take(inside_ref, 3)[:, edge : edge + 1] / take(inside_ref, 1)[:, edge : edge + 1]
+        extra = land * drift(speed, toward) * (take(beyond_ref, 5) - take(inside_ref, 5))
+        for tracer in range(2):
+            for k in range(levels):
+                p = tracer * levels + k
+                moved_ref[tracer, k, :, lanes] = moved_ref[tracer, k, :, lanes] + jnp.where(
+                    lane == edge, extra[:, p : p + 1], 0.0
+                )
+
     at_edge = step == (0 if part == 0 else pl.num_programs(0) - 1)
     run = functools.partial(
         solve_rows, flux_ref, mask_ref, depth_ref, flow_ref, near_ref, own_ref, moved_ref, out_ref, ratio_ref, absorb, decay
@@ -414,7 +398,7 @@
         out_ref[1, k] = salt_last
 
 
-def solve(flux, mask, depth, flow, near, own, moved, part, parts):
+def solve(flux, mask, depth, flow, near, own, margins, moved, done, part, parts):
     count, levels, rows, columns = moved.shape
     depths = np.arange(levels, dtype=np.float64)
     absorb = tuple(float(a) for a in np.exp(-depths / 3.0) - np.exp(-(depths + 1.0) / 3.0))
@@ -422,6 +406,7 @@
     steps = rows // EDGE // parts
     first = part * steps
     line = pl.BlockSpec((EDGE, columns), lambda i: (first + i, 0))
+    block = pl.BlockSpec((count, levels, EDGE, columns), lambda i: (0, 0, first + i, 0))
     return pl.pallas_call(
         functools.partial(solve_kernel, part=part, parts=parts, absorb=absorb, decay=decay),
         name=f"column_solve_{part}",
@@ -433,15 +418,17 @@
             pl.BlockSpec((1, EDGE, columns), lambda i: (1, first + i, 0)),
             whole(near),
             whole(own),
-            pl.BlockSpec((count, levels, EDGE, columns), lambda i: (0, 0, first + i, 0)),
+            *[whole(margin) for margin in margins],
+            block,
+            *[pl.BlockSpec(memory_space=pl.ANY) for _ in done],
         ],
-        out_specs=pl.BlockSpec((count, levels, EDGE, columns), lambda i: (0, 0, first + i, 0)),
+        out_specs=block,
         out_shape=jax.ShapeDtypeStruct(moved.shape, f32),
         scratch_shapes=[pltpu.VMEM((levels, EDGE, columns), f32)],
-        input_output_aliases={6: 0},
-        compiler_params=params(48),
+        input_output_aliases={11: 0} if done else {},
+        compiler_params=params(24),
         cost_estimate=pl.CostEstimate(flops=1 << 24, bytes_accessed=9 << 20, transcendentals=0),
-    )(flux, mask, depth, flow, near, own, moved)
+    )(flux, mask, depth, flow, near, own, *margins, moved, *done)
 
 
 def sides_kernel(left_ref, right_ref, south_ref, north_ref, low_ref, high_ref, west_ref, east_ref):
@@ -595,7 +582,7 @@
     from_west = to_next(own_east, "tx")
     from_east = to_previous(own_west, "tx")
     moved = move(land_mask, sea_depth, transport, planes)
-    moved = patch_columns(from_west, from_east, own_west, own_east, moved).reshape(tracers.shape)
+    moved = moved.reshape(tracers.shape)
     own_south, own_north, moved = lax.optimization_barrier((own_south, own_north, moved))
     from_south = to_next(own_north, ROWS)
     from_north = to_previous(own_south, ROWS)
@@ -604,12 +591,13 @@
     winds, heats, flux_low, flux_high = spread(arrived, rows, columns)
     flux_south = to_next(flux_high, ROWS)
     flux_north = to_previous(flux_low, ROWS)
-    moved = solve(heats, land_mask, sea_depth, transport, from_south, own_south, moved, 0, 2)
-    flux_south, flux_north, moved = lax.optimization_barrier((flux_south, flux_north, moved))
+    margins = (from_west, from_east, own_west, own_east)
+    half = solve(heats, land_mask, sea_depth, transport, from_south, own_south, margins, moved, (), 0, 2)
+    flux_south, flux_north, half = lax.optimization_barrier((flux_south, flux_north, half))
     side_west, side_east = sides(winds, flux_south, flux_north, from_south, from_north)
     flux_west = to_next(side_east, "tx")
     flux_east = to_previous(side_west, "tx")
-    solved = solve(heats, land_mask, sea_depth, transport, from_north, own_north, moved, 1, 2)
+    solved = solve(heats, land_mask, sea_depth, transport, from_north, own_north, margins, moved, (half,), 1, 2)
     flux_west, flux_east, solved = lax.optimization_barrier((flux_west, flux_east, solved))
     new_height, new_transport = barotropic(
         land_mask, sea_depth, sea_height, transport, from_south, from_north, from_west, from_east,

time: 100 us -> 95.2 us (0.952)
  the two profiles are of different devices: /device:TPU:15 before, /device:TPU:37 now
where the time goes in v6:
time: 95.2 us; the launch traced here: 94.6 us
  Pallas kernels  47.7 us (50%)
  starting transfers between devices  39.1 us (41%)
  waiting for transfers between devices  3.45 us (4%)
  local copies, waits for them, and re-layouts  3.42 us (4%)
    ppermute x4, starting transfers between devices, to_next(): return lax.ppermute(array, axes, [(i, i + 1) for i in range(ends)])  15.4 us
    pallas_call x1, Pallas kernels, spread(): pl.pallas_call(functools.partial(spread_kernel, group=group), name='sprea...  14.4 us
    ppermute x4, starting transfers between devices, to_previous(): return lax.ppermute(array, axes, [(i + 1, i) for i in range(ends)])  12.8 us
    pallas_call x1, Pallas kernels, move(): pl.pallas_call(functools.partial(move_kernel, per=per), name='tracer_move...  11.3 us
    all_to_all x1, starting transfers between devices, all_to_all(): return lax.all_to_all(array, EVERY, split_axis=0, concat_axis=0, tiled=True)  10.9 us
    pallas_call x2, Pallas kernels, solve(): pl.pallas_call(functools.partial(solve_kernel, part=part, parts=parts, ab...  9.34 us
    pallas_call x1, Pallas kernels, pack(): pl.pallas_call(functools.partial(pack_kernel, beyond=beyond), name='pack_...  5.7 us
    pallas_call x1, Pallas kernels, edges(): pl.pallas_call(edges_kernel, name='tile_edges', grid=(1,), in_specs=[pl.B...  4.23 us
  transfers between devices with their start and end apart: 9, of which 2 were waited for; matrix products, arithmetic and copies ran while one was open for 0% of the time, Pallas kernels for 42%

profile of v6, /device:TPU:37, one launch (start us, length us, event | category | flops | bytes accessed | tf_op | source)
XLA Modules:
  0.0 94.6 jit_solution(3603976789090506315)
XLA Ops:
  0.6 5.7 %pack_margin.1 = f32[128,9,4,128]{3,2,1,0:T(4,128)} custom-call(s32[256]{0:T(256)} %bitcast.10, f32[8,16384]{1,0:T(8,128)} %flux_ref.1, s32[256,128]{1,0:T(8,128)} %source_ref.1, s32[256,128]{1,0:T(8,128)} %cell_ref.1, f32[256,128]{1,0:T(8,128)} %weight_ref.1), custom_call_target="tpu_custom_call" | custom-call | flops 4194304 | bytes 4194304 | tf_op jit(solution)/shard_map/pack_margin/pallas_call | solution.py:71
  6.3 10.9 %all-to-all-start = ((f32[128,9,4,128]{3,2,1,0:T(4,128)}), f32[128,9,4,128]{3,2,1,0:T(4,128)}, u32[]{:S(2)}, u32[]{:S(2)}) async-start(f32[128,9,4,128]{3,2,1,0:T(4,128)} %pack_margin.1), calls=%async_computation | async-start | bytes 4718592 | tf_op jit(solution)/shard_map/all_to_all | solution.py:555
  17.2 4.2 %tile_edges.1 = (f32[72,1024]{1,0:T(8,128)}, f32[72,1024]{1,0:T(8,128)}, f32[384,128]{1,0:T(8,128)}, f32[384,128]{1,0:T(8,128)}) custom-call(f32[32,64,1024]{2,1,0:T(8,128)} %bitcast.5, f32[32,64,1024]{2,1,0:T(8,128)} %bitcast.6, f32[32,64,1024]{2,1,0:T(8,128)} %bitcast.7, f32[32,64,1024]{2,1,0:T(8,128)} %bitcast.8, s32[64,1024]{1,0:T(8,128)} %mask_ref.4, ...), custom_call_target="tpu_custom_call" | custom-call | flops 1048576 | bytes 6291456 | tf_op jit(solution)/shard_map/tile_edges/pallas_call | solution.py:202
  21.5 0.0 copy-start.7
  21.5 0.0 copy-start.8
  21.5 0.0 copy-start.5
  21.5 0.0 copy-start.1
  21.5 0.0 copy-start.2
  21.5 0.0 copy-start.3
  21.5 0.0 copy-start.6
  21.5 3.2 %collective-permute-start.2 = (f32[384,128]{1,0:T(8,128)}, f32[384,128]{1,0:T(8,128)S(1)}, u32[]{:S(2)}, u32[]{:S(2)}) collective-permute-start(f32[384,128]{1,0:T(8,128)} %get-tuple-element.41.own_east_ref), channel_id=1, source_target_pairs={{0,1},{1,2},{2,3},{3,4},{4,5},{5,6},{6,7},{8,9},{9,10},{10,11},{11... | collective-permute-start | bytes 589832 | tf_op jit(solution)/shard_map/ppermute | solution.py:546
  24.7 11.3 %tracer_move.1 = f32[32,64,1024]{2,1,0:T(8,128)} custom-call(s32[64,1024]{1,0:T(8,128)} %mask_ref.4, f32[64,1024]{1,0:T(8,128)} %depth_ref.4, f32[2,64,1024]{2,1,0:T(8,128)} %stream_ref, f32[32,64,1024]{2,1,0:T(8,128)} %bitcast.9), custom_call_target="tpu_custom_call" | custom-call | flops 33554432 | bytes 18874368 | tf_op jit(solution)/shard_map/tracer_move/pallas_call | solution.py:276
  36.1 0.0 copy-done.7
  36.1 4.2 %collective-permute-start = (f32[72,1024]{1,0:T(8,128)S(1)}, f32[72,1024]{1,0:T(8,128)S(1)}, u32[]{:S(2)}, u32[]{:S(2)}) collective-permute-start(f32[72,1024]{1,0:T(8,128)S(1)} %copy-done.7), channel_id=1, source_target_pairs={{0,8},{8,16},{16,24},{24,32},{32,40},{40,48},{48,56},{56,64},{64,7... | collective-permute-start | bytes 884744 | tf_op jit(solution)/shard_map/ppermute | solution.py:546
  40.3 0.0 copy-done.8
  40.3 3.4 %collective-permute-start.1 = (f32[72,1024]{1,0:T(8,128)S(1)}, f32[72,1024]{1,0:T(8,128)S(1)}, u32[]{:S(2)}, u32[]{:S(2)}) collective-permute-start(f32[72,1024]{1,0:T(8,128)S(1)} %copy-done.8), channel_id=1, source_target_pairs={{8,0},{16,8},{24,16},{32,24},{40,32},{48,40},{56,48},{64,56},{72,6... | collective-permute-start | bytes 884744 | tf_op jit(solution)/shard_map/ppermute | solution.py:551
  43.7 0.0 copy-done.5
  43.7 1.9 %collective-permute-start.3 = (f32[384,128]{1,0:T(8,128)S(1)}, f32[384,128]{1,0:T(8,128)S(1)}, u32[]{:S(2)}, u32[]{:S(2)}) collective-permute-start(f32[384,128]{1,0:T(8,128)S(1)} %copy-done.5), channel_id=1, source_target_pairs={{1,0},{2,1},{3,2},{4,3},{5,4},{6,5},{7,6},{9,8},{10,9},{11,10},{12... | collective-permute-start | bytes 589832 | tf_op jit(solution)/shard_map/ppermute | solution.py:551
  45.6 3.0 %all-to-all-done.load_ref = f32[128,9,4,128]{3,2,1,0:T(4,128)} async-done(((f32[128,9,4,128]{3,2,1,0:T(4,128)}), f32[128,9,4,128]{3,2,1,0:T(4,128)}, u32[]{:S(2)}, u32[]{:S(2)}) %all-to-all-start) | async-done | bytes 2359328 | tf_op jit(solution)/shard_map/all_to_all | solution.py:555
  48.6 14.4 %spread_all.1 = (f32[4,64,1024]{2,1,0:T(8,128)S(1)}, f32[4,64,1024]{2,1,0:T(8,128)S(1)}, f32[4,8,1024]{2,1,0:T(8,128)S(1)}, f32[4,8,1024]{2,1,0:T(8,128)S(1)}) custom-call(f32[128,9,4,128]{3,2,1,0:T(4,128)} %all-to-all-done.load_ref), custom_call_target="tpu_custom_call" | custom-call | flops 1073741824 | bytes 4194304 | tf_op jit(solution)/shard_map/spread_all/pallas_call | solution.py:158
  63.0 1.9 %collective-permute-start.4 = (f32[4,8,1024]{2,1,0:T(8,128)S(1)}, f32[4,8,1024]{2,1,0:T(8,128)S(1)}, u32[]{:S(2)}, u32[]{:S(2)}) collective-permute-start(f32[4,8,1024]{2,1,0:T(8,128)S(1)} %get-tuple-element.47), channel_id=1, source_target_pairs={{0,8},{8,16},{16,24},{24,32},{32,40},{40,48},{48,56},{56,64},{64,7... | collective-permute-start | bytes 393224 | tf_op jit(solution)/shard_map/ppermute | solution.py:546
  64.9 0.0 collective-permute-done.2.west_ref.left_ref
  64.9 5.5 %collective-permute-start.5 = (f32[4,8,1024]{2,1,0:T(8,128)S(1)}, f32[4,8,1024]{2,1,0:T(8,128)S(1)}, u32[]{:S(2)}, u32[]{:S(2)}) collective-permute-start(f32[4,8,1024]{2,1,0:T(8,128)S(1)} %get-tuple-element.48), channel_id=1, source_target_pairs={{8,0},{16,8},{24,16},{32,24},{40,32},{48,40},{56,48},{64,56},{72,6... | collective-permute-start | bytes 393224 | tf_op jit(solution)/shard_map/ppermute | solution.py:551
  70.4 0.0 collective-permute-done.3.east_ref.right_ref
  70.4 0.0 collective-permute-done.near_ref.low_ref
  70.4 0.0 copy-done.1
  70.4 0.0 copy-done.2
  70.4 0.0 copy-done.3
  70.4 0.0 copy-done.6
  70.5 0.0 copy-start
  70.5 3.4 %copy-done = f32[32,64,1024]{2,1,0:T(8,128)S(1)} copy-done((f32[32,64,1024]{2,1,0:T(8,128)S(1)}, f32[32,64,1024]{2,1,0:T(8,128)}, u32[]{:S(2)}) %copy-start) | copy-done | bytes 8388632
  73.8 4.7 %column_solve_0.1.refs_1_ = f32[2,16,64,1024]{3,2,1,0:T(8,128)} custom-call(f32[4,64,1024]{2,1,0:T(8,128)S(1)} %get-tuple-element.49.flux_ref, s32[64,1024]{1,0:T(8,128)S(1)} %copy-done.2, f32[64,1024]{1,0:T(8,128)S(1)} %copy-done.3, f32[2,64,1024]{2,1,0:T(8,128)S(1)} %copy-done.1, f32[72,1024]{1,0:T(8,128)S(1)} %collective-permute-done.near_ref.low_ref, ...), custom_call_target="tpu_custom_call" | custom-call | flops 16777216 | bytes 9437184 | tf_op jit(solution)/shard_map/column_solve_0/pallas_call | solution.py:410
  78.5 0.0 collective-permute-done.4.south_ref
  78.5 0.0 collective-permute-done.5.north_ref
  78.5 0.0 collective-permute-done.1.high_ref.near_ref
  78.6 6.1 %collective-permute-start.6 = (f32[400,128]{1,0:T(8,128)S(1)}, f32[400,128]{1,0:T(8,128)S(1)}, u32[]{:S(2)}, u32[]{:S(2)}) collective-permute-start(f32[400,128]{1,0:T(8,128)S(1)} %get-tuple-element.53), channel_id=1, source_target_pairs={{0,1},{1,2},{2,3},{3,4},{4,5},{5,6},{6,7},{8,9},{9,10},{10,11},{11... | collective-permute-start | bytes 614408 | tf_op jit(solution)/shard_map/ppermute | solution.py:546
  84.6 0.0 copy-start.4
  84.6 2.1 %collective-permute-start.7 = (f32[400,128]{1,0:T(8,128)S(1)}, f32[400,128]{1,0:T(8,128)S(1)}, u32[]{:S(2)}, u32[]{:S(2)}) collective-permute-start(f32[400,128]{1,0:T(8,128)S(1)} %get-tuple-element.54), channel_id=1, source_target_pairs={{1,0},{2,1},{3,2},{4,3},{5,4},{6,5},{7,6},{9,8},{10,9},{11,10},{12... | collective-permute-start | bytes 614408 | tf_op jit(solution)/shard_map/ppermute | solution.py:551
  86.7 4.7 %column_solve_1.1 = f32[2,16,64,1024]{3,2,1,0:T(8,128)} custom-call(f32[4,64,1024]{2,1,0:T(8,128)S(1)} %get-tuple-element.49.flux_ref, s32[64,1024]{1,0:T(8,128)S(1)} %copy-done.2, f32[64,1024]{1,0:T(8,128)S(1)} %copy-done.3, f32[2,64,1024]{2,1,0:T(8,128)S(1)} %copy-done.1, ...), custom_call_target="tpu_custom_call", output_to_operand_aliasing={{}: (11, {})} | custom-call | flops 16777216 | bytes 9437184 | tf_op jit(solution)/shard_map/column_solve_1/pallas_call | solution.py:410
  91.4 0.0 collective-permute-done.6.west_ref
  91.4 0.5 collective-permute-done.7.east_ref
  91.8 0.0 copy-done.4
  91.8 2.7 %barotropic.1 = (f32[64,1024]{1,0:T(8,128)}, f32[2,64,1024]{2,1,0:T(8,128)}) custom-call(s32[64,1024]{1,0:T(8,128)S(1)} %copy-done.2, f32[64,1024]{1,0:T(8,128)S(1)} %copy-done.3, f32[64,1024]{1,0:T(8,128)S(1)} %copy-done.4, f32[2,64,1024]{2,1,0:T(8,128)S(1)} %copy-done.1, f32[72,1024]{1,0:T(8,128)S(1)} %collective-permute-done.near_ref.low_ref, ...), custom_call_target="tpu_custom_call" | custom-call | flops 16777216 | bytes 6291456 | tf_op jit(solution)/shard_map/barotropic/pallas_call | solution.py:531
  (1 shorter events, 0.0 us)
Async XLA Ops:
  6.3 42.2 %all-to-all-start = ((f32[128,9,4,128]{3,2,1,0:T(4,128)}), f32[128,9,4,128]{3,2,1,0:T(4,128)}, u32[]{:S(2)}, u32[]{:S(2)}) async-start(f32[128,9,4,128]{3,2,1,0:T(4,128)} %pack_margin.1), calls=%async_computation | async-start | bytes 4718592 | tf_op jit(solution)/shard_map/all_to_all | solution.py:555
  21.5 14.6 %copy-start.7 = (f32[72,1024]{1,0:T(8,128)S(1)}, f32[72,1024]{1,0:T(8,128)}, u32[]{:S(2)}) copy-start(f32[72,1024]{1,0:T(8,128)} %get-tuple-element.39.own_ref) | copy-start | bytes 884740
  21.5 18.8 %copy-start.8 = (f32[72,1024]{1,0:T(8,128)S(1)}, f32[72,1024]{1,0:T(8,128)}, u32[]{:S(2)}) copy-start(f32[72,1024]{1,0:T(8,128)} %get-tuple-element.40.own_ref) | copy-start | bytes 884740
  21.5 22.2 %copy-start.5 = (f32[384,128]{1,0:T(8,128)S(1)}, f32[384,128]{1,0:T(8,128)}, u32[]{:S(2)}) copy-start(f32[384,128]{1,0:T(8,128)} %get-tuple-element.42.own_west_ref) | copy-start | bytes 589828
  21.5 48.9 %copy-start.1 = (f32[2,64,1024]{2,1,0:T(8,128)S(1)}, f32[2,64,1024]{2,1,0:T(8,128)}, u32[]{:S(2)}) copy-start(f32[2,64,1024]{2,1,0:T(8,128)} %stream_ref) | copy-start | bytes 1572868
  21.5 48.9 %copy-start.2 = (s32[64,1024]{1,0:T(8,128)S(1)}, s32[64,1024]{1,0:T(8,128)}, u32[]{:S(2)}) copy-start(s32[64,1024]{1,0:T(8,128)} %mask_ref.4) | copy-start | bytes 786436
  21.5 48.9 %copy-start.3 = (f32[64,1024]{1,0:T(8,128)S(1)}, f32[64,1024]{1,0:T(8,128)}, u32[]{:S(2)}) copy-start(f32[64,1024]{1,0:T(8,128)} %depth_ref.4) | copy-start | bytes 786436
  21.5 48.9 %copy-start.6 = (f32[384,128]{1,0:T(8,128)S(1)}, f32[384,128]{1,0:T(8,128)}, u32[]{:S(2)}) copy-start(f32[384,128]{1,0:T(8,128)} %get-tuple-element.41.own_east_ref) | copy-start | bytes 589828
  21.5 43.4 %collective-permute-start.2 = (f32[384,128]{1,0:T(8,128)}, f32[384,128]{1,0:T(8,128)S(1)}, u32[]{:S(2)}, u32[]{:S(2)}) collective-permute-start(f32[384,128]{1,0:T(8,128)} %get-tuple-element.41.own_east_ref), channel_id=1, source_target_pairs={{0,1},{1,2},{2,3},{3,4},{4,5},{5,6},{6,7},{8,9},{9,10},{10,11},{11... | collective-permute-start | bytes 589832 | tf_op jit(solution)/shard_map/ppermute | solution.py:546
  36.1 34.3 %collective-permute-start = (f32[72,1024]{1,0:T(8,128)S(1)}, f32[72,1024]{1,0:T(8,128)S(1)}, u32[]{:S(2)}, u32[]{:S(2)}) collective-permute-start(f32[72,1024]{1,0:T(8,128)S(1)} %copy-done.7), channel_id=1, source_target_pairs={{0,8},{8,16},{16,24},{24,32},{32,40},{40,48},{48,56},{56,64},{64,7... | collective-permute-start | bytes 884744 | tf_op jit(solution)/shard_map/ppermute | solution.py:546
  40.3 38.2 %collective-permute-start.1 = (f32[72,1024]{1,0:T(8,128)S(1)}, f32[72,1024]{1,0:T(8,128)S(1)}, u32[]{:S(2)}, u32[]{:S(2)}) collective-permute-start(f32[72,1024]{1,0:T(8,128)S(1)} %copy-done.8), channel_id=1, source_target_pairs={{8,0},{16,8},{24,16},{32,24},{40,32},{48,40},{56,48},{64,56},{72,6... | collective-permute-start | bytes 884744 | tf_op jit(solution)/shard_map/ppermute | solution.py:551
  43.7 26.7 %collective-permute-start.3 = (f32[384,128]{1,0:T(8,128)S(1)}, f32[384,128]{1,0:T(8,128)S(1)}, u32[]{:S(2)}, u32[]{:S(2)}) collective-permute-start(f32[384,128]{1,0:T(8,128)S(1)} %copy-done.5), channel_id=1, source_target_pairs={{1,0},{2,1},{3,2},{4,3},{5,4},{6,5},{7,6},{9,8},{10,9},{11,10},{12... | collective-permute-start | bytes 589832 | tf_op jit(solution)/shard_map/ppermute | solution.py:551
  63.0 15.5 %collective-permute-start.4 = (f32[4,8,1024]{2,1,0:T(8,128)S(1)}, f32[4,8,1024]{2,1,0:T(8,128)S(1)}, u32[]{:S(2)}, u32[]{:S(2)}) collective-permute-start(f32[4,8,1024]{2,1,0:T(8,128)S(1)} %get-tuple-element.47), channel_id=1, source_target_pairs={{0,8},{8,16},{16,24},{24,32},{32,40},{40,48},{48,56},{56,64},{64,7... | collective-permute-start | bytes 393224 | tf_op jit(solution)/shard_map/ppermute | solution.py:546
  64.9 13.6 %collective-permute-start.5 = (f32[4,8,1024]{2,1,0:T(8,128)S(1)}, f32[4,8,1024]{2,1,0:T(8,128)S(1)}, u32[]{:S(2)}, u32[]{:S(2)}) collective-permute-start(f32[4,8,1024]{2,1,0:T(8,128)S(1)} %get-tuple-element.48), channel_id=1, source_target_pairs={{8,0},{16,8},{24,16},{32,24},{40,32},{48,40},{56,48},{64,56},{72,6... | collective-permute-start | bytes 393224 | tf_op jit(solution)/shard_map/ppermute | solution.py:551
  70.5 3.4 %copy-start = (f32[32,64,1024]{2,1,0:T(8,128)S(1)}, f32[32,64,1024]{2,1,0:T(8,128)}, u32[]{:S(2)}) copy-start(f32[32,64,1024]{2,1,0:T(8,128)} %tracer_move.1) | copy-start | bytes 25165828
  78.6 12.8 %collective-permute-start.6 = (f32[400,128]{1,0:T(8,128)S(1)}, f32[400,128]{1,0:T(8,128)S(1)}, u32[]{:S(2)}, u32[]{:S(2)}) collective-permute-start(f32[400,128]{1,0:T(8,128)S(1)} %get-tuple-element.53), channel_id=1, source_target_pairs={{0,1},{1,2},{2,3},{3,4},{4,5},{5,6},{6,7},{8,9},{9,10},{10,11},{11... | collective-permute-start | bytes 614408 | tf_op jit(solution)/shard_map/ppermute | solution.py:546
  84.6 7.2 %copy-start.4 = (f32[64,1024]{1,0:T(8,128)S(1)}, f32[64,1024]{1,0:T(8,128)}, u32[]{:S(2)}) copy-start(f32[64,1024]{1,0:T(8,128)} %begin_ref) | copy-start | bytes 786436
  84.6 7.2 %collective-permute-start.7 = (f32[400,128]{1,0:T(8,128)S(1)}, f32[400,128]{1,0:T(8,128)S(1)}, u32[]{:S(2)}, u32[]{:S(2)}) collective-permute-start(f32[400,128]{1,0:T(8,128)S(1)} %get-tuple-element.54), channel_id=1, source_target_pairs={{1,0},{2,1},{3,2},{4,3},{5,4},{6,5},{7,6},{9,8},{10,9},{11,10},{12... | collective-permute-start | bytes 614408 | tf_op jit(solution)/shard_map/ppermute | solution.py:551

commit v7 on v6

--- a/solution.py
+++ b/solution.py
@@ -38,7 +38,11 @@
         out_ref[t, 8] = nowhere
         return carry
 
-    lax.fori_loop(0, tiles, clear, 0, unroll=True)
+    @pl.when(pl.program_id(0) == 0)
+    def _():
+        lax.fori_loop(0, tiles, clear, 0, unroll=True)
+
+    begin = pl.program_id(0) * blocks
     sub = lax.broadcasted_iota(i32, (8, LANES), 0)
 
     def step(i, carry):
@@ -53,7 +57,7 @@
             y = jnp.where(sub == 3, 0.1 * (six - five), y)
             for half in range(2):
                 b = 2 * w + half
-                tile = tile_ref[b]
+                tile = tile_ref[begin + b]
                 slot = count_ref[tile]
                 count_ref[tile] = slot + 1
                 index = jnp.broadcast_to(source_ref[pl.ds(b, 1), :], (8, LANES))
@@ -68,11 +72,14 @@
 
 
 def pack(tile, flux, source, cell, weight, tiles, beyond):
+    blocks = source.shape[0]
+    steps = 4 if blocks % 32 == 0 else 1
+    line = pl.BlockSpec((blocks // steps, LANES), lambda i: (i, 0))
     return pl.pallas_call(
         functools.partial(pack_kernel, beyond=beyond),
         name="pack_margin",
-        grid=(1,),
-        in_specs=[SM, whole(flux), whole(source), whole(cell), whole(weight)],
+        grid=(steps,),
+        in_specs=[SM, pl.BlockSpec((8, flux.shape[1] // steps), lambda i: (0, i)), line, line, line],
         out_specs=pl.BlockSpec((tiles, 9, 4, LANES), lambda i: (0, 0, 0, 0)),
         out_shape=jax.ShapeDtypeStruct((tiles, 9, 4, LANES), f32),
         scratch_shapes=[pltpu.SMEM((tiles,), i32)],
@@ -81,7 +88,7 @@
     )(tile, flux, source, cell, weight)
 
 
-def spread_kernel(load_ref, winds_ref, heats_ref, south_ref, north_ref, acc_ref, *, group):
+def spread_kernel(cells_ref, load_ref, winds_ref, heats_ref, south_ref, north_ref, acc_ref, turned_ref, *, group):
     _, rows, columns = winds_ref.shape
     fields = 8
     high = columns // LANES
@@ -92,8 +99,19 @@
     @pl.when(pl.program_id(0) == 0)
     def _():
         lax.fori_loop(0, rows * depth // 256, clear, 0)
-
-    low_iota = lax.broadcasted_iota(i32, (LANES, LANES), 0).astype(f32).astype(jnp.bfloat16)
+        per = 4 * group
+        chunk = min(cells_ref.shape[0], LANES // 4)
+        for i in range(0, cells_ref.shape[0], chunk):
+            cells = cells_ref[i : i + chunk, 0].reshape(4 * chunk, LANES)
+            if chunk < LANES // 4:
+                cells = jnp.concatenate([cells] * (LANES // (4 * chunk)), axis=0)
+            columns_of = (cells.astype(i32) & (LANES - 1)).astype(f32).T
+            for n in range(4 * chunk // per):
+                part = columns_of if n == 0 else pltpu.roll(columns_of, LANES - n * per, 1)
+                turned_ref[i // group + n] = part
+
+    step = pl.program_id(0)
+    low_iota = lax.broadcasted_iota(i32, (LANES, LANES), 1).astype(f32).astype(jnp.bfloat16)
     pattern = [
         (2 * i + (lax.broadcasted_iota(i32, (16, LANES), 0) >> 3)).astype(f32).astype(jnp.bfloat16) for i in range(high // 2)
     ]
@@ -104,7 +122,6 @@
     for s in range(group):
         cells = load_ref[s, 8].astype(i32)
         highs = ((cells & (columns - 1)) >> 7).astype(f32)
-        lows = (cells & (LANES - 1)).astype(f32)
         for k in range(4):
             value = jnp.concatenate([load_ref[s, k], load_ref[s, 4 + k]], axis=0)
             coarse = value.astype(jnp.bfloat16).astype(f32)
@@ -112,8 +129,8 @@
             coarse = jnp.concatenate([coarse, coarse], axis=0).astype(jnp.bfloat16)
             fine = jnp.concatenate([fine, fine], axis=0).astype(jnp.bfloat16)
             hk = jnp.broadcast_to(highs[k : k + 1], (16, LANES)).astype(jnp.bfloat16)
-            lk = jnp.broadcast_to(lows[k : k + 1], (16, LANES)).astype(jnp.bfloat16)
-            lk = jnp.concatenate([lk] * (LANES // 16), axis=0)
+            c = 4 * s + k
+            lk = jnp.broadcast_to(turned_ref[step, :, c : c + 1], (LANES, LANES)).astype(jnp.bfloat16)
             left = []
             right = []
             for p in pattern:
@@ -122,8 +139,8 @@
                 right.append(jnp.where(hit, fine, zero16))
             lhs = jnp.concatenate([jnp.concatenate(left, axis=0), jnp.concatenate(right, axis=0)], axis=1)
             onehot = jnp.where(lk == low_iota, one, zero)
-            rhs = jnp.concatenate([onehot, onehot], axis=1)
-            both = lax.dot_general(lhs, rhs, (((1,), (1,)), ((), ())), preferred_element_type=f32)
+            rhs = jnp.concatenate([onehot, onehot], axis=0)
+            both = lax.dot_general(lhs, rhs, (((1,), (0,)), ((), ())), preferred_element_type=f32)
             row = cells[k, 0] >> (columns.bit_length() - 1)
             place = pl.ds(pl.multiple_of(row * depth, depth), depth)
             acc_ref[place, :] += both
@@ -159,13 +176,19 @@
         functools.partial(spread_kernel, group=group),
         name="spread_all",
         grid=(sources // group,),
-        in_specs=[pl.BlockSpec((group, *load.shape[1:]), lambda i: (i, 0, 0, 0))],
+        in_specs=[
+            pl.BlockSpec((sources, 1, 4, LANES), lambda i: (0, 8, 0, 0)),
+            pl.BlockSpec((group, *load.shape[1:]), lambda i: (i, 0, 0, 0)),
+        ],
         out_specs=[whole(out) for out in outs],
         out_shape=outs,
-        scratch_shapes=[pltpu.VMEM(((rows + 1) * depth, LANES), f32)],
+        scratch_shapes=[
+            pltpu.VMEM(((rows + 1) * depth, LANES), f32),
+            pltpu.VMEM((sources // group, LANES, LANES), f32),
+        ],
         compiler_params=params(24),
         cost_estimate=pl.CostEstimate(flops=1 << 30, bytes_accessed=4 << 20, transcendentals=0),
-    )(load)
+    )(load, load)
 
 
 def edges_kernel(
@@ -426,7 +449,7 @@
         out_shape=jax.ShapeDtypeStruct(moved.shape, f32),
         scratch_shapes=[pltpu.VMEM((levels, EDGE, columns), f32)],
         input_output_aliases={11: 0} if done else {},
-        compiler_params=params(24),
+        compiler_params=params(48),
         cost_estimate=pl.CostEstimate(flops=1 << 24, bytes_accessed=9 << 20, transcendentals=0),
     )(flux, mask, depth, flow, near, own, *margins, moved, *done)
 

time: 95.2 us -> 95.4 us (level)
  the two profiles are of different devices: /device:TPU:37 before, /device:TPU:15 now
where the time goes in v7:
time: 95.4 us; the launch traced here: 94.6 us
  Pallas kernels  49 us (51%)
  starting transfers between devices  36.2 us (38%)
  waiting for transfers between devices  7.67 us (8%)
    ppermute x4, starting transfers between devices, to_previous(): return lax.ppermute(array, axes, [(i + 1, i) for i in range(ends)])  13.9 us
    pallas_call x2, Pallas kernels, solve(): pl.pallas_call(functools.partial(solve_kernel, part=part, parts=parts, ab...  13.4 us
    ppermute x4, starting transfers between devices, to_next(): return lax.ppermute(array, axes, [(i, i + 1) for i in range(ends)])  11.6 us
    pallas_call x1, Pallas kernels, move(): pl.pallas_call(functools.partial(move_kernel, per=per), name='tracer_move...  11.4 us
    all_to_all x1, starting transfers between devices, all_to_all(): return lax.all_to_all(array, EVERY, split_axis=0, concat_axis=0, tiled=True)  10.6 us
    pallas_call x1, Pallas kernels, spread(): pl.pallas_call(functools.partial(spread_kernel, group=group), name='sprea...  9.27 us
    all_to_all x1, waiting for transfers between devices, all_to_all(): return lax.all_to_all(array, EVERY, split_axis=0, concat_axis=0, tiled=True)  7.65 us
    pallas_call x1, Pallas kernels, pack(): pl.pallas_call(functools.partial(pack_kernel, beyond=beyond), name='pack_...  5.72 us
  transfers between devices with their start and end apart: 9, of which 1 were waited for; matrix products, arithmetic and copies ran while one was open for 0% of the time, Pallas kernels for 41%

profile of v7, /device:TPU:15, one launch (start us, length us, event | category | flops | bytes accessed | tf_op | source)
XLA Modules:
  0.0 94.6 jit_solution(5591082089708903307)
XLA Ops:
  0.6 5.7 %pack_margin.1 = f32[128,9,4,128]{3,2,1,0:T(4,128)} custom-call(s32[256]{0:T(256)} %bitcast.10, f32[8,16384]{1,0:T(8,128)} %flux_ref.1, s32[256,128]{1,0:T(8,128)} %source_ref.1, s32[256,128]{1,0:T(8,128)} %cell_ref.1, f32[256,128]{1,0:T(8,128)} %weight_ref.1), custom_call_target="tpu_custom_call" | custom-call | flops 4194304 | bytes 4194304 | tf_op jit(solution)/shard_map/pack_margin/pallas_call | solution.py:78
  6.3 10.6 %all-to-all-start = ((f32[128,9,4,128]{3,2,1,0:T(4,128)}), f32[128,9,4,128]{3,2,1,0:T(4,128)S(1)}, u32[]{:S(2)}, u32[]{:S(2)}) async-start(f32[128,9,4,128]{3,2,1,0:T(4,128)} %pack_margin.1), calls=%async_computation | async-start | bytes 4718592 | tf_op jit(solution)/shard_map/all_to_all | solution.py:578
  17.0 4.2 %tile_edges.1 = (f32[72,1024]{1,0:T(8,128)}, f32[72,1024]{1,0:T(8,128)}, f32[384,128]{1,0:T(8,128)}, f32[384,128]{1,0:T(8,128)}) custom-call(f32[32,64,1024]{2,1,0:T(8,128)} %bitcast.3, f32[32,64,1024]{2,1,0:T(8,128)} %bitcast.4, f32[32,64,1024]{2,1,0:T(8,128)} %bitcast.5, f32[32,64,1024]{2,1,0:T(8,128)} %bitcast.6, s32[64,1024]{1,0:T(8,128)} %mask_ref.4, ...), custom_call_target="tpu_custom_call" | custom-call | flops 1048576 | bytes 6291456 | tf_op jit(solution)/shard_map/tile_edges/pallas_call | solution.py:225
  21.3 0.0 copy-start
  21.3 0.0 copy-start.1
  21.3 0.0 copy-start.2
  21.3 1.4 %collective-permute-start.2 = (f32[384,128]{1,0:T(8,128)}, f32[384,128]{1,0:T(8,128)}, u32[]{:S(2)}, u32[]{:S(2)}) collective-permute-start(f32[384,128]{1,0:T(8,128)} %get-tuple-element.41.own_east_ref), channel_id=1, source_target_pairs={{0,1},{1,2},{2,3},{3,4},{4,5},{5,6},{6,7},{8,9},{9,10},{10,11},{11... | collective-permute-start | bytes 589832 | tf_op jit(solution)/shard_map/ppermute | solution.py:569
  22.7 11.4 %tracer_move.1 = f32[32,64,1024]{2,1,0:T(8,128)} custom-call(s32[64,1024]{1,0:T(8,128)} %mask_ref.4, f32[64,1024]{1,0:T(8,128)} %depth_ref.4, f32[2,64,1024]{2,1,0:T(8,128)} %stream_ref, f32[32,64,1024]{2,1,0:T(8,128)} %bitcast.7), custom_call_target="tpu_custom_call" | custom-call | flops 33554432 | bytes 18874368 | tf_op jit(solution)/shard_map/tracer_move/pallas_call | solution.py:299
  34.1 5.1 %collective-permute-start = (f32[72,1024]{1,0:T(8,128)}, f32[72,1024]{1,0:T(8,128)}, u32[]{:S(2)}, u32[]{:S(2)}) collective-permute-start(f32[72,1024]{1,0:T(8,128)} %get-tuple-element.39.own_ref), channel_id=1, source_target_pairs={{0,8},{8,16},{16,24},{24,32},{32,40},{40,48},{48,56},{56,64},{64,7... | collective-permute-start | bytes 884744 | tf_op jit(solution)/shard_map/ppermute | solution.py:569
  39.2 2.6 %collective-permute-start.1 = (f32[72,1024]{1,0:T(8,128)}, f32[72,1024]{1,0:T(8,128)}, u32[]{:S(2)}, u32[]{:S(2)}) collective-permute-start(f32[72,1024]{1,0:T(8,128)} %get-tuple-element.40.own_ref), channel_id=1, source_target_pairs={{8,0},{16,8},{24,16},{32,24},{40,32},{48,40},{56,48},{64,56},{72,6... | collective-permute-start | bytes 884744 | tf_op jit(solution)/shard_map/ppermute | solution.py:574
  41.8 4.3 %collective-permute-start.3 = (f32[384,128]{1,0:T(8,128)}, f32[384,128]{1,0:T(8,128)}, u32[]{:S(2)}, u32[]{:S(2)}) collective-permute-start(f32[384,128]{1,0:T(8,128)} %get-tuple-element.42.own_west_ref), channel_id=1, source_target_pairs={{1,0},{2,1},{3,2},{4,3},{5,4},{6,5},{7,6},{9,8},{10,9},{11,10},{12... | collective-permute-start | bytes 589832 | tf_op jit(solution)/shard_map/ppermute | solution.py:574
  46.1 7.7 %all-to-all-done.cells_ref.load_ref = f32[128,9,4,128]{3,2,1,0:T(4,128)S(1)} async-done(((f32[128,9,4,128]{3,2,1,0:T(4,128)}), f32[128,9,4,128]{3,2,1,0:T(4,128)S(1)}, u32[]{:S(2)}, u32[]{:S(2)}) %all-to-all-start) | async-done | bytes 2359328 | tf_op jit(solution)/shard_map/all_to_all | solution.py:578
  53.7 9.3 %spread_all.1 = (f32[4,64,1024]{2,1,0:T(8,128)S(1)}, f32[4,64,1024]{2,1,0:T(8,128)S(1)}, f32[4,8,1024]{2,1,0:T(8,128)S(1)}, f32[4,8,1024]{2,1,0:T(8,128)S(1)}) custom-call(f32[128,9,4,128]{3,2,1,0:T(4,128)S(1)} %all-to-all-done.cells_ref.load_ref, f32[128,9,4,128]{3,2,1,0:T(4,128)S(1)} %all-to-all-done.cells_ref.load_ref), custom_call_target="tpu_custom_call" | custom-call | flops 1073741824 | bytes 4194304 | tf_op jit(solution)/shard_map/spread_all/pallas_call | solution.py:175
  63.0 3.8 %collective-permute-start.4 = (f32[4,8,1024]{2,1,0:T(8,128)S(1)}, f32[4,8,1024]{2,1,0:T(8,128)S(1)}, u32[]{:S(2)}, u32[]{:S(2)}) collective-permute-start(f32[4,8,1024]{2,1,0:T(8,128)S(1)} %get-tuple-element.47), channel_id=1, source_target_pairs={{0,8},{8,16},{16,24},{24,32},{32,40},{40,48},{48,56},{56,64},{64,7... | collective-permute-start | bytes 393224 | tf_op jit(solution)/shard_map/ppermute | solution.py:569
  66.8 0.0 collective-permute-done.2.west_ref.left_ref
  66.8 3.9 %collective-permute-start.5 = (f32[4,8,1024]{2,1,0:T(8,128)S(1)}, f32[4,8,1024]{2,1,0:T(8,128)S(1)}, u32[]{:S(2)}, u32[]{:S(2)}) collective-permute-start(f32[4,8,1024]{2,1,0:T(8,128)S(1)} %get-tuple-element.48), channel_id=1, source_target_pairs={{8,0},{16,8},{24,16},{32,24},{40,32},{48,40},{56,48},{64,56},{72,6... | collective-permute-start | bytes 393224 | tf_op jit(solution)/shard_map/ppermute | solution.py:574
  70.7 0.0 collective-permute-done.3.east_ref.right_ref
  70.7 0.0 collective-permute-done.near_ref.low_ref
  70.7 0.0 copy-done
  70.7 0.0 copy-done.1
  70.7 0.0 copy-done.2
  70.8 0.0 copy-start.4
  70.8 0.9 copy-done.4
  71.7 6.7 %column_solve_0.1.refs_1_ = f32[2,16,64,1024]{3,2,1,0:T(8,128)} custom-call(f32[4,64,1024]{2,1,0:T(8,128)S(1)} %get-tuple-element.49.flux_ref, s32[64,1024]{1,0:T(8,128)S(1)} %copy-done.1, f32[64,1024]{1,0:T(8,128)S(1)} %copy-done.2, f32[2,64,1024]{2,1,0:T(8,128)S(1)} %copy-done, f32[72,1024]{1,0:T(8,128)} %collective-permute-done.near_ref.low_ref, ...), custom_call_target="tpu_custom_call" | custom-call | flops 16777216 | bytes 9437184 | tf_op jit(solution)/shard_map/column_solve_0/pallas_call | solution.py:433
  78.4 0.0 collective-permute-done.4.south_ref
  78.4 0.0 collective-permute-done.5.north_ref
  78.4 0.0 collective-permute-done.1.high_ref.near_ref
  78.4 1.1 %tile_sides.1 = (f32[400,128]{1,0:T(8,128)S(1)}, f32[400,128]{1,0:T(8,128)S(1)}) custom-call(f32[4,64,1024]{2,1,0:T(8,128)S(1)} %get-tuple-element.46.left_ref.right_ref.flux_ref, f32[4,64,1024]{2,1,0:T(8,128)S(1)} %get-tuple-element.46.left_ref.right_ref.flux_ref, f32[4,8,1024]{2,1,0:T(8,128)S(1)} %collective-permute-done.4.south_ref, ...), custom_call_target="tpu_custom_call" | custom-call | flops 65536 | bytes 2097152 | tf_op jit(solution)/shard_map/tile_sides/pallas_call | solution.py:482
  79.5 1.3 %collective-permute-start.6 = (f32[400,128]{1,0:T(8,128)S(1)}, f32[400,128]{1,0:T(8,128)S(1)}, u32[]{:S(2)}, u32[]{:S(2)}) collective-permute-start(f32[400,128]{1,0:T(8,128)S(1)} %get-tuple-element.53), channel_id=1, source_target_pairs={{0,1},{1,2},{2,3},{3,4},{4,5},{5,6},{6,7},{8,9},{9,10},{10,11},{11... | collective-permute-start | bytes 614408 | tf_op jit(solution)/shard_map/ppermute | solution.py:569
  80.8 0.0 copy-start.3
  80.8 3.2 %collective-permute-start.7 = (f32[400,128]{1,0:T(8,128)S(1)}, f32[400,128]{1,0:T(8,128)S(1)}, u32[]{:S(2)}, u32[]{:S(2)}) collective-permute-start(f32[400,128]{1,0:T(8,128)S(1)} %get-tuple-element.54), channel_id=1, source_target_pairs={{1,0},{2,1},{3,2},{4,3},{5,4},{6,5},{7,6},{9,8},{10,9},{11,10},{12... | collective-permute-start | bytes 614408 | tf_op jit(solution)/shard_map/ppermute | solution.py:574
  84.0 6.7 %column_solve_1.1 = f32[2,16,64,1024]{3,2,1,0:T(8,128)} custom-call(f32[4,64,1024]{2,1,0:T(8,128)S(1)} %get-tuple-element.49.flux_ref, s32[64,1024]{1,0:T(8,128)S(1)} %copy-done.1, f32[64,1024]{1,0:T(8,128)S(1)} %copy-done.2, f32[2,64,1024]{2,1,0:T(8,128)S(1)} %copy-done, ...), custom_call_target="tpu_custom_call", output_to_operand_aliasing={{}: (11, {})} | custom-call | flops 16777216 | bytes 9437184 | tf_op jit(solution)/shard_map/column_solve_1/pallas_call | solution.py:433
  90.7 0.0 collective-permute-done.6.west_ref
  90.7 0.0 collective-permute-done.7.east_ref
  90.7 0.0 copy-done.3
  90.7 3.9 %barotropic.1 = (f32[64,1024]{1,0:T(8,128)}, f32[2,64,1024]{2,1,0:T(8,128)}) custom-call(s32[64,1024]{1,0:T(8,128)S(1)} %copy-done.1, f32[64,1024]{1,0:T(8,128)S(1)} %copy-done.2, f32[64,1024]{1,0:T(8,128)S(1)} %copy-done.3, f32[2,64,1024]{2,1,0:T(8,128)S(1)} %copy-done, f32[72,1024]{1,0:T(8,128)} %collective-permute-done.near_ref.low_ref, ...), custom_call_target="tpu_custom_call" | custom-call | flops 16777216 | bytes 6291456 | tf_op jit(solution)/shard_map/barotropic/pallas_call | solution.py:554
Async XLA Ops:
  6.3 47.4 %all-to-all-start = ((f32[128,9,4,128]{3,2,1,0:T(4,128)}), f32[128,9,4,128]{3,2,1,0:T(4,128)S(1)}, u32[]{:S(2)}, u32[]{:S(2)}) async-start(f32[128,9,4,128]{3,2,1,0:T(4,128)} %pack_margin.1), calls=%async_computation | async-start | bytes 4718592 | tf_op jit(solution)/shard_map/all_to_all | solution.py:578
  21.3 49.5 %copy-start = (f32[2,64,1024]{2,1,0:T(8,128)S(1)}, f32[2,64,1024]{2,1,0:T(8,128)}, u32[]{:S(2)}) copy-start(f32[2,64,1024]{2,1,0:T(8,128)} %stream_ref) | copy-start | bytes 1572868
  21.3 49.5 %copy-start.1 = (s32[64,1024]{1,0:T(8,128)S(1)}, s32[64,1024]{1,0:T(8,128)}, u32[]{:S(2)}) copy-start(s32[64,1024]{1,0:T(8,128)} %mask_ref.4) | copy-start | bytes 786436
  21.3 49.5 %copy-start.2 = (f32[64,1024]{1,0:T(8,128)S(1)}, f32[64,1024]{1,0:T(8,128)}, u32[]{:S(2)}) copy-start(f32[64,1024]{1,0:T(8,128)} %depth_ref.4) | copy-start | bytes 786436
  21.3 45.6 %collective-permute-start.2 = (f32[384,128]{1,0:T(8,128)}, f32[384,128]{1,0:T(8,128)}, u32[]{:S(2)}, u32[]{:S(2)}) collective-permute-start(f32[384,128]{1,0:T(8,128)} %get-tuple-element.41.own_east_ref), channel_id=1, source_target_pairs={{0,1},{1,2},{2,3},{3,4},{4,5},{5,6},{6,7},{8,9},{9,10},{10,11},{11... | collective-permute-start | bytes 589832 | tf_op jit(solution)/shard_map/ppermute | solution.py:569
  34.1 36.6 %collective-permute-start = (f32[72,1024]{1,0:T(8,128)}, f32[72,1024]{1,0:T(8,128)}, u32[]{:S(2)}, u32[]{:S(2)}) collective-permute-start(f32[72,1024]{1,0:T(8,128)} %get-tuple-element.39.own_ref), channel_id=1, source_target_pairs={{0,8},{8,16},{16,24},{24,32},{32,40},{40,48},{48,56},{56,64},{64,7... | collective-permute-start | bytes 884744 | tf_op jit(solution)/shard_map/ppermute | solution.py:569
  39.2 39.2 %collective-permute-start.1 = (f32[72,1024]{1,0:T(8,128)}, f32[72,1024]{1,0:T(8,128)}, u32[]{:S(2)}, u32[]{:S(2)}) collective-permute-start(f32[72,1024]{1,0:T(8,128)} %get-tuple-element.40.own_ref), channel_id=1, source_target_pairs={{8,0},{16,8},{24,16},{32,24},{40,32},{48,40},{56,48},{64,56},{72,6... | collective-permute-start | bytes 884744 | tf_op jit(solution)/shard_map/ppermute | solution.py:574
  41.8 28.9 %collective-permute-start.3 = (f32[384,128]{1,0:T(8,128)}, f32[384,128]{1,0:T(8,128)}, u32[]{:S(2)}, u32[]{:S(2)}) collective-permute-start(f32[384,128]{1,0:T(8,128)} %get-tuple-element.42.own_west_ref), channel_id=1, source_target_pairs={{1,0},{2,1},{3,2},{4,3},{5,4},{6,5},{7,6},{9,8},{10,9},{11,10},{12... | collective-permute-start | bytes 589832 | tf_op jit(solution)/shard_map/ppermute | solution.py:574
  63.0 15.4 %collective-permute-start.4 = (f32[4,8,1024]{2,1,0:T(8,128)S(1)}, f32[4,8,1024]{2,1,0:T(8,128)S(1)}, u32[]{:S(2)}, u32[]{:S(2)}) collective-permute-start(f32[4,8,1024]{2,1,0:T(8,128)S(1)} %get-tuple-element.47), channel_id=1, source_target_pairs={{0,8},{8,16},{16,24},{24,32},{32,40},{40,48},{48,56},{56,64},{64,7... | collective-permute-start | bytes 393224 | tf_op jit(solution)/shard_map/ppermute | solution.py:569
  66.8 11.6 %collective-permute-start.5 = (f32[4,8,1024]{2,1,0:T(8,128)S(1)}, f32[4,8,1024]{2,1,0:T(8,128)S(1)}, u32[]{:S(2)}, u32[]{:S(2)}) collective-permute-start(f32[4,8,1024]{2,1,0:T(8,128)S(1)} %get-tuple-element.48), channel_id=1, source_target_pairs={{8,0},{16,8},{24,16},{32,24},{40,32},{48,40},{56,48},{64,56},{72,6... | collective-permute-start | bytes 393224 | tf_op jit(solution)/shard_map/ppermute | solution.py:574
  70.8 0.9 copy-start.4
  79.5 11.2 %collective-permute-start.6 = (f32[400,128]{1,0:T(8,128)S(1)}, f32[400,128]{1,0:T(8,128)S(1)}, u32[]{:S(2)}, u32[]{:S(2)}) collective-permute-start(f32[400,128]{1,0:T(8,128)S(1)} %get-tuple-element.53), channel_id=1, source_target_pairs={{0,1},{1,2},{2,3},{3,4},{4,5},{5,6},{6,7},{8,9},{9,10},{10,11},{11... | collective-permute-start | bytes 614408 | tf_op jit(solution)/shard_map/ppermute | solution.py:569
  80.8 9.9 %copy-start.3 = (f32[64,1024]{1,0:T(8,128)S(1)}, f32[64,1024]{1,0:T(8,128)}, u32[]{:S(2)}) copy-start(f32[64,1024]{1,0:T(8,128)} %begin_ref) | copy-start | bytes 786436
  80.8 9.9 %collective-permute-start.7 = (f32[400,128]{1,0:T(8,128)S(1)}, f32[400,128]{1,0:T(8,128)S(1)}, u32[]{:S(2)}, u32[]{:S(2)}) collective-permute-start(f32[400,128]{1,0:T(8,128)S(1)} %get-tuple-element.54), channel_id=1, source_target_pairs={{1,0},{2,1},{3,2},{4,3},{5,4},{6,5},{7,6},{9,8},{10,9},{11,10},{12... | collective-permute-start | bytes 614408 | tf_op jit(solution)/shard_map/ppermute | solution.py:574

commit v8 on v7

--- a/solution.py
+++ b/solution.py
@@ -449,7 +449,7 @@
         out_shape=jax.ShapeDtypeStruct(moved.shape, f32),
         scratch_shapes=[pltpu.VMEM((levels, EDGE, columns), f32)],
         input_output_aliases={11: 0} if done else {},
-        compiler_params=params(48),
+        compiler_params=params(24),
         cost_estimate=pl.CostEstimate(flops=1 << 24, bytes_accessed=9 << 20, transcendentals=0),
     )(flux, mask, depth, flow, near, own, *margins, moved, *done)
 

time: 95.4 us -> 97.1 us (1.018)
  local copies, waits for them, and re-layouts: 0.94 us -> 4.32 us
  Pallas kernels: 49 us -> 47.3 us
    unnamed x10 -> x12, local copies, waits for them, and re-layouts: 0.94 us -> 4.32 us
    pallas_call x2, Pallas kernels: 13.4 us -> 11.7 us  [solve(): pl.pallas_call(functools.partial(solve_kernel, part=part, parts=parts, ab...]
  transfers between devices with their start and end apart: 9 -> 9, of which waited for: 1 -> 1; matrix products, arithmetic and copies ran while one was open for 0% -> 0% of each run, Pallas kernels for 41% -> 38%
where the time goes in v8:
time: 97.1 us; the launch traced here: 96.3 us
  Pallas kernels  47.3 us (49%)
  starting transfers between devices  36.2 us (37%)
  waiting for transfers between devices  7.76 us (8%)
  local copies, waits for them, and re-layouts  4.32 us (4%)
    ppermute x4, starting transfers between devices, to_previous(): return lax.ppermute(array, axes, [(i + 1, i) for i in range(ends)])  13.9 us
    pallas_call x2, Pallas kernels, solve(): pl.pallas_call(functools.partial(solve_kernel, part=part, parts=parts, ab...  11.7 us
    ppermute x4, starting transfers between devices, to_next(): return lax.ppermute(array, axes, [(i, i + 1) for i in range(ends)])  11.6 us
    pallas_call x1, Pallas kernels, move(): pl.pallas_call(functools.partial(move_kernel, per=per), name='tracer_move...  11.3 us
    all_to_all x1, starting transfers between devices, all_to_all(): return lax.all_to_all(array, EVERY, split_axis=0, concat_axis=0, tiled=True)  10.6 us
    pallas_call x1, Pallas kernels, spread(): pl.pallas_call(functools.partial(spread_kernel, group=group), name='sprea...  9.27 us
    all_to_all x1, waiting for transfers between devices, all_to_all(): return lax.all_to_all(array, EVERY, split_axis=0, concat_axis=0, tiled=True)  7.74 us
    pallas_call x1, Pallas kernels, pack(): pl.pallas_call(functools.partial(pack_kernel, beyond=beyond), name='pack_...  5.74 us
  transfers between devices with their start and end apart: 9, of which 1 were waited for; matrix products, arithmetic and copies ran while one was open for 0% of the time, Pallas kernels for 38%

profile of v8, /device:TPU:15, one launch (start us, length us, event | category | flops | bytes accessed | tf_op | source)
XLA Modules:
  0.0 96.3 jit_solution(13601377002737779323)
XLA Ops:
  0.6 5.7 %pack_margin.1 = f32[128,9,4,128]{3,2,1,0:T(4,128)} custom-call(s32[256]{0:T(256)} %bitcast.10, f32[8,16384]{1,0:T(8,128)} %flux_ref.1, s32[256,128]{1,0:T(8,128)} %source_ref.1, s32[256,128]{1,0:T(8,128)} %cell_ref.1, f32[256,128]{1,0:T(8,128)} %weight_ref.1), custom_call_target="tpu_custom_call" | custom-call | flops 4194304 | bytes 4194304 | tf_op jit(solution)/shard_map/pack_margin/pallas_call | solution.py:78
  6.4 10.6 %all-to-all-start = ((f32[128,9,4,128]{3,2,1,0:T(4,128)}), f32[128,9,4,128]{3,2,1,0:T(4,128)S(1)}, u32[]{:S(2)}, u32[]{:S(2)}) async-start(f32[128,9,4,128]{3,2,1,0:T(4,128)} %pack_margin.1), calls=%async_computation | async-start | bytes 4718592 | tf_op jit(solution)/shard_map/all_to_all | solution.py:578
  17.0 4.2 %tile_edges.1 = (f32[72,1024]{1,0:T(8,128)}, f32[72,1024]{1,0:T(8,128)}, f32[384,128]{1,0:T(8,128)}, f32[384,128]{1,0:T(8,128)}) custom-call(f32[32,64,1024]{2,1,0:T(8,128)} %bitcast.5, f32[32,64,1024]{2,1,0:T(8,128)} %bitcast.6, f32[32,64,1024]{2,1,0:T(8,128)} %bitcast.7, f32[32,64,1024]{2,1,0:T(8,128)} %bitcast.8, s32[64,1024]{1,0:T(8,128)} %mask_ref.4, ...), custom_call_target="tpu_custom_call" | custom-call | flops 1048576 | bytes 6291456 | tf_op jit(solution)/shard_map/tile_edges/pallas_call | solution.py:225
  21.2 0.0 copy-start.1
  21.3 0.0 copy-start.2
  21.3 0.0 copy-start.3
  21.3 1.4 %collective-permute-start.2 = (f32[384,128]{1,0:T(8,128)}, f32[384,128]{1,0:T(8,128)}, u32[]{:S(2)}, u32[]{:S(2)}) collective-permute-start(f32[384,128]{1,0:T(8,128)} %get-tuple-element.41.own_east_ref), channel_id=1, source_target_pairs={{0,1},{1,2},{2,3},{3,4},{4,5},{5,6},{6,7},{8,9},{9,10},{10,11},{11... | collective-permute-start | bytes 589832 | tf_op jit(solution)/shard_map/ppermute | solution.py:569
  22.7 11.3 %tracer_move.1 = f32[32,64,1024]{2,1,0:T(8,128)} custom-call(s32[64,1024]{1,0:T(8,128)} %mask_ref.4, f32[64,1024]{1,0:T(8,128)} %depth_ref.4, f32[2,64,1024]{2,1,0:T(8,128)} %stream_ref, f32[32,64,1024]{2,1,0:T(8,128)} %bitcast.9), custom_call_target="tpu_custom_call" | custom-call | flops 33554432 | bytes 18874368 | tf_op jit(solution)/shard_map/tracer_move/pallas_call | solution.py:299
  34.0 5.1 %collective-permute-start = (f32[72,1024]{1,0:T(8,128)}, f32[72,1024]{1,0:T(8,128)}, u32[]{:S(2)}, u32[]{:S(2)}) collective-permute-start(f32[72,1024]{1,0:T(8,128)} %get-tuple-element.39.own_ref), channel_id=1, source_target_pairs={{0,8},{8,16},{16,24},{24,32},{32,40},{40,48},{48,56},{56,64},{64,7... | collective-permute-start | bytes 884744 | tf_op jit(solution)/shard_map/ppermute | solution.py:569
  39.1 2.6 %collective-permute-start.1 = (f32[72,1024]{1,0:T(8,128)}, f32[72,1024]{1,0:T(8,128)}, u32[]{:S(2)}, u32[]{:S(2)}) collective-permute-start(f32[72,1024]{1,0:T(8,128)} %get-tuple-element.40.own_ref), channel_id=1, source_target_pairs={{8,0},{16,8},{24,16},{32,24},{40,32},{48,40},{56,48},{64,56},{72,6... | collective-permute-start | bytes 884744 | tf_op jit(solution)/shard_map/ppermute | solution.py:574
  41.7 4.3 %collective-permute-start.3 = (f32[384,128]{1,0:T(8,128)}, f32[384,128]{1,0:T(8,128)}, u32[]{:S(2)}, u32[]{:S(2)}) collective-permute-start(f32[384,128]{1,0:T(8,128)} %get-tuple-element.42.own_west_ref), channel_id=1, source_target_pairs={{1,0},{2,1},{3,2},{4,3},{5,4},{6,5},{7,6},{9,8},{10,9},{11,10},{12... | collective-permute-start | bytes 589832 | tf_op jit(solution)/shard_map/ppermute | solution.py:574
  46.0 7.7 %all-to-all-done.cells_ref.load_ref = f32[128,9,4,128]{3,2,1,0:T(4,128)S(1)} async-done(((f32[128,9,4,128]{3,2,1,0:T(4,128)}), f32[128,9,4,128]{3,2,1,0:T(4,128)S(1)}, u32[]{:S(2)}, u32[]{:S(2)}) %all-to-all-start) | async-done | bytes 2359328 | tf_op jit(solution)/shard_map/all_to_all | solution.py:578
  53.7 9.3 %spread_all.1 = (f32[4,64,1024]{2,1,0:T(8,128)S(1)}, f32[4,64,1024]{2,1,0:T(8,128)S(1)}, f32[4,8,1024]{2,1,0:T(8,128)S(1)}, f32[4,8,1024]{2,1,0:T(8,128)S(1)}) custom-call(f32[128,9,4,128]{3,2,1,0:T(4,128)S(1)} %all-to-all-done.cells_ref.load_ref, f32[128,9,4,128]{3,2,1,0:T(4,128)S(1)} %all-to-all-done.cells_ref.load_ref), custom_call_target="tpu_custom_call" | custom-call | flops 1073741824 | bytes 4194304 | tf_op jit(solution)/shard_map/spread_all/pallas_call | solution.py:175
  63.0 3.8 %collective-permute-start.4 = (f32[4,8,1024]{2,1,0:T(8,128)S(1)}, f32[4,8,1024]{2,1,0:T(8,128)S(1)}, u32[]{:S(2)}, u32[]{:S(2)}) collective-permute-start(f32[4,8,1024]{2,1,0:T(8,128)S(1)} %get-tuple-element.47), channel_id=1, source_target_pairs={{0,8},{8,16},{16,24},{24,32},{32,40},{40,48},{48,56},{56,64},{64,7... | collective-permute-start | bytes 393224 | tf_op jit(solution)/shard_map/ppermute | solution.py:569
  66.8 0.0 collective-permute-done.2.west_ref.left_ref
  66.9 3.9 %collective-permute-start.5 = (f32[4,8,1024]{2,1,0:T(8,128)S(1)}, f32[4,8,1024]{2,1,0:T(8,128)S(1)}, u32[]{:S(2)}, u32[]{:S(2)}) collective-permute-start(f32[4,8,1024]{2,1,0:T(8,128)S(1)} %get-tuple-element.48), channel_id=1, source_target_pairs={{8,0},{16,8},{24,16},{32,24},{40,32},{48,40},{56,48},{64,56},{72,6... | collective-permute-start | bytes 393224 | tf_op jit(solution)/shard_map/ppermute | solution.py:574
  70.7 0.0 collective-permute-done.3.east_ref.right_ref
  70.7 0.0 collective-permute-done.near_ref.low_ref
  70.8 0.0 copy-done.1
  70.8 0.0 copy-done.2
  70.8 0.0 copy-done.3
  70.8 0.0 copy-start
  70.8 3.4 %copy-done = f32[32,64,1024]{2,1,0:T(8,128)S(1)} copy-done((f32[32,64,1024]{2,1,0:T(8,128)S(1)}, f32[32,64,1024]{2,1,0:T(8,128)}, u32[]{:S(2)}) %copy-start) | copy-done | bytes 8388632
  74.2 0.0 copy-start.5
  74.2 0.9 copy-done.5
  75.1 5.9 %column_solve_0.1.refs_1_ = f32[2,16,64,1024]{3,2,1,0:T(8,128)} custom-call(f32[4,64,1024]{2,1,0:T(8,128)S(1)} %get-tuple-element.49.flux_ref, s32[64,1024]{1,0:T(8,128)S(1)} %copy-done.2, f32[64,1024]{1,0:T(8,128)S(1)} %copy-done.3, f32[2,64,1024]{2,1,0:T(8,128)S(1)} %copy-done.1, f32[72,1024]{1,0:T(8,128)} %collective-permute-done.near_ref.low_ref, ...), custom_call_target="tpu_custom_call" | custom-call | flops 16777216 | bytes 9437184 | tf_op jit(solution)/shard_map/column_solve_0/pallas_call | solution.py:433
  81.0 0.0 collective-permute-done.4.south_ref
  81.0 0.0 collective-permute-done.5.north_ref
  81.0 0.0 collective-permute-done.1.high_ref.near_ref
  81.0 1.1 %tile_sides.1 = (f32[400,128]{1,0:T(8,128)S(1)}, f32[400,128]{1,0:T(8,128)S(1)}) custom-call(f32[4,64,1024]{2,1,0:T(8,128)S(1)} %get-tuple-element.46.left_ref.right_ref.flux_ref, f32[4,64,1024]{2,1,0:T(8,128)S(1)} %get-tuple-element.46.left_ref.right_ref.flux_ref, f32[4,8,1024]{2,1,0:T(8,128)S(1)} %collective-permute-done.4.south_ref, ...), custom_call_target="tpu_custom_call" | custom-call | flops 65536 | bytes 2097152 | tf_op jit(solution)/shard_map/tile_sides/pallas_call | solution.py:482
  82.1 1.3 %collective-permute-start.6 = (f32[400,128]{1,0:T(8,128)S(1)}, f32[400,128]{1,0:T(8,128)S(1)}, u32[]{:S(2)}, u32[]{:S(2)}) collective-permute-start(f32[400,128]{1,0:T(8,128)S(1)} %get-tuple-element.53), channel_id=1, source_target_pairs={{0,1},{1,2},{2,3},{3,4},{4,5},{5,6},{6,7},{8,9},{9,10},{10,11},{11... | collective-permute-start | bytes 614408 | tf_op jit(solution)/shard_map/ppermute | solution.py:569
  83.4 0.0 copy-start.4
  83.4 3.2 %collective-permute-start.7 = (f32[400,128]{1,0:T(8,128)S(1)}, f32[400,128]{1,0:T(8,128)S(1)}, u32[]{:S(2)}, u32[]{:S(2)}) collective-permute-start(f32[400,128]{1,0:T(8,128)S(1)} %get-tuple-element.54), channel_id=1, source_target_pairs={{1,0},{2,1},{3,2},{4,3},{5,4},{6,5},{7,6},{9,8},{10,9},{11,10},{12... | collective-permute-start | bytes 614408 | tf_op jit(solution)/shard_map/ppermute | solution.py:574
  86.6 5.9 %column_solve_1.1 = f32[2,16,64,1024]{3,2,1,0:T(8,128)} custom-call(f32[4,64,1024]{2,1,0:T(8,128)S(1)} %get-tuple-element.49.flux_ref, s32[64,1024]{1,0:T(8,128)S(1)} %copy-done.2, f32[64,1024]{1,0:T(8,128)S(1)} %copy-done.3, f32[2,64,1024]{2,1,0:T(8,128)S(1)} %copy-done.1, ...), custom_call_target="tpu_custom_call", output_to_operand_aliasing={{}: (11, {})} | custom-call | flops 16777216 | bytes 9437184 | tf_op jit(solution)/shard_map/column_solve_1/pallas_call | solution.py:433
  92.4 0.0 collective-permute-done.6.west_ref
  92.5 0.0 collective-permute-done.7.east_ref
  92.5 0.0 copy-done.4
  92.5 3.9 %barotropic.1 = (f32[64,1024]{1,0:T(8,128)}, f32[2,64,1024]{2,1,0:T(8,128)}) custom-call(s32[64,1024]{1,0:T(8,128)S(1)} %copy-done.2, f32[64,1024]{1,0:T(8,128)S(1)} %copy-done.3, f32[64,1024]{1,0:T(8,128)S(1)} %copy-done.4, f32[2,64,1024]{2,1,0:T(8,128)S(1)} %copy-done.1, f32[72,1024]{1,0:T(8,128)} %collective-permute-done.near_ref.low_ref, ...), custom_call_target="tpu_custom_call" | custom-call | flops 16777216 | bytes 6291456 | tf_op jit(solution)/shard_map/barotropic/pallas_call | solution.py:554
Async XLA Ops:
  6.4 47.4 %all-to-all-start = ((f32[128,9,4,128]{3,2,1,0:T(4,128)}), f32[128,9,4,128]{3,2,1,0:T(4,128)S(1)}, u32[]{:S(2)}, u32[]{:S(2)}) async-start(f32[128,9,4,128]{3,2,1,0:T(4,128)} %pack_margin.1), calls=%async_computation | async-start | bytes 4718592 | tf_op jit(solution)/shard_map/all_to_all | solution.py:578
  21.2 49.5 %copy-start.1 = (f32[2,64,1024]{2,1,0:T(8,128)S(1)}, f32[2,64,1024]{2,1,0:T(8,128)}, u32[]{:S(2)}) copy-start(f32[2,64,1024]{2,1,0:T(8,128)} %stream_ref) | copy-start | bytes 1572868
  21.3 49.5 %copy-start.2 = (s32[64,1024]{1,0:T(8,128)S(1)}, s32[64,1024]{1,0:T(8,128)}, u32[]{:S(2)}) copy-start(s32[64,1024]{1,0:T(8,128)} %mask_ref.4) | copy-start | bytes 786436
  21.3 49.5 %copy-start.3 = (f32[64,1024]{1,0:T(8,128)S(1)}, f32[64,1024]{1,0:T(8,128)}, u32[]{:S(2)}) copy-start(f32[64,1024]{1,0:T(8,128)} %depth_ref.4) | copy-start | bytes 786436
  21.3 45.6 %collective-permute-start.2 = (f32[384,128]{1,0:T(8,128)}, f32[384,128]{1,0:T(8,128)}, u32[]{:S(2)}, u32[]{:S(2)}) collective-permute-start(f32[384,128]{1,0:T(8,128)} %get-tuple-element.41.own_east_ref), channel_id=1, source_target_pairs={{0,1},{1,2},{2,3},{3,4},{4,5},{5,6},{6,7},{8,9},{9,10},{10,11},{11... | collective-permute-start | bytes 589832 | tf_op jit(solution)/shard_map/ppermute | solution.py:569
  34.0 36.7 %collective-permute-start = (f32[72,1024]{1,0:T(8,128)}, f32[72,1024]{1,0:T(8,128)}, u32[]{:S(2)}, u32[]{:S(2)}) collective-permute-start(f32[72,1024]{1,0:T(8,128)} %get-tuple-element.39.own_ref), channel_id=1, source_target_pairs={{0,8},{8,16},{16,24},{24,32},{32,40},{40,48},{48,56},{56,64},{64,7... | collective-permute-start | bytes 884744 | tf_op jit(solution)/shard_map/ppermute | solution.py:569
  39.1 41.8 %collective-permute-start.1 = (f32[72,1024]{1,0:T(8,128)}, f32[72,1024]{1,0:T(8,128)}, u32[]{:S(2)}, u32[]{:S(2)}) collective-permute-start(f32[72,1024]{1,0:T(8,128)} %get-tuple-element.40.own_ref), channel_id=1, source_target_pairs={{8,0},{16,8},{24,16},{32,24},{40,32},{48,40},{56,48},{64,56},{72,6... | collective-permute-start | bytes 884744 | tf_op jit(solution)/shard_map/ppermute | solution.py:574
  41.7 29.0 %collective-permute-start.3 = (f32[384,128]{1,0:T(8,128)}, f32[384,128]{1,0:T(8,128)}, u32[]{:S(2)}, u32[]{:S(2)}) collective-permute-start(f32[384,128]{1,0:T(8,128)} %get-tuple-element.42.own_west_ref), channel_id=1, source_target_pairs={{1,0},{2,1},{3,2},{4,3},{5,4},{6,5},{7,6},{9,8},{10,9},{11,10},{12... | collective-permute-start | bytes 589832 | tf_op jit(solution)/shard_map/ppermute | solution.py:574
  63.0 17.9 %collective-permute-start.4 = (f32[4,8,1024]{2,1,0:T(8,128)S(1)}, f32[4,8,1024]{2,1,0:T(8,128)S(1)}, u32[]{:S(2)}, u32[]{:S(2)}) collective-permute-start(f32[4,8,1024]{2,1,0:T(8,128)S(1)} %get-tuple-element.47), channel_id=1, source_target_pairs={{0,8},{8,16},{16,24},{24,32},{32,40},{40,48},{48,56},{56,64},{64,7... | collective-permute-start | bytes 393224 | tf_op jit(solution)/shard_map/ppermute | solution.py:569
  66.9 14.1 %collective-permute-start.5 = (f32[4,8,1024]{2,1,0:T(8,128)S(1)}, f32[4,8,1024]{2,1,0:T(8,128)S(1)}, u32[]{:S(2)}, u32[]{:S(2)}) collective-permute-start(f32[4,8,1024]{2,1,0:T(8,128)S(1)} %get-tuple-element.48), channel_id=1, source_target_pairs={{8,0},{16,8},{24,16},{32,24},{40,32},{48,40},{56,48},{64,56},{72,6... | collective-permute-start | bytes 393224 | tf_op jit(solution)/shard_map/ppermute | solution.py:574
  70.8 3.4 %copy-start = (f32[32,64,1024]{2,1,0:T(8,128)S(1)}, f32[32,64,1024]{2,1,0:T(8,128)}, u32[]{:S(2)}) copy-start(f32[32,64,1024]{2,1,0:T(8,128)} %tracer_move.1) | copy-start | bytes 25165828
  74.2 0.9 copy-start.5
  82.1 10.4 %collective-permute-start.6 = (f32[400,128]{1,0:T(8,128)S(1)}, f32[400,128]{1,0:T(8,128)S(1)}, u32[]{:S(2)}, u32[]{:S(2)}) collective-permute-start(f32[400,128]{1,0:T(8,128)S(1)} %get-tuple-element.53), channel_id=1, source_target_pairs={{0,1},{1,2},{2,3},{3,4},{4,5},{5,6},{6,7},{8,9},{9,10},{10,11},{11... | collective-permute-start | bytes 614408 | tf_op jit(solution)/shard_map/ppermute | solution.py:569
  83.4 9.1 %copy-start.4 = (f32[64,1024]{1,0:T(8,128)S(1)}, f32[64,1024]{1,0:T(8,128)}, u32[]{:S(2)}) copy-start(f32[64,1024]{1,0:T(8,128)} %begin_ref) | copy-start | bytes 786436
  83.4 9.1 %collective-permute-start.7 = (f32[400,128]{1,0:T(8,128)S(1)}, f32[400,128]{1,0:T(8,128)S(1)}, u32[]{:S(2)}, u32[]{:S(2)}) collective-permute-start(f32[400,128]{1,0:T(8,128)S(1)} %get-tuple-element.54), channel_id=1, source_target_pairs={{1,0},{2,1},{3,2},{4,3},{5,4},{6,5},{7,6},{9,8},{10,9},{11,10},{12... | collective-permute-start | bytes 614408 | tf_op jit(solution)/shard_map/ppermute | solution.py:574
